TPU v7x, 32 devices: a whole 2x2x4 slice. The times are simulated.
32 devices in a mesh: dp: 2 (over x), seq: 16 (over z, y, core).
Axes of the slice: x: 2, y: 2, z: 4, core: 2. Of those that a mesh axis runs over, the one named last changes fastest.
Arguments:
- hidden: bfloat16 [2, 2048, 2048], P('dp', 'seq'), may hold values from -7 to 7
- cotangent: bfloat16 [2, 2048, 2048], P('dp', 'seq'), may hold values from -6 to 6
- picks: int32 [2, 2048], P('dp', 'seq'), may hold values from 0 to 1, as said below
- gain: float32 [2048], replicated, may hold values from 0.5 to 1.5
- router: float32 [2048], replicated, may hold values from -0.125 to 0.125
- w_query: bfloat16 [2048, 1024], P('seq'), may hold values from -2 to 2
- w_kv: bfloat16 [2048, 256], P('seq'), may hold values from -2 to 2
- w_out: bfloat16 [1024, 2048], P('seq'), may hold values from -0.1875 to 0.1875
Outputs:
- mixed: bfloat16 [2, 2048, 2048], P('dp', 'seq')
- input_grad: bfloat16 [2, 2048, 2048], P('dp', 'seq')
- kv_grad: float32 [2048, 256], P('seq')
- router_grad: float32 [2048], P('seq')
Inputs may be any that keep to these rules, and one draw needn't show every extreme that they name: `picks`: every sequence has exactly 256 picked tokens; each aligned block of 128 tokens has 0 to 32 of them, and in every sequence some block has exactly 32.
All inputs are finite; a program needn't handle non-finite values.
Results may differ from a plain program's by a relative error of at most 0.013.
The roundings to bfloat16 on the way count: a program that leaves them out, or rounds other values in their place, can miss the bound.
Values may be sent and summed in bfloat16 or wider, within the bound.
No kernel may reach another device: no remote copies, remote signals or barrier semaphores. Data moves between devices by JAX's collectives and lax.ppermute only.
A program may use at most 64 MiB of HBM per device.

v0:
```python
import jax
import jax.numpy as jnp
from jax import lax
from jax.sharding import PartitionSpec as P

MODEL_WIDTH = 2048
QUERY_HEADS = 16
KEY_VALUE_HEADS = 2
HEAD_SIZE = 64


EPSILON = 1e-05


def carried_in(value, axis, combine, identity):
    peers, index = (lax.axis_size(axis), lax.axis_index(axis))
    everything = lax.all_gather(value, axis)
    start = jnp.broadcast_to(jnp.asarray(identity, value.dtype), value.shape)

    def lap(k, before):
        reached = k < index
        new = combine(before, everything[k])
        return jnp.where(reached, new, before)

    return lax.fori_loop(0, peers, lap, start)


def dot_transposed(left, right):
    return lax.dot_general(
        left, right, (((1,), (1,)), ((), ())), preferred_element_type=jnp.float32
    )


def route_table(pick_mask, offset, devices_seq, slot_rows):
    token_count = pick_mask.shape[0]
    local_rank = jnp.cumsum(pick_mask) - pick_mask
    global_rank = offset + local_rank
    placed_at = global_rank % devices_seq * slot_rows + local_rank // devices_seq
    target = jnp.where(pick_mask > 0, placed_at, -1)
    route_hits = (
        lax.broadcasted_iota(jnp.int32, (devices_seq * slot_rows, token_count), 0)
        == target[None, :]
    )
    sent_rank = jnp.max(jnp.where(route_hits, global_rank[None, :], -1), axis=1)
    return (route_hits.astype(jnp.bfloat16), sent_rank.reshape(devices_seq, slot_rows))


def compact_table(got_rank, devices_seq, capacity_rows):
    rank_list = got_rank.reshape(-1)
    local_index = jnp.where(rank_list >= 0, rank_list // devices_seq, -1)
    matches = (
        lax.broadcasted_iota(jnp.int32, (capacity_rows, rank_list.shape[0]), 0)
        == local_index[None, :]
    )
    return matches.astype(jnp.bfloat16)


def select_rows(table, source):
    return jnp.dot(table, source, preferred_element_type=jnp.float32).astype(jnp.bfloat16)


def spread_rows(table, source):
    placed = lax.dot_general(
        table, source, (((0,), (0,)), ((), ())), preferred_element_type=jnp.float32
    )
    return placed.astype(jnp.bfloat16)


def local(hidden, cotangent, picks, gain, router, w_query, w_kv, w_out):
    devices_seq = lax.axis_size("seq")
    my_index = lax.axis_index("seq")
    token_count = hidden.shape[1]
    capacity_rows = token_count // 8
    slot_rows = (2 * capacity_rows + devices_seq - 1) // devices_seq
    key_value_width = KEY_VALUE_HEADS * HEAD_SIZE
    query_group_size = QUERY_HEADS // KEY_VALUE_HEADS
    head_scale = HEAD_SIZE ** (-0.5)
    token_half = hidden[0]
    token_rows = token_half.astype(jnp.float32)
    grad_rows = cotangent[0].astype(jnp.float32)
    pick_mask = picks[0]
    whole_query, whole_kv, whole_out = (
        lax.all_gather(w_query, "seq", axis=0, tiled=True),
        lax.all_gather(w_kv, "seq", axis=0, tiled=True),
        lax.all_gather(w_out, "seq", axis=0, tiled=True),
    )
    gate_prob = jax.nn.sigmoid(jnp.dot(token_rows, router, precision=lax.Precision.HIGHEST))
    offset = carried_in(
        jnp.sum(pick_mask), "seq", lambda earlier, later: earlier + later, jnp.int32(0)
    )
    route, sent_rank = route_table(pick_mask, offset, devices_seq, slot_rows)
    send_tokens = select_rows(route, token_half).reshape(devices_seq, slot_rows, MODEL_WIDTH)
    scaled_grad = (gate_prob[:, None] * grad_rows).astype(jnp.bfloat16)
    got_tokens, got_rank = (
        lax.all_to_all(send_tokens, "seq", split_axis=0, concat_axis=0, tiled=True),
        lax.all_to_all(sent_rank, "seq", split_axis=0, concat_axis=0, tiled=True),
    )
    compact = compact_table(got_rank, devices_seq, capacity_rows)
    block_float = select_rows(
        compact, got_tokens.reshape(devices_seq * slot_rows, MODEL_WIDTH)
    ).astype(jnp.float32)
    inv_norm = lax.rsqrt(jnp.mean(block_float * block_float, axis=1, keepdims=True) + EPSILON)
    normed = (block_float * inv_norm * gain[None, :]).astype(jnp.bfloat16)
    normed_cols = lax.all_to_all(normed.T, "seq", split_axis=0, concat_axis=1, tiled=True)
    query_head_rows = jnp.dot(normed, whole_query, preferred_element_type=jnp.float32).astype(
        jnp.bfloat16
    )
    own_kv = jnp.dot(normed, whole_kv, preferred_element_type=jnp.float32).astype(jnp.bfloat16)
    every_key_value = lax.all_gather(own_kv, "seq", axis=0, tiled=True)
    key_total_count = every_key_value.shape[0]
    key_head_rows = every_key_value[:, :key_value_width].reshape(
        key_total_count, KEY_VALUE_HEADS, HEAD_SIZE
    )
    value_head_rows = every_key_value[:, key_value_width:].reshape(
        key_total_count, KEY_VALUE_HEADS, HEAD_SIZE
    )
    query_split_parts = query_head_rows.reshape(
        capacity_rows, KEY_VALUE_HEADS, query_group_size, HEAD_SIZE
    )
    position = lax.broadcasted_iota(jnp.int32, (key_total_count,), 0)
    key_rank = position // capacity_rows + devices_seq * (position % capacity_rows)
    query_rank = my_index + devices_seq * lax.broadcasted_iota(jnp.int32, (capacity_rows,), 0)
    allowed = (key_rank[None, :] <= query_rank[:, None])[:, None, None, :]
    scores = (
        jnp.einsum(
            "cgrd,ngd->cgrn", query_split_parts, key_head_rows, preferred_element_type=jnp.float32
        )
        * head_scale
    )
    scores = jnp.where(allowed, scores, -jnp.inf)
    score_top = jnp.max(scores, axis=3, keepdims=True)
    score_exp = jnp.exp(scores - score_top)
    attn_probs = score_exp / jnp.sum(score_exp, axis=3, keepdims=True)
    probs_half = attn_probs.astype(jnp.bfloat16)
    mixed_heads = jnp.einsum(
        "cgrn,ngd->cgrd", probs_half, value_head_rows, preferred_element_type=jnp.float32
    )
    mixed_heads = mixed_heads.astype(jnp.bfloat16).reshape(capacity_rows, QUERY_HEADS * HEAD_SIZE)
    block_out = jnp.dot(mixed_heads, whole_out, preferred_element_type=jnp.float32).astype(
        jnp.bfloat16
    )
    returned = lax.all_to_all(
        spread_rows(compact, block_out).reshape(devices_seq, slot_rows, MODEL_WIDTH),
        "seq",
        split_axis=0,
        concat_axis=0,
        tiled=True,
    )
    send_grads = select_rows(route, scaled_grad).reshape(devices_seq, slot_rows, MODEL_WIDTH)
    got_grads = lax.all_to_all(send_grads, "seq", split_axis=0, concat_axis=0, tiled=True)
    block_grad = select_rows(compact, got_grads.reshape(devices_seq * slot_rows, MODEL_WIDTH))
    gradient_heads = dot_transposed(block_grad, whole_out).astype(jnp.bfloat16)
    gradient_split = gradient_heads.reshape(
        capacity_rows, KEY_VALUE_HEADS, query_group_size, HEAD_SIZE
    )
    grad_probs = jnp.einsum(
        "cgrd,ngd->cgrn", gradient_split, value_head_rows, preferred_element_type=jnp.float32
    )
    inner_sum = jnp.sum(attn_probs * grad_probs, axis=3, keepdims=True)
    grad_scores = (attn_probs * (grad_probs - inner_sum)).astype(jnp.bfloat16)
    grad_query = (
        jnp.einsum("cgrn,ngd->cgrd", grad_scores, key_head_rows, preferred_element_type=jnp.float32)
        * head_scale
    )
    grad_query = grad_query.astype(jnp.bfloat16).reshape(capacity_rows, QUERY_HEADS * HEAD_SIZE)
    grad_keys = (
        jnp.einsum(
            "cgrn,cgrd->ngd", grad_scores, query_split_parts, preferred_element_type=jnp.float32
        )
        * head_scale
    )
    grad_values = jnp.einsum(
        "cgrn,cgrd->ngd", probs_half, gradient_split, preferred_element_type=jnp.float32
    )
    grad_terms = jnp.concatenate(
        [
            grad_keys.reshape(key_total_count, key_value_width),
            grad_values.reshape(key_total_count, key_value_width),
        ],
        axis=1,
    )
    grad_kv = lax.psum_scatter(grad_terms, "seq", scatter_dimension=0, tiled=True).astype(
        jnp.bfloat16
    )
    grad_normed = dot_transposed(grad_query, whole_query) + dot_transposed(grad_kv, whole_kv)
    upstream = grad_normed * gain[None, :]
    grad_block = inv_norm * upstream - block_float * inv_norm**3 * jnp.mean(
        upstream * block_float, axis=1, keepdims=True
    )
    grad_block = grad_block.astype(jnp.bfloat16)
    returned_grads = lax.all_to_all(
        spread_rows(compact, grad_block).reshape(devices_seq, slot_rows, MODEL_WIDTH),
        "seq",
        split_axis=0,
        concat_axis=0,
        tiled=True,
    )
    out_tokens = spread_rows(route, returned.reshape(devices_seq * slot_rows, MODEL_WIDTH)).astype(
        jnp.float32
    )
    mixed = (token_rows + gate_prob[:, None] * out_tokens).astype(jnp.bfloat16)
    through = jnp.sum(grad_rows * out_tokens, axis=1)
    grad_logit = through * gate_prob * (1.0 - gate_prob)
    router_part = jnp.dot(grad_logit, token_rows, precision=lax.Precision.HIGHEST)
    grad_tokens = spread_rows(
        route, returned_grads.reshape(devices_seq * slot_rows, MODEL_WIDTH)
    ).astype(jnp.float32)
    input_grad = (grad_rows + grad_logit[:, None] * router[None, :] + grad_tokens).astype(
        jnp.bfloat16
    )
    kv_rows = jnp.dot(
        normed_cols,
        lax.all_gather(grad_kv, "seq", axis=0, tiled=True),
        preferred_element_type=jnp.float32,
    )
    router_piece = lax.psum_scatter(router_part, "seq", scatter_dimension=0, tiled=True)
    kv_grad, router_grad = (
        lax.psum(kv_rows.astype(jnp.bfloat16), "dp").astype(jnp.float32),
        lax.psum(router_piece.astype(jnp.bfloat16), "dp").astype(jnp.float32),
    )
    return (mixed[None], input_grad[None], kv_grad, router_grad)


def solution(mesh):
    return jax.shard_map(
        local,
        mesh=mesh,
        in_specs=(
            P("dp", "seq", None),
            P("dp", "seq", None),
            P("dp", "seq"),
            P(),
            P(),
            P("seq", None),
            P("seq", None),
            P("seq", None),
        ),
        out_specs=(P("dp", "seq", None), P("dp", "seq", None), P("seq", None), P("seq")),
        check_vma=False,
    )
```

profile of v0, /device:TPU:0, one launch (start us, length us, event | category | flops | bytes accessed | tf_op | source)
XLA Modules:
  0.0 293.2 jit_solution(4432911283777500641)
XLA Ops:
  9.4 1.3 reduce_sum.54
  10.7 1.4 fusion.67
  12.1 1.4 dynamic-update-slice
  13.5 13.8 %all-reduce = s32[16]{0:T(128)S(1)} all-reduce(s32[16]{0:T(128)S(1)} %dynamic-update-slice), channel_id=1, replica_groups=mesh['dp'=2,'seq'=16] {'seq'}, use_global_device_ids=true, to_apply=%add | all-reduce | flops 16 | bytes 128
  28.2 20.1 %while.13 = (s32[]{:T(128)}, s32[]{:T(128)}, s32[]{:T(128)}, s32[16]{0:T(128)S(1)}, s32[]{:T(128)}) while((s32[]{:T(128)}, s32[]{:T(128)}, s32[]{:T(128)}, s32[16]{0:T(128)S(1)}, s32[]{:T(128)}) %tuple.42), condition=%wide.region_2.3_spmd, body=%wide.region_1.2_spmd.sunk | while | flops 5 | bytes 107 | solution.py:25
  49.8 3.5 %all-to-all-start = ((s32[16,1,2]{2,1,0:T(1,128)}), s32[16,1,2]{2,1,0:T(1,128)S(1)}, u32[]{:S(2)}, u32[]{:S(2)}) async-start(s32[16,1,2]{2,1,0:T(1,128)} %bitcast.8), calls=%async_computation | async-start | bytes 16384 | tf_op jit(solution)/shard_map/all_to_all | solution.py:96
  53.3 1.2 convolution_convert_fusion.5
  54.5 1.6 fusion.21
  56.9 2.7 all-to-all-done
  59.6 3.5 %all-to-all-start.1 = ((bf16[16,2,2048]{2,1,0:T(2,128)(2,1)}), bf16[16,2,2048]{2,1,0:T(2,128)(2,1)S(1)}, u32[]{:S(2)}, u32[]{:S(2)}) async-start(bf16[16,2,2048]{2,1,0:T(2,128)(2,1)} %reshape.185), calls=%async_computation.1 | async-start | bytes 262144 | tf_op jit(solution)/shard_map/all_to_all | solution.py:95
  63.1 1.3 convolution_convert_fusion.3
  65.2 8.1 %all-to-all-done.1 = bf16[16,2,2048]{2,1,0:T(2,128)(2,1)S(1)} async-done(((bf16[16,2,2048]{2,1,0:T(2,128)(2,1)}), bf16[16,2,2048]{2,1,0:T(2,128)(2,1)S(1)}, u32[]{:S(2)}, u32[]{:S(2)}) %all-to-all-start.1) | async-done | bytes 131104 | tf_op jit(solution)/shard_map/all_to_all | solution.py:95
  73.4 3.5 %all-to-all-start.3 = ((bf16[16,2,2048]{2,1,0:T(2,128)(2,1)}), bf16[16,2,2048]{2,1,0:T(2,128)(2,1)S(1)}, u32[]{:S(2)}, u32[]{:S(2)}) async-start(bf16[16,2,2048]{2,1,0:T(2,128)(2,1)} %reshape.193), calls=%async_computation.3 | async-start | bytes 262144 | tf_op jit(solution)/shard_map/all_to_all | solution.py:150
  79.0 5.8 %all-to-all-done.3 = bf16[16,2,2048]{2,1,0:T(2,128)(2,1)S(1)} async-done(((bf16[16,2,2048]{2,1,0:T(2,128)(2,1)}), bf16[16,2,2048]{2,1,0:T(2,128)(2,1)S(1)}, u32[]{:S(2)}, u32[]{:S(2)}) %all-to-all-start.3) | async-done | bytes 131104 | tf_op jit(solution)/shard_map/all_to_all | solution.py:150
  85.8 1.5 convolution_convert_fusion.12
  87.3 18.9 %all_gather.24 = bf16[256,256]{1,0:T(8,128)(2,1)S(1)} all-gather(bf16[16,256]{1,0:T(8,128)(2,1)S(1)} %convolution_convert_fusion.12), channel_id=1, replica_groups=mesh['dp'=2,'seq'=16] {'seq'}, dimensions={0}, use_global_device_ids=true | all-gather | bytes 139264 | tf_op jit(solution)/shard_map/all_gather | solution.py:109
  106.5 2.9 convolution_convert_fusion.11
  109.5 47.3 %all-gather.8.cloned.1.call-done = bf16[1024,2048]{1,0:T(8,128)(2,1)} async-done(((bf16[64,2048]{1,0:T(8,128)(2,1)}), bf16[1024,2048]{1,0:T(8,128)(2,1)}) %all-gather.8.cloned.1.call-update) | async-done | bytes 4194320 | tf_op jit(solution)/shard_map/all_gather | solution.py:85
  156.8 3.4 %fusion.17 = bf16[16,1024]{1,0:T(8,128)(2,1)S(1)} fusion(bf16[1024,2048]{1,0:T(8,128)(2,1)} %all-gather.8.cloned.1.call-done, bf16[32,2048]{1,0:T(8,128)(2,1)S(1)} %reshape.194, s32[32]{0:T(128)S(1)} %compare_select_fusion.2), kind=kOutput, calls=%fused_computation.36 | convolution fusion | flops 69255680 | bytes 4358272 | tf_op jit(solution)/shard_map/dot_general | solution.py:29
  163.1 3.1 %convolution_convert_fusion.4 = bf16[32,2048]{1,0:T(8,128)(2,1)S(1)} fusion(bf16[16,1024]{1,0:T(8,128)(2,1)S(1)} %reshape.190, bf16[1024,2048]{1,0:T(8,128)(2,1)} %all-gather.8.cloned.1.call-done, s32[32]{0:T(128)S(1)} %compare_select_fusion.2), kind=kOutput, calls=%fused_computation.10 | convolution fusion | flops 69304832 | bytes 4358272 | tf_op jit(solution)/shard_map/dot_general | solution.py:63
  167.0 3.5 %all-to-all-start.2 = ((bf16[16,2,2048]{2,1,0:T(2,128)(2,1)}), bf16[16,2,2048]{2,1,0:T(2,128)(2,1)S(1)}, u32[]{:S(2)}, u32[]{:S(2)}) async-start(bf16[16,2,2048]{2,1,0:T(2,128)(2,1)} %reshape.191), calls=%async_computation.2 | async-start | bytes 262144 | tf_op jit(solution)/shard_map/all_to_all | solution.py:142
  170.5 3.4 %fusion.71 = f32[16,2048]{1,0:T(8,128)S(1)} fusion(bf16[16,1024]{1,0:T(8,128)(2,1)S(1)} %reshape.196, bf16[2048,1024]{1,0:T(8,128)(2,1)} %all-gather.6.cloned.1.call-done), kind=kOutput, calls=%fused_computation.124 | convolution fusion | flops 67108864 | bytes 4358144 | tf_op jit(solution)/shard_map/dot_general | solution.py:29
  173.9 4.4 %all-to-all-done.2 = bf16[16,2,2048]{2,1,0:T(2,128)(2,1)S(1)} async-done(((bf16[16,2,2048]{2,1,0:T(2,128)(2,1)}), bf16[16,2,2048]{2,1,0:T(2,128)(2,1)S(1)}, u32[]{:S(2)}, u32[]{:S(2)}) %all-to-all-start.2) | async-done | bytes 131104 | tf_op jit(solution)/shard_map/all_to_all | solution.py:142
  178.4 3.5 %all-to-all-start.5 = ((bf16[16,128,16]{1,2,0:T(8,128)(2,1)}), bf16[16,128,16]{1,2,0:T(8,128)(2,1)S(1)}, u32[]{:S(2)}, u32[]{:S(2)}) async-start(bf16[16,128,16]{1,2,0:T(8,128)(2,1)} %copy_bitcast_fusion), calls=%async_computation.5 | async-start | bytes 131072 | tf_op jit(solution)/shard_map/all_to_all | solution.py:104
  181.9 1.3 fusion.22
  183.3 34.0 %reduce-scatter.4.cloned.1.call-done = f32[16,256]{1,0:T(8,128)} async-done(((f32[256,256]{1,0:T(8,128)}), f32[16,256]{1,0:T(8,128)}) %reduce-scatter.4.cloned.1.call-update) | async-done | bytes 16400
  219.7 19.8 %all_gather.27 = bf16[256,256]{1,0:T(8,128)(2,1)S(1)} all-gather(bf16[16,256]{1,0:T(8,128)(2,1)S(1)} %copy.50), channel_id=1, replica_groups=mesh['dp'=2,'seq'=16] {'seq'}, dimensions={0}, use_global_device_ids=true | all-gather | bytes 139264 | tf_op jit(solution)/shard_map/all_gather | solution.py:213
  239.4 3.5 %all-to-all-start.4 = ((bf16[16,2,2048]{2,1,0:T(2,128)(2,1)}), bf16[16,2,2048]{2,1,0:T(2,128)(2,1)S(1)}, u32[]{:S(2)}, u32[]{:S(2)}) async-start(bf16[16,2,2048]{2,1,0:T(2,128)(2,1)} %reshape.199), calls=%async_computation.4 | async-start | bytes 262144 | tf_op jit(solution)/shard_map/all_to_all | solution.py:191
  244.2 34.3 %all-reduce.1 = bf16[2048]{0:T(1024)(128)(2,1)S(1)} all-reduce(f32[2048]{0:T(1024)S(1)} %bitcast.132), channel_id=3, replica_groups=mesh['dp'=2,'seq'=16] {'seq'}, use_global_device_ids=true, to_apply=%region_13.14.clone | all-reduce | flops 2048 | bytes 12288
  278.6 4.9 %psum.15 = bf16[128]{0:T(256)(128)(2,1)S(1)} all-reduce(bf16[128]{0:T(256)(128)(2,1)S(1)} %dynamic-slice.4), channel_id=1, replica_groups=mesh['dp'=2,'seq'=16] {'dp'}, use_global_device_ids=true, to_apply=%region_14.15 | all-reduce | flops 128 | bytes 512 | tf_op jit(solution)/shard_map/psum | solution.py:219
  284.0 1.5 convert_element_type.140
  285.6 1.1 fusion.5
  (92 shorter events, 26.2 us)
Async XLA Ops:
  7.2 77.9 %copy-start.3 = (f32[2048]{0:T(1024)S(1)}, f32[2048]{0:T(1024)}, u32[]{:S(2)}) copy-start(f32[2048]{0:T(1024)} %param.13) | copy-start | bytes 24580
  7.2 78.6 %all-gather.4.cloned.1.call-start = ((), (), s32[]{:S(2)}) async-start(), calls=%async_computation.7 | async-start | bytes 1114112 | tf_op jit(solution)/shard_map/all_gather | solution.py:84
  7.9 98.6 %all-gather.6.cloned.1.call-start = ((), (), s32[]{:S(2)}) async-start(), calls=%async_computation.8 | async-start | bytes 4456448 | tf_op jit(solution)/shard_map/all_gather | solution.py:83
  8.7 148.2 %all-gather.8.cloned.1.call-start = ((), (), s32[]{:S(2)}) async-start(), calls=%async_computation.9 | async-start | bytes 4456448 | tf_op jit(solution)/shard_map/all_gather | solution.py:85
  49.8 9.8 %all-to-all-start = ((s32[16,1,2]{2,1,0:T(1,128)}), s32[16,1,2]{2,1,0:T(1,128)S(1)}, u32[]{:S(2)}, u32[]{:S(2)}) async-start(s32[16,1,2]{2,1,0:T(1,128)} %bitcast.8), calls=%async_computation | async-start | bytes 16384 | tf_op jit(solution)/shard_map/all_to_all | solution.py:96
  59.6 13.8 %all-to-all-start.1 = ((bf16[16,2,2048]{2,1,0:T(2,128)(2,1)}), bf16[16,2,2048]{2,1,0:T(2,128)(2,1)S(1)}, u32[]{:S(2)}, u32[]{:S(2)}) async-start(bf16[16,2,2048]{2,1,0:T(2,128)(2,1)} %reshape.185), calls=%async_computation.1 | async-start | bytes 262144 | tf_op jit(solution)/shard_map/all_to_all | solution.py:95
  73.4 11.4 %all-to-all-start.3 = ((bf16[16,2,2048]{2,1,0:T(2,128)(2,1)}), bf16[16,2,2048]{2,1,0:T(2,128)(2,1)S(1)}, u32[]{:S(2)}, u32[]{:S(2)}) async-start(bf16[16,2,2048]{2,1,0:T(2,128)(2,1)} %reshape.193), calls=%async_computation.3 | async-start | bytes 262144 | tf_op jit(solution)/shard_map/all_to_all | solution.py:150
  76.9 140.3 %reduce-scatter.4.cloned.1.call-start = ((), (), s32[]{:S(2)}) async-start(), calls=%async_computation.11 | async-start | bytes 278528
  163.1 18.8 %copy-start = (bf16[1,128,2048]{2,1,0:T(8,128)(2,1)S(1)}, bf16[1,128,2048]{2,1,0:T(8,128)(2,1)}, u32[]{:S(2)}) copy-start(bf16[1,128,2048]{2,1,0:T(8,128)(2,1)} %param.10) | copy-start | bytes 1572868
  163.1 18.8 %copy-start.1 = (bf16[1,128,2048]{2,1,0:T(8,128)(2,1)S(1)}, bf16[1,128,2048]{2,1,0:T(8,128)(2,1)}, u32[]{:S(2)}) copy-start(bf16[1,128,2048]{2,1,0:T(8,128)(2,1)} %param.11) | copy-start | bytes 1572868
  166.2 51.9 %copy-start.2 = (bf16[2048,256]{1,0:T(8,128)(2,1)S(1)}, bf16[2048,256]{1,0:T(8,128)(2,1)}, u32[]{:S(2)}) copy-start(bf16[2048,256]{1,0:T(8,128)(2,1)} %all-gather.4.cloned.1.call-done) | copy-start | bytes 3145732
  167.0 11.4 %all-to-all-start.2 = ((bf16[16,2,2048]{2,1,0:T(2,128)(2,1)}), bf16[16,2,2048]{2,1,0:T(2,128)(2,1)S(1)}, u32[]{:S(2)}, u32[]{:S(2)}) async-start(bf16[16,2,2048]{2,1,0:T(2,128)(2,1)} %reshape.191), calls=%async_computation.2 | async-start | bytes 262144 | tf_op jit(solution)/shard_map/all_to_all | solution.py:142
  170.5 115.1 %copy-start.4 = (f32[2048]{0:T(1024)S(1)}, f32[2048]{0:T(1024)}, u32[]{:S(2)}) copy-start(f32[2048]{0:T(1024)} %param.14) | copy-start | bytes 24580
  178.4 61.1 %all-to-all-start.5 = ((bf16[16,128,16]{1,2,0:T(8,128)(2,1)}), bf16[16,128,16]{1,2,0:T(8,128)(2,1)S(1)}, u32[]{:S(2)}, u32[]{:S(2)}) async-start(bf16[16,128,16]{1,2,0:T(8,128)(2,1)} %copy_bitcast_fusion), calls=%async_computation.5 | async-start | bytes 131072 | tf_op jit(solution)/shard_map/all_to_all | solution.py:104
  239.4 46.1 %all-to-all-start.4 = ((bf16[16,2,2048]{2,1,0:T(2,128)(2,1)}), bf16[16,2,2048]{2,1,0:T(2,128)(2,1)S(1)}, u32[]{:S(2)}, u32[]{:S(2)}) async-start(bf16[16,2,2048]{2,1,0:T(2,128)(2,1)} %reshape.199), calls=%async_computation.4 | async-start | bytes 262144 | tf_op jit(solution)/shard_map/all_to_all | solution.py:191
  243.0 41.0 %all-reduce.4.cloned.1.call-start = ((), (), s32[]{:S(2)}) async-start(), calls=%async_computation.10 | async-start | bytes 131072 | tf_op jit(solution)/shard_map/psum | solution.py:218
Sparse Core Ops, SparseCore 0:
  10.1 40.5 all-gather.3
  52.9 52.0 all-gather.5
  107.3 49.5 all-gather.7
  163.0 54.2 reduce-scatter.3
  246.3 22.1 all-reduce.3
where the time goes:
time: 294 us; the launch traced here: 293 us
  waiting for transfers between devices  104 us (35%)
  blocking collectives  91.7 us (31%)
  matrix products  24.4 us (8%)
  starting transfers between devices  21.2 us (7%)
  local copies, waits for them, and re-layouts  19.3 us (7%)
  between operations  14.7 us (5%)
  loops' own time  10.7 us (4%)
  other arithmetic  6.71 us (2%)
    unnamed x2, blocking collectives  48.1 us
    all_gather x1, waiting for transfers between devices, local(): lax.all_gather(w_out, 'seq', axis=0, tiled=True)  47.3 us
    unnamed x6, waiting for transfers between devices  36 us
    all_gather x1, blocking collectives, local(): lax.all_gather(grad_kv, 'seq', axis=0, tiled=True)  19.8 us
    all_gather x1, blocking collectives, local(): every_key_value = lax.all_gather(own_kv, 'seq', axis=0, tiled=True)  18.9 us
    another operation x1, loops' own time, carried_in(): return lax.fori_loop(0, peers, lap, start)  10.7 us
    dynamic_slice x16, local copies, waits for them, and re-layouts, lap(): new = combine(before, everything[k])  9.38 us
    all_to_all x1, waiting for transfers between devices, local(): lax.all_to_all(send_tokens, 'seq', split_axis=0, concat_axis=0, tiled=True)  8.13 us
  transfers between devices with their start and end apart: 11, of which 6 were waited for; matrix products, arithmetic and copies ran while one was open for 15% of the time, Pallas kernels for 0%

commit v1 on v0

v1 whole, which is shorter than its diff:
```python
import functools

import jax
import jax.numpy as jnp
from jax import lax
from jax.experimental import pallas as pl
from jax.experimental.pallas import tpu as pltpu
from jax.sharding import Mesh, PartitionSpec as P

MODEL_WIDTH = 2048
QUERY_HEADS = 16
KEY_VALUE_HEADS = 2
HEAD_SIZE = 64
GROUP = QUERY_HEADS // KEY_VALUE_HEADS
KV_WIDTH = 2 * KEY_VALUE_HEADS * HEAD_SIZE
Q_WIDTH = QUERY_HEADS * HEAD_SIZE
EPSILON = 1e-05
EMPTY = 2.0**100
PLANE = 4
SEQ = ("zz", "pp")

F32 = jnp.float32
BF16 = jnp.bfloat16


def dot(a, b, ca=1, cb=0):
    return lax.dot_general(a, b, (((ca,), (cb,)), ((), ())), preferred_element_type=F32)


def iota(shape, dim):
    return lax.broadcasted_iota(jnp.int32, shape, dim)


def call(body, name, out_shape, *args, scalars=(), scratch=()):
    vmem = pl.BlockSpec(memory_space=pltpu.VMEM)
    smem = pl.BlockSpec(memory_space=pltpu.SMEM)
    return pl.pallas_call(
        body,
        name=name,
        out_shape=out_shape,
        in_specs=[smem] * len(scalars) + [vmem] * len(args),
        out_specs=jax.tree.map(lambda _: vmem, out_shape),
        scratch_shapes=list(scratch),
    )(*scalars, *args)


def shaped(shape, dtype):
    return jax.ShapeDtypeStruct(shape, dtype)


def selection(picks, slots):
    tokens = picks.shape[1]
    picked = jnp.broadcast_to(picks.astype(F32), (8, tokens)).astype(BF16)
    before = (iota((tokens, tokens), 0) < iota((tokens, tokens), 1)).astype(F32).astype(BF16)
    rank = dot(picked, before)[:1].astype(jnp.int32)
    hit = (iota((slots, tokens), 0) == rank) & (picks > 0)
    return hit.astype(F32).astype(BF16)


def pick_kernel(h_ref, c_ref, picks_ref, gain_ref, router_ref, send_ref, gate_ref, x_ref, inv_ref, *, slots, fb):
    lines = send_ref.shape[0] // PLANE
    hidden = h_ref[...].astype(F32)
    logit = jnp.sum(hidden * router_ref[...], axis=1, keepdims=True)
    gate = 1.0 / (1.0 + jnp.exp(-logit))
    gate_ref[...] = gate
    picks = picks_ref[...]
    sel = selection(picks, slots)
    scaled = (gate * c_ref[...].astype(F32)).astype(BF16)
    x = dot(sel, h_ref[...])
    grads = dot(sel, scaled).astype(BF16)
    inv = lax.rsqrt(jnp.mean(x * x, axis=1, keepdims=True) + EPSILON)
    x_ref[...] = x.astype(BF16)
    inv_ref[...] = inv
    normed = x * inv * gain_ref[...]
    count = jnp.sum(picks)
    normed = jnp.where(iota((slots, 1), 0) < count, normed, EMPTY).astype(BF16)
    for p in range(PLANE):
        blocks = [slice((PLANE * z + p) * fb, (PLANE * z + p + 1) * fb) for z in range(lines)]
        part = jnp.concatenate([normed[:, b] for b in blocks] + [grads[:, b] for b in blocks], axis=1)
        for z in range(lines):
            send_ref[PLANE * z + p] = part


def heads_kernel(
    p_ref, got_ref, wqkv_ref, wout_ref, keep_ref, send_ref, keep_kv_ref, send_kv_ref, normed_ref, place_ref, *, rows, cpd, kpd
):
    slots, width = got_ref.shape
    half = width // 2
    valid = got_ref[:, :1].astype(F32) < EMPTY / 2
    ones = jnp.broadcast_to(jnp.where(valid, 1.0, 0.0), (slots, 128)).astype(BF16)
    earlier = (iota((slots, slots), 1) < iota((slots, slots), 0)).astype(F32).astype(BF16)
    rank = dot(earlier, ones)[:, :1].astype(jnp.int32)
    rank = jnp.where(valid, rank, -1)
    place = (rank == iota((slots, rows), 1)).astype(F32).astype(BF16)
    place_ref[...] = place
    compact = dot(place, got_ref[...], 0, 0).astype(BF16)
    normed, grads = compact[:, :half], compact[:, half:]
    lines, _, fb = normed_ref.shape
    for z in range(lines):
        normed_ref[z] = normed[:, z * fb : (z + 1) * fb]
    query = dot(normed, wqkv_ref[:, : PLANE * cpd])
    grad_heads = dot(grads, wout_ref[...], 1, 1)
    kv = dot(wqkv_ref[:, PLANE * cpd :], normed, 0, 1)
    for pp in range(PLANE):
        cols = slice(pp * cpd, (pp + 1) * cpd)
        both = jnp.concatenate([query[:, cols], grad_heads[:, cols]], axis=1)
        kv_part = kv[pp * kpd : (pp + 1) * kpd]
        away = p_ref[0] ^ pp

        @pl.when(away % 2 == 0)
        def _():
            keep_ref[away // 2] = both
            keep_kv_ref[away // 2] = kv_part

        @pl.when(away % 2 == 1)
        def _():
            send_ref[away // 2] = both
            send_kv_ref[away // 2] = kv_part


def attention_kernel(
    z_ref, qg_ref, kv_ref, wq_ref, wkv_ref, wout_ref, gain_ref, normed_ref, place_ref,
    send_ref, kvg_ref, mixed_ref, gq_ref, gkv_ref, *, step
):
    rows = qg_ref.shape[1]
    n, slots, _ = send_ref.shape
    fb = wq_ref.shape[0]
    scale = HEAD_SIZE**-0.5
    span = GROUP // 2
    gkv_ref[...] = jnp.zeros(gkv_ref.shape, F32)

    def one_head(head, group, start):
        kt = kv_ref[pl.ds(group * HEAD_SIZE, HEAD_SIZE), :]
        vt = kv_ref[pl.ds((KEY_VALUE_HEADS + group) * HEAD_SIZE, HEAD_SIZE), :]
        zero = jnp.zeros_like(kt)
        qg = qg_ref[head, pl.ds(start, step), :]
        scores = dot(qg, jnp.concatenate([kt, zero], axis=0)) * scale
        allowed = iota((step, rows), 1) <= iota((step, rows), 0) + start
        scores = jnp.where(allowed, scores, -jnp.inf)
        e = jnp.exp(scores - jnp.max(scores, axis=1, keepdims=True))
        probs = e / jnp.sum(e, axis=1, keepdims=True)
        probs_half = probs.astype(BF16)
        mixed = dot(probs_half, vt, 1, 1)
        gp = dot(qg, jnp.concatenate([zero, vt], axis=0))
        inner = jnp.sum(probs * gp, axis=1, keepdims=True)
        gs = (probs * (gp - inner)).astype(BF16)
        gq = dot(gs, kt, 1, 1) * scale
        gk = dot(qg, gs, 0, 0)[:HEAD_SIZE] * scale
        gv = dot(qg, probs_half, 0, 0)[HEAD_SIZE:]
        gkv_ref[pl.ds(group * HEAD_SIZE, HEAD_SIZE), :] += gk
        gkv_ref[pl.ds((KEY_VALUE_HEADS + group) * HEAD_SIZE, HEAD_SIZE), :] += gv
        return mixed, gq

    def pair(j, start):
        group = j // span
        m0, g0 = one_head(2 * j, group, start)
        m1, g1 = one_head(2 * j + 1, group, start)
        lanes = pl.ds(j * 2 * HEAD_SIZE, 2 * HEAD_SIZE)
        mixed_ref[pl.ds(start, step), lanes] = jnp.concatenate([m0, m1], axis=1).astype(BF16)
        gq_ref[pl.ds(start, step), lanes] = jnp.concatenate([g0, g1], axis=1).astype(BF16)

    if rows == step:
        for j in range(QUERY_HEADS // 2):
            pair(j, 0)
    else:

        @pl.loop(0, QUERY_HEADS // 2)
        def _(j):
            @pl.loop(0, rows // step)
            def _(b):
                pair(j, pl.multiple_of(b * step, step))

    place = place_ref[...]
    out = dot(mixed_ref[...], wout_ref[...]).astype(BF16)
    gkv = gkv_ref[...].astype(BF16)
    up = (dot(gq_ref[...], wq_ref[...], 1, 1) + dot(gkv, wkv_ref[...], 0, 1)) * gain_ref[...]
    kvg_ref[...] = dot(normed_ref[z_ref[0]], gkv, 0, 1)
    high = up.astype(BF16)
    low = (up - high.astype(F32)).astype(BF16)
    for k, piece in enumerate((out, high, low)):
        spread = dot(place, piece).astype(BF16)
        for d in range(n):
            send_ref[d, :, k * fb : (k + 1) * fb] = spread[d * slots : (d + 1) * slots]


def finish_kernel(
    h_ref, c_ref, picks_ref, router_ref, gate_ref, x_ref, inv_ref, got_ref, mixed_ref, grad_ref, router_grad_ref
):
    n, slots, width = got_ref.shape
    fb = width // 3
    sel = selection(picks_ref[...], slots)
    take = lambda k: jnp.concatenate([got_ref[d, :, k * fb : (k + 1) * fb] for d in range(n)], axis=1)
    out = dot(sel, take(0), 0, 0)
    gate = gate_ref[...]
    hidden = h_ref[...].astype(F32)
    cotangent = c_ref[...].astype(F32)
    mixed_ref[...] = (hidden + gate * out).astype(BF16)
    through = jnp.sum(cotangent * out, axis=1, keepdims=True)
    grad_logit = through * gate * (1.0 - gate)
    router_grad_ref[...] = jnp.sum(grad_logit * hidden, axis=0, keepdims=True)
    up = take(1).astype(F32) + take(2).astype(F32)
    x = x_ref[...].astype(F32)
    inv = inv_ref[...]
    grad_block = inv * up - x * inv**3 * jnp.mean(up * x, axis=1, keepdims=True)
    grad_tokens = dot(sel, grad_block.astype(BF16), 0, 0)
    grad_ref[...] = (cotangent + grad_logit * router_ref[...] + grad_tokens).astype(BF16)


def swap(x, n, bit):
    return lax.ppermute(x, SEQ, [(i, i ^ bit) for i in range(n)])


def local(hidden, cotangent, picks, gain, router, w_query, w_kv, w_out):
    lines = lax.axis_size("zz")
    n = lines * PLANE
    dp = lax.axis_size("dp")
    z, p = lax.axis_index("zz"), lax.axis_index("pp")
    me = (PLANE * z + p).astype(jnp.int32)
    hidden, cotangent = hidden[0], cotangent[0]
    tokens = hidden.shape[0]
    slots = tokens // 4
    rows = n * (tokens // 8)
    fb = MODEL_WIDTH // n
    cpd = Q_WIDTH // n
    kpd = KV_WIDTH // n
    as_row = lambda v: v.reshape(1, -1)
    scalar = lambda v: v.astype(jnp.int32).reshape(1)

    wqkv = jnp.concatenate(
        [w_query.reshape(fb, lines, PLANE * cpd), w_kv.reshape(fb, lines, PLANE * kpd)], axis=2
    ).transpose(1, 0, 2)
    wqkv = lax.all_to_all(wqkv, "zz", 0, 0, tiled=True).reshape(lines * fb, PLANE * (cpd + kpd))
    wout_rows = w_out.reshape(cpd, lines, PLANE, fb).transpose(2, 0, 1, 3).reshape(PLANE, cpd, lines * fb)
    wout_rows = lax.all_to_all(wout_rows, "pp", 0, 0, tiled=True).reshape(PLANE * cpd, lines * fb)
    wout_cols = w_out.reshape(cpd, n, fb).transpose(1, 0, 2)
    wout_cols = lax.all_to_all(wout_cols, SEQ, 0, 0, tiled=True).reshape(Q_WIDTH, fb)

    send, gate, x, inv = call(
        functools.partial(pick_kernel, slots=slots, fb=fb),
        "pick",
        (
            shaped((n, slots, 2 * lines * fb), BF16),
            shaped((tokens, 1), F32),
            shaped((slots, MODEL_WIDTH), BF16),
            shaped((slots, 1), F32),
        ),
        hidden,
        cotangent,
        picks,
        as_row(gain),
        as_row(router),
    )
    got = lax.all_to_all(send, SEQ, 0, 0, tiled=True).reshape(n * slots, 2 * lines * fb)
    qg_shape, kv_shape = (2, rows, 2 * cpd), (2, kpd, rows)
    keep, away, keep_kv, away_kv, normed, place = call(
        functools.partial(heads_kernel, rows=rows, cpd=cpd, kpd=kpd),
        "heads",
        (
            shaped(qg_shape, F32),
            shaped(qg_shape, F32),
            shaped(kv_shape, F32),
            shaped(kv_shape, F32),
            shaped((lines, rows, fb), BF16),
            shaped((n * slots, rows), BF16),
        ),
        got,
        wqkv,
        wout_rows,
        scalars=(scalar(p),),
    )
    keep = keep + swap(away, n, 1)
    keep_kv = keep_kv + swap(away_kv, n, 1)
    qg = (keep[0] + swap(keep[1], n, 2)).astype(BF16)
    kv = (keep_kv[0] + swap(keep_kv[1], n, 2)).astype(BF16)
    packed = jnp.concatenate([qg, kv.reshape(-1, 2 * cpd)], axis=0)

    everything = packed[None]
    if lines == 4:
        everything = jnp.stack([packed] + [swap(packed, n, PLANE * k) for k in range(1, lines)])
        everything = jnp.concatenate([everything[k : k + 1] for k in range(lines)], axis=0)
        index = z ^ jnp.arange(lines)
        everything = everything[index]
    else:
        everything = lax.all_gather(packed, "zz", axis=0)
    everything = everything[:, None]
    for bit in (2, 1):
        other = swap(everything, n, bit)
        first = (p & bit) == 0
        everything = jnp.where(
            first,
            jnp.concatenate([everything, other], axis=1),
            jnp.concatenate([other, everything], axis=1),
        )
    everything = everything.reshape((lines, 2, 2) + packed.shape).transpose(0, 2, 1, 3, 4)
    everything = everything.reshape((n,) + packed.shape)
    qg_all = everything[:, :rows]
    kv_all = everything[:, rows:].reshape(KV_WIDTH, rows)
    if cpd != HEAD_SIZE:
        per = HEAD_SIZE // cpd
        qg_all = qg_all.reshape(QUERY_HEADS, per, rows, 2, cpd).transpose(0, 2, 3, 1, 4)
        qg_all = qg_all.reshape(QUERY_HEADS, rows, 2 * HEAD_SIZE)

    send, kv_part = call(
        functools.partial(attention_kernel, step=min(rows, 256)),
        "attention",
        (shaped((n, slots, 3 * fb), BF16), shaped((fb, KV_WIDTH), F32)),
        qg_all,
        kv_all,
        w_query,
        w_kv,
        wout_cols,
        as_row(lax.dynamic_slice(gain, (me * fb,), (fb,))),
        normed,
        place,
        scalars=(scalar(z),),
        scratch=(
            pltpu.VMEM((rows, Q_WIDTH), BF16),
            pltpu.VMEM((rows, Q_WIDTH), BF16),
            pltpu.VMEM((KV_WIDTH, rows), F32),
        ),
    )
    got = lax.all_to_all(send, SEQ, 0, 0, tiled=True)
    if dp == 2:
        kv_grad = kv_part + lax.ppermute(kv_part, "dp", [(0, 1), (1, 0)])
    else:
        kv_grad = lax.psum(kv_part, "dp")
    mixed, input_grad, router_part = call(
        finish_kernel,
        "finish",
        (
            shaped((tokens, MODEL_WIDTH), BF16),
            shaped((tokens, MODEL_WIDTH), BF16),
            shaped((1, MODEL_WIDTH), F32),
        ),
        hidden,
        cotangent,
        picks,
        as_row(router),
        gate,
        x,
        inv,
        got,
    )
    parts = jnp.broadcast_to(router_part.reshape(1, n, fb), (dp, n, fb)).reshape(dp * n, fb)
    parts = lax.all_to_all(parts, ("dp",) + SEQ, 0, 0, tiled=True)
    router_grad = jnp.sum(parts, axis=0)
    return mixed[None], input_grad[None], kv_grad, router_grad


def solution(mesh):
    dp, n = mesh.shape["dp"], mesh.shape["seq"]
    split = Mesh(mesh.devices.reshape(dp, n // PLANE, PLANE), ("dp",) + SEQ)
    rows = P("dp", SEQ, None)
    return jax.shard_map(
        local,
        mesh=split,
        in_specs=(rows, rows, P("dp", SEQ), P(), P(), P(SEQ, None), P(SEQ, None), P(SEQ, None)),
        out_specs=(rows, rows, P(SEQ, None), P(SEQ)),
        check_vma=False,
    )
```

time: 294 us -> 150 us (0.51)
  blocking collectives: 91.7 us -> 0 us
  waiting for transfers between devices: 104 us -> 77.7 us
  matrix products: 24.4 us -> 0 us
  Pallas kernels: 0 us -> 21.1 us
  between operations: 14.7 us -> 0.84 us
  starting transfers between devices: 21.2 us -> 33.6 us
  loops' own time: 10.7 us -> 0 us
  local copies, waits for them, and re-layouts: 19.3 us -> 11.7 us
    unnamed x2 -> x0, blocking collectives: 48.1 us -> none
    all_gather x3 -> x0, waiting for transfers between devices: 47.4 us -> none  [the longest x1 47.3 us: local(): lax.all_gather(w_out, 'seq', axis=0, tiled=True)]
    all_gather x2 -> x0, blocking collectives: 38.7 us -> none  [the longest x1 19.8 us: local(): lax.all_gather(grad_kv, 'seq', axis=0, tiled=True)]
    all_to_all x6, waiting for transfers between devices: 21.1 us -> 57.8 us  [the longest x1 21.9 us: local(): lax.all_to_all(send, SEQ, 0, 0, tiled=True)]
    unnamed x6 -> x0, waiting for transfers between devices: 36 us -> none
    dot_general x20 -> x0, matrix products: 24.1 us -> none  [the longest x3 7.35 us: dot_transposed(): lax.dot_general(left, right, (((1,), (1,)), ((), ())), preferred_element_...]
    pallas_call x0 -> x4, Pallas kernels: none -> 21.1 us  [call(): pl.pallas_call(body, name=name, out_shape=out_shape, in_specs=[smem] * le...]
    ppermute x0 -> x10, waiting for transfers between devices: none -> 19.9 us  [the longest x9 19.9 us: swap(): return lax.ppermute(x, SEQ, [(i, i ^ bit) for i in range(n)])]
  transfers between devices with their start and end apart: 11 -> 16, of which waited for: 6 -> 12; matrix products, arithmetic and copies ran while one was open for 15% -> 7% of each run, Pallas kernels for 0% -> 4%
where the time goes in v1:
time: 150 us; the launch traced here: 149 us
  waiting for transfers between devices  77.7 us (52%)
  starting transfers between devices  33.6 us (22%)
  Pallas kernels  21.1 us (14%)
  local copies, waits for them, and re-layouts  11.7 us (8%)
  other arithmetic  4.1 us (3%)
    all_to_all x1, waiting for transfers between devices, local(): lax.all_to_all(send, SEQ, 0, 0, tiled=True)  21.9 us
    pallas_call x4, Pallas kernels, call(): pl.pallas_call(body, name=name, out_shape=out_shape, in_specs=[smem] * le...  21.1 us
    ppermute x9, waiting for transfers between devices, swap(): return lax.ppermute(x, SEQ, [(i, i ^ bit) for i in range(n)])  19.9 us
    all_to_all x1, waiting for transfers between devices, local(): got = lax.all_to_all(send, SEQ, 0, 0, tiled=True)  10.6 us
    ppermute x9, starting transfers between devices, swap(): return lax.ppermute(x, SEQ, [(i, i ^ bit) for i in range(n)])  7.89 us
    all_to_all x1, waiting for transfers between devices, local(): lax.all_to_all(wqkv, 'zz', 0, 0, tiled=True)  7.31 us
    all_to_all x1, waiting for transfers between devices, local(): lax.all_to_all(wout_cols, SEQ, 0, 0, tiled=True).reshape(Q_WIDTH, fb)  6.56 us
    all_to_all x1, waiting for transfers between devices, local(): parts = lax.all_to_all(parts, ('dp',) + SEQ, 0, 0, tiled=True)  6.48 us
  transfers between devices with their start and end apart: 16, of which 12 were waited for; matrix products, arithmetic and copies ran while one was open for 7% of the time, Pallas kernels for 4%

profile of v1, /device:TPU:0, one launch (start us, length us, event | category | flops | bytes accessed | tf_op | source)
XLA Modules:
  0.0 149.0 jit_solution(12346661430839899308)
XLA Ops:
  0.7 1.2 reshape.95
  1.9 0.8 reshape.96
  2.7 4.3 %all-to-all-start.2 = ((bf16[4,64,512]{2,1,0:T(8,128)(2,1)}), bf16[4,64,512]{2,1,0:T(8,128)(2,1)S(1)}, u32[]{:S(2)}, u32[]{:S(2)}) async-start(bf16[4,64,512]{2,1,0:T(8,128)(2,1)} %reshape.96), calls=%async_computation.2 | async-start | bytes 524288 | tf_op jit(solution)/shard_map/all_to_all | solution.py:234
  8.1 4.9 %all-to-all-done.2 = bf16[4,64,512]{2,1,0:T(8,128)(2,1)S(1)} async-done(((bf16[4,64,512]{2,1,0:T(8,128)(2,1)}), bf16[4,64,512]{2,1,0:T(8,128)(2,1)S(1)}, u32[]{:S(2)}, u32[]{:S(2)}) %all-to-all-start.2) | async-done | bytes 262176 | tf_op jit(solution)/shard_map/all_to_all | solution.py:234
  13.0 5.5 %all-to-all-start.1 = ((bf16[4,128,320]{1,2,0:T(8,128)(2,1)}), bf16[4,128,320]{1,2,0:T(8,128)(2,1)S(1)}, u32[]{:S(2)}, u32[]{:S(2)}) async-start(bf16[4,128,320]{1,2,0:T(8,128)(2,1)} %maximum_bitcast_fusion), calls=%async_computation.1 | async-start | bytes 655360 | tf_op jit(solution)/shard_map/all_to_all | solution.py:232
  18.5 2.7 %pick.1 = (bf16[16,32,1024]{2,1,0:T(8,128)(2,1)}, f32[128,1]{1,0:T(8,128)}, bf16[32,2048]{1,0:T(8,128)(2,1)}, f32[32,1]{1,0:T(8,128)}) custom-call(bf16[128,2048]{1,0:T(8,128)(2,1)} %bitcast.60, bf16[128,2048]{1,0:T(8,128)(2,1)} %bitcast.62, s32[1,128]{1,0:T(1,128)} %picks_ref.3, f32[1,2048]{1,0:T(1,128)} %bitcast.77, f32[1,2048]{1,0:T(1,128)} %bitcast.75), custom_call_target="tpu_custom_call" | custom-call | tf_op jit(solution)/shard_map/pick/pallas_call | solution.py:37
  21.2 7.3 %all-to-all-done.1 = bf16[4,128,320]{1,2,0:T(8,128)(2,1)S(1)} async-done(((bf16[4,128,320]{1,2,0:T(8,128)(2,1)}), bf16[4,128,320]{1,2,0:T(8,128)(2,1)S(1)}, u32[]{:S(2)}, u32[]{:S(2)}) %all-to-all-start.1) | async-done | bytes 327712 | tf_op jit(solution)/shard_map/all_to_all | solution.py:232
  28.5 3.7 %all-to-all-start = ((bf16[16,32,1024]{2,1,0:T(8,128)(2,1)}), bf16[16,32,1024]{2,1,0:T(8,128)(2,1)S(1)}, u32[]{:S(2)}, u32[]{:S(2)}) async-start(bf16[16,32,1024]{2,1,0:T(8,128)(2,1)} %get-tuple-element.22), calls=%async_computation | async-start | bytes 2097152 | tf_op jit(solution)/shard_map/all_to_all | solution.py:253
  32.2 0.9 copy.25
  33.1 21.9 %all-to-all-done = bf16[16,32,1024]{2,1,0:T(8,128)(2,1)S(1)} async-done(((bf16[16,32,1024]{2,1,0:T(8,128)(2,1)}), bf16[16,32,1024]{2,1,0:T(8,128)(2,1)S(1)}, u32[]{:S(2)}, u32[]{:S(2)}) %all-to-all-start) | async-done | bytes 1048608 | tf_op jit(solution)/shard_map/all_to_all | solution.py:253
  55.0 1.0 copy-done
  56.0 4.1 %heads.1 = (f32[2,256,128]{2,1,0:T(8,128)}, f32[2,256,128]{2,1,0:T(8,128)}, f32[2,16,256]{2,1,0:T(8,128)}, f32[2,16,256]{2,1,0:T(8,128)}, bf16[4,256,128]{2,1,0:T(8,128)(2,1)}, /*index=5*/bf16[512,256]{1,0:T(8,128)(2,1)}) custom-call(s32[1]{0:T(128)} %bitcast.5.p_ref, bf16[512,1024]{1,0:T(8,128)(2,1)} %bitcast.59, bf16[512,320]{1,0:T(8,128)(2,1)} %bitcast.64, ...), custom_call_target="tpu_custom_call" | custom-call | tf_op jit(solution)/shard_map/heads/pallas_call | solution.py:37
  60.8 1.1 collective-permute-done.2
  62.6 2.0 %collective-permute-start.3 = (f32[16,256]{1,0:T(8,128)S(1)}, f32[16,256]{1,0:T(8,128)S(1)}, u32[]{:S(2)}, u32[]{:S(2)}) collective-permute-start(f32[16,256]{1,0:T(8,128)S(1)} %slice_bitcast_fusion.2), channel_id=1, source_target_pairs={{0,2},{1,3},{2,0},{3,1},{4,6},{5,7},{6,4},{7,5},{8,10},{9,11},{10,... | collective-permute-start | bytes 49160 | tf_op jit(solution)/shard_map/ppermute | solution.py:210
  64.6 1.0 add.31
  66.3 4.8 %collective-permute-done.1 = f32[256,128]{1,0:T(8,128)S(1)} collective-permute-done((f32[256,128]{1,0:T(8,128)S(1)}, f32[256,128]{1,0:T(8,128)S(1)}, u32[]{:S(2)}, u32[]{:S(2)}) %collective-permute-start.1) | collective-permute-done | bytes 131104 | tf_op jit(solution)/shard_map/ppermute | solution.py:210
  71.1 3.7 %collective-permute-start.6 = (bf16[288,128]{1,0:T(8,128)(2,1)S(1)}, bf16[288,128]{1,0:T(8,128)(2,1)S(1)}, u32[]{:S(2)}, u32[]{:S(2)}) collective-permute-start(bf16[288,128]{1,0:T(8,128)(2,1)S(1)} %get-tuple-element.35), channel_id=1, source_target_pairs={{0,12},{1,13},{2,14},{3,15},{4,8},{5,9},{6,10},{7,11},{8,4},{9,5},... | collective-permute-start | bytes 221192 | tf_op jit(solution)/shard_map/ppermute | solution.py:210
  75.6 2.6 %collective-permute-done.6 = bf16[288,128]{1,0:T(8,128)(2,1)S(1)} collective-permute-done((bf16[288,128]{1,0:T(8,128)(2,1)S(1)}, bf16[288,128]{1,0:T(8,128)(2,1)S(1)}, u32[]{:S(2)}, u32[]{:S(2)}) %collective-permute-start.6) | collective-permute-done | bytes 73760 | tf_op jit(solution)/shard_map/ppermute | solution.py:210
  78.2 3.1 %collective-permute-done.5 = bf16[288,128]{1,0:T(8,128)(2,1)S(1)} collective-permute-done((bf16[288,128]{1,0:T(8,128)(2,1)S(1)}, bf16[288,128]{1,0:T(8,128)(2,1)S(1)}, u32[]{:S(2)}, u32[]{:S(2)}) %collective-permute-start.5) | collective-permute-done | bytes 73760 | tf_op jit(solution)/shard_map/ppermute | solution.py:210
  82.6 7.7 %collective-permute-done.7 = bf16[4,1,288,128]{3,2,0,1:T(8,128)(2,1)S(1)} collective-permute-done((bf16[4,1,288,128]{3,2,0,1:T(8,128)(2,1)S(1)}, bf16[4,1,288,128]{3,2,0,1:T(8,128)(2,1)S(1)}, u32[]{:S(2)}, u32[]{:S(2)}) %collective-permute-start.7) | collective-permute-done | bytes 294944 | tf_op jit(solution)/shard_map/ppermute | solution.py:210
  91.2 3.9 %all-to-all-start.3 = ((bf16[16,64,128]{2,1,0:T(8,128)(2,1)}), bf16[16,64,128]{2,1,0:T(8,128)(2,1)S(1)}, u32[]{:S(2)}, u32[]{:S(2)}) async-start(bf16[16,64,128]{2,1,0:T(8,128)(2,1)} %bitcast_bitcast_fusion), calls=%async_computation.3 | async-start | bytes 524288 | tf_op jit(solution)/shard_map/all_to_all | solution.py:236
  95.1 1.4 dynamic-slice_bitcast_fusion.gain_ref
  96.8 1.1 slice.30.qg_ref
  98.6 6.6 %all-to-all-done.3 = bf16[16,64,128]{2,1,0:T(8,128)(2,1)S(1)} async-done(((bf16[16,64,128]{2,1,0:T(8,128)(2,1)}), bf16[16,64,128]{2,1,0:T(8,128)(2,1)S(1)}, u32[]{:S(2)}, u32[]{:S(2)}) %all-to-all-start.3) | async-done | bytes 262176 | tf_op jit(solution)/shard_map/all_to_all | solution.py:236
  105.8 11.1 %attention.1 = (bf16[16,32,384]{2,1,0:T(8,128)(2,1)}, f32[128,256]{1,0:T(8,128)}) custom-call(s32[1]{0:T(128)} %bitcast.4.z_ref, bf16[16,256,128]{2,1,0:T(8,128)(2,1)} %slice.30.qg_ref, bf16[256,256]{1,0:T(8,128)(2,1)} %reshape.100.kv_ref, bf16[128,1024]{1,0:T(8,128)(2,1)} %wq_ref.1, bf16[128,256]{1,0:T(8,128)(2,1)} %wkv_ref.1, bf16[1024,128]{1,0:T(8,128)(2,1)} %bitcast.70, ...), custom_call_target="tpu_custom_call" | custom-call | tf_op jit(solution)/shard_map/attention/pallas_call | solution.py:37
  116.9 3.7 %all-to-all-start.4 = ((bf16[16,32,384]{2,1,0:T(8,128)(2,1)}), bf16[16,32,384]{2,1,0:T(8,128)(2,1)S(1)}, u32[]{:S(2)}, u32[]{:S(2)}) async-start(bf16[16,32,384]{2,1,0:T(8,128)(2,1)} %get-tuple-element.29), calls=%async_computation.4 | async-start | bytes 786432 | tf_op jit(solution)/shard_map/all_to_all | solution.py:322
  120.6 1.6 %collective-permute-start.9 = (f32[128,256]{1,0:T(8,128)}, f32[128,256]{1,0:T(8,128)S(1)}, u32[]{:S(2)}, u32[]{:S(2)}) collective-permute-start(f32[128,256]{1,0:T(8,128)} %get-tuple-element.32), channel_id=1, source_target_pairs={{0,16},{16,0},{1,17},{17,1},{2,18},{18,2},{3,19},{19,3},{4,20},{20... | collective-permute-start | bytes 393224 | tf_op jit(solution)/shard_map/ppermute | solution.py:324
  122.2 10.6 %all-to-all-done.4.got_ref = bf16[16,32,384]{2,1,0:T(8,128)(2,1)S(1)} async-done(((bf16[16,32,384]{2,1,0:T(8,128)(2,1)}), bf16[16,32,384]{2,1,0:T(8,128)(2,1)S(1)}, u32[]{:S(2)}, u32[]{:S(2)}) %all-to-all-start.4) | async-done | bytes 393248 | tf_op jit(solution)/shard_map/all_to_all | solution.py:322
  133.5 3.2 %finish.1 = (bf16[128,2048]{1,0:T(8,128)(2,1)}, bf16[128,2048]{1,0:T(8,128)(2,1)}, f32[1,2048]{1,0:T(1,128)}) custom-call(bf16[128,2048]{1,0:T(8,128)(2,1)} %bitcast.61, bf16[128,2048]{1,0:T(8,128)(2,1)} %bitcast.63, s32[1,128]{1,0:T(1,128)} %picks_ref.3, f32[1,2048]{1,0:T(1,128)} %bitcast.76, f32[128,1]{1,0:T(8,128)} %get-tuple-element.19.gate_ref, ...), custom_call_target="tpu_custom_call" | custom-call | tf_op jit(solution)/shard_map/finish/pallas_call | solution.py:37
  136.7 1.3 broadcast_in_dim.21
  138.0 3.3 %all-to-all-start.5 = ((f32[32,1,128]{2,1,0:T(1,128)}), f32[32,1,128]{2,1,0:T(1,128)S(1)}, u32[]{:S(2)}, u32[]{:S(2)}) async-start(f32[32,1,128]{2,1,0:T(1,128)} %bitcast.33), calls=%async_computation.5 | async-start | bytes 32768 | tf_op jit(solution)/shard_map/all_to_all | solution.py:345
  142.0 6.5 %all-to-all-done.5 = f32[32,1,128]{2,1,0:T(1,128)S(1)} async-done(((f32[32,1,128]{2,1,0:T(1,128)}), f32[32,1,128]{2,1,0:T(1,128)S(1)}, u32[]{:S(2)}, u32[]{:S(2)}) %all-to-all-start.5) | async-done | bytes 16416 | tf_op jit(solution)/shard_map/all_to_all | solution.py:345
  (50 shorter events, 10.0 us)
Async XLA Ops:
  0.6 6.4 %copy-start.6 = (bf16[128,256]{1,0:T(8,128)(2,1)S(1)}, bf16[128,256]{1,0:T(8,128)(2,1)}, u32[]{:S(2)}) copy-start(bf16[128,256]{1,0:T(8,128)(2,1)} %wkv_ref.1) | copy-start | bytes 196612
  0.6 6.5 %copy-start.4 = (bf16[128,1024]{1,0:T(8,128)(2,1)S(1)}, bf16[128,1024]{1,0:T(8,128)(2,1)}, u32[]{:S(2)}) copy-start(bf16[128,1024]{1,0:T(8,128)(2,1)} %wq_ref.1) | copy-start | bytes 786436
  2.7 10.3 %all-to-all-start.2 = ((bf16[4,64,512]{2,1,0:T(8,128)(2,1)}), bf16[4,64,512]{2,1,0:T(8,128)(2,1)S(1)}, u32[]{:S(2)}, u32[]{:S(2)}) async-start(bf16[4,64,512]{2,1,0:T(8,128)(2,1)} %reshape.96), calls=%async_computation.2 | async-start | bytes 524288 | tf_op jit(solution)/shard_map/all_to_all | solution.py:234
  13.0 15.5 %copy-start.2 = (bf16[4,64,512]{2,1,0:T(8,128)(2,1)}, bf16[4,64,512]{2,1,0:T(8,128)(2,1)S(1)}, u32[]{:S(2)}) copy-start(bf16[4,64,512]{2,1,0:T(8,128)(2,1)S(1)} %all-to-all-done.2) | copy-start | bytes 786436
  13.0 15.5 %all-to-all-start.1 = ((bf16[4,128,320]{1,2,0:T(8,128)(2,1)}), bf16[4,128,320]{1,2,0:T(8,128)(2,1)S(1)}, u32[]{:S(2)}, u32[]{:S(2)}) async-start(bf16[4,128,320]{1,2,0:T(8,128)(2,1)} %maximum_bitcast_fusion), calls=%async_computation.1 | async-start | bytes 655360 | tf_op jit(solution)/shard_map/all_to_all | solution.py:232
  28.5 26.5 %all-to-all-start = ((bf16[16,32,1024]{2,1,0:T(8,128)(2,1)}), bf16[16,32,1024]{2,1,0:T(8,128)(2,1)S(1)}, u32[]{:S(2)}, u32[]{:S(2)}) async-start(bf16[16,32,1024]{2,1,0:T(8,128)(2,1)} %get-tuple-element.22), calls=%async_computation | async-start | bytes 2097152 | tf_op jit(solution)/shard_map/all_to_all | solution.py:253
  55.0 1.0 copy-start
  60.1 1.8 %collective-permute-start.2 = (f32[2,16,256]{2,1,0:T(8,128)}, f32[2,16,256]{2,1,0:T(8,128)S(1)}, u32[]{:S(2)}, u32[]{:S(2)}) collective-permute-start(f32[2,16,256]{2,1,0:T(8,128)} %get-tuple-element.26), channel_id=1, source_target_pairs={{0,1},{1,0},{2,3},{3,2},{4,5},{5,4},{6,7},{7,6},{8,9},{9,8},{10,11... | collective-permute-start | bytes 98312 | tf_op jit(solution)/shard_map/ppermute | solution.py:210
  60.7 3.8 %collective-permute-start = (f32[2,256,128]{2,1,0:T(8,128)}, f32[2,256,128]{2,1,0:T(8,128)S(1)}, u32[]{:S(2)}, u32[]{:S(2)}) collective-permute-start(f32[2,256,128]{2,1,0:T(8,128)} %get-tuple-element.24), channel_id=1, source_target_pairs={{0,1},{1,0},{2,3},{3,2},{4,5},{5,4},{6,7},{7,6},{8,9},{9,8},{10,11... | collective-permute-start | bytes 786440 | tf_op jit(solution)/shard_map/ppermute | solution.py:210
  62.6 3.7 %collective-permute-start.3 = (f32[16,256]{1,0:T(8,128)S(1)}, f32[16,256]{1,0:T(8,128)S(1)}, u32[]{:S(2)}, u32[]{:S(2)}) collective-permute-start(f32[16,256]{1,0:T(8,128)S(1)} %slice_bitcast_fusion.2), channel_id=1, source_target_pairs={{0,2},{1,3},{2,0},{3,1},{4,6},{5,7},{6,4},{7,5},{8,10},{9,11},{10,... | collective-permute-start | bytes 49160 | tf_op jit(solution)/shard_map/ppermute | solution.py:210
  65.6 5.5 %collective-permute-start.1 = (f32[256,128]{1,0:T(8,128)S(1)}, f32[256,128]{1,0:T(8,128)S(1)}, u32[]{:S(2)}, u32[]{:S(2)}) collective-permute-start(f32[256,128]{1,0:T(8,128)S(1)} %slice_bitcast_fusion), channel_id=1, source_target_pairs={{0,2},{1,3},{2,0},{3,1},{4,6},{5,7},{6,4},{7,5},{8,10},{9,11},{10,... | collective-permute-start | bytes 393224 | tf_op jit(solution)/shard_map/ppermute | solution.py:210
  71.1 7.1 %collective-permute-start.6 = (bf16[288,128]{1,0:T(8,128)(2,1)S(1)}, bf16[288,128]{1,0:T(8,128)(2,1)S(1)}, u32[]{:S(2)}, u32[]{:S(2)}) collective-permute-start(bf16[288,128]{1,0:T(8,128)(2,1)S(1)} %get-tuple-element.35), channel_id=1, source_target_pairs={{0,12},{1,13},{2,14},{3,15},{4,8},{5,9},{6,10},{7,11},{8,4},{9,5},... | collective-permute-start | bytes 221192 | tf_op jit(solution)/shard_map/ppermute | solution.py:210
  74.9 6.4 %collective-permute-start.5 = (bf16[288,128]{1,0:T(8,128)(2,1)S(1)}, bf16[288,128]{1,0:T(8,128)(2,1)S(1)}, u32[]{:S(2)}, u32[]{:S(2)}) collective-permute-start(bf16[288,128]{1,0:T(8,128)(2,1)S(1)} %get-tuple-element.35), channel_id=1, source_target_pairs={{0,8},{1,9},{2,10},{3,11},{4,12},{5,13},{6,14},{7,15},{8,0},{9,1},... | collective-permute-start | bytes 221192 | tf_op jit(solution)/shard_map/ppermute | solution.py:210
  75.5 5.8 %collective-permute-start.4 = (bf16[288,128]{1,0:T(8,128)(2,1)S(1)}, bf16[288,128]{1,0:T(8,128)(2,1)S(1)}, u32[]{:S(2)}, u32[]{:S(2)}) collective-permute-start(bf16[288,128]{1,0:T(8,128)(2,1)S(1)} %get-tuple-element.35), channel_id=1, source_target_pairs={{0,4},{1,5},{2,6},{3,7},{4,0},{5,1},{6,2},{7,3},{8,12},{9,13},{10,... | collective-permute-start | bytes 221192 | tf_op jit(solution)/shard_map/ppermute | solution.py:210
  81.3 9.2 %copy-start.3 = (bf16[64,2048]{1,0:T(8,128)(2,1)S(1)}, bf16[64,2048]{1,0:T(8,128)(2,1)}, u32[]{:S(2)}) copy-start(bf16[64,2048]{1,0:T(8,128)(2,1)} %param.15) | copy-start | bytes 786436
  82.0 8.3 %collective-permute-start.7 = (bf16[4,1,288,128]{3,2,0,1:T(8,128)(2,1)S(1)}, bf16[4,1,288,128]{3,2,0,1:T(8,128)(2,1)S(1)}, u32[]{:S(2)}, u32[]{:S(2)}) collective-permute-start(bf16[4,1,288,128]{3,2,0,1:T(8,128)(2,1)S(1)} %bitcast.65), channel_id=1, source_target_pairs={{0,2},{1,3},{2,0},{3,1},{4,6},{5,7},{6,4},{7,5},{8,10},{9,11},{10,... | collective-permute-start | bytes 884744 | tf_op jit(solution)/shard_map/ppermute | solution.py:210
  90.4 6.1 %collective-permute-start.8 = (bf16[4,2,288,128]{3,2,0,1:T(8,128)(2,1)S(1)}, bf16[4,2,288,128]{3,2,0,1:T(8,128)(2,1)S(1)}, u32[]{:S(2)}, u32[]{:S(2)}) collective-permute-start(bf16[4,2,288,128]{3,2,0,1:T(8,128)(2,1)S(1)} %maximum_select_fusion.1), channel_id=1, source_target_pairs={{0,1},{1,0},{2,3},{3,2},{4,5},{5,4},{6,7},{7,6},{8,9},{9,8},{10,11... | collective-permute-start | bytes 1769480 | tf_op jit(solution)/shard_map/ppermute | solution.py:210
  91.2 13.9 %all-to-all-start.3 = ((bf16[16,64,128]{2,1,0:T(8,128)(2,1)}), bf16[16,64,128]{2,1,0:T(8,128)(2,1)S(1)}, u32[]{:S(2)}, u32[]{:S(2)}) async-start(bf16[16,64,128]{2,1,0:T(8,128)(2,1)} %bitcast_bitcast_fusion), calls=%async_computation.3 | async-start | bytes 524288 | tf_op jit(solution)/shard_map/all_to_all | solution.py:236
  105.1 0.7 copy-start.5
  116.9 24.3 %copy-start.7 = (f32[128,256]{1,0:T(8,128)S(1)}, f32[128,256]{1,0:T(8,128)}, u32[]{:S(2)}) copy-start(f32[128,256]{1,0:T(8,128)} %get-tuple-element.32) | copy-start | bytes 393220
  116.9 15.8 %all-to-all-start.4 = ((bf16[16,32,384]{2,1,0:T(8,128)(2,1)}), bf16[16,32,384]{2,1,0:T(8,128)(2,1)S(1)}, u32[]{:S(2)}, u32[]{:S(2)}) async-start(bf16[16,32,384]{2,1,0:T(8,128)(2,1)} %get-tuple-element.29), calls=%async_computation.4 | async-start | bytes 786432 | tf_op jit(solution)/shard_map/all_to_all | solution.py:322
  120.6 20.6 %collective-permute-start.9 = (f32[128,256]{1,0:T(8,128)}, f32[128,256]{1,0:T(8,128)S(1)}, u32[]{:S(2)}, u32[]{:S(2)}) collective-permute-start(f32[128,256]{1,0:T(8,128)} %get-tuple-element.32), channel_id=1, source_target_pairs={{0,16},{16,0},{1,17},{17,1},{2,18},{18,2},{3,19},{19,3},{4,20},{20... | collective-permute-start | bytes 393224 | tf_op jit(solution)/shard_map/ppermute | solution.py:324
  132.8 0.8 copy-start.1
  138.0 10.4 %all-to-all-start.5 = ((f32[32,1,128]{2,1,0:T(1,128)}), f32[32,1,128]{2,1,0:T(1,128)S(1)}, u32[]{:S(2)}, u32[]{:S(2)}) async-start(f32[32,1,128]{2,1,0:T(1,128)} %bitcast.33), calls=%async_computation.5 | async-start | bytes 32768 | tf_op jit(solution)/shard_map/all_to_all | solution.py:345

commit v2 on v1

v2 whole, which is shorter than its diff:
```python
import functools

import jax
import jax.numpy as jnp
from jax import lax
from jax.experimental import pallas as pl
from jax.experimental.pallas import tpu as pltpu
from jax.sharding import Mesh, PartitionSpec as P


MODEL_WIDTH = 2048
QUERY_HEADS = 16
KEY_VALUE_HEADS = 2
HEAD_SIZE = 64
GROUP = QUERY_HEADS // KEY_VALUE_HEADS
KV_WIDTH = 2 * KEY_VALUE_HEADS * HEAD_SIZE
Q_WIDTH = QUERY_HEADS * HEAD_SIZE
EPSILON = 1e-05
EMPTY = 2.0**100
PLANE = 4
LINES = ("zz", "yy")
SEQ = LINES + ("cc",)

F32 = jnp.float32
BF16 = jnp.bfloat16


def dot(a, b, ca=1, cb=0):
    return lax.dot_general(a, b, (((ca,), (cb,)), ((), ())), preferred_element_type=F32)


def iota(shape, dim):
    return lax.broadcasted_iota(jnp.int32, shape, dim)


def call(body, out_shape, *args, scalars=(), scratch=()):
    vmem = pl.BlockSpec(memory_space=pltpu.VMEM)
    smem = pl.BlockSpec(memory_space=pltpu.SMEM)
    return pl.pallas_call(
        body,
        out_shape=out_shape,
        in_specs=[smem] * len(scalars) + [vmem] * len(args),
        out_specs=jax.tree.map(lambda _: vmem, out_shape),
        scratch_shapes=list(scratch),
    )(*scalars, *args)


def shaped(shape, dtype):
    return jax.ShapeDtypeStruct(shape, dtype)


def selection(picks, slots):
    tokens = picks.shape[1]
    picked = jnp.broadcast_to(picks.astype(F32), (8, tokens)).astype(BF16)
    before = (iota((tokens, tokens), 0) < iota((tokens, tokens), 1)).astype(F32).astype(BF16)
    rank = dot(picked, before)[:1].astype(jnp.int32)
    hit = (iota((slots, tokens), 0) == rank) & (picks > 0)
    return hit.astype(F32).astype(BF16)


def pick_kernel(h_ref, c_ref, picks_ref, gain_ref, router_ref, send_ref, x_ref, cot_ref, inv_ref, gate_ref):
    lines, slots, width = send_ref.shape[0] // 2, send_ref.shape[1], send_ref.shape[2] // 2
    picks = picks_ref[...]
    sel = selection(picks, slots)
    x = dot(sel, h_ref[...])
    cot = dot(sel, c_ref[...])
    gate = 1.0 / (1.0 + jnp.exp(-jnp.sum(x * router_ref[...], axis=1, keepdims=True)))
    inv = lax.rsqrt(jnp.mean(x * x, axis=1, keepdims=True) + EPSILON)
    x_ref[...] = x.astype(BF16)
    cot_ref[...] = cot.astype(BF16)
    inv_ref[...] = inv
    gate_ref[...] = gate
    grads = (gate * cot).astype(BF16)
    normed = x * inv * gain_ref[...]
    normed = jnp.where(iota((slots, 1), 0) < jnp.sum(picks), normed, EMPTY).astype(BF16)
    for z in range(lines):
        cols = slice(z * width, (z + 1) * width)
        part = jnp.concatenate([normed[:, cols], grads[:, cols]], axis=1)
        send_ref[2 * z] = part
        send_ref[2 * z + 1] = part


def put(refs, at, value):
    if len(refs) == 1:
        refs[0][at] = value
        return
    for k, ref in enumerate(refs):

        @pl.when(at == k)
        def _(ref=ref):
            ref[...] = value


def weights_kernel(at_ref, wq_ref, wkv_ref, wo_ref, *outs, lines, cpd, kpd):
    z, p = at_ref[0], at_ref[1]
    to_plane, to_lines = outs[:PLANE], outs[PLANE:]
    width = wo_ref.shape[1] // lines
    for r in range(PLANE):
        places = [PLANE * k + r for k in range(lines)]
        columns = [wq_ref[:, i * cpd : (i + 1) * cpd] for i in places]
        columns += [wkv_ref[:, i * kpd : (i + 1) * kpd] for i in places]
        put(to_plane, p ^ r, jnp.concatenate(columns, axis=1))
    for k in range(lines):
        put(to_lines, z ^ k, wo_ref[:, k * width : (k + 1) * width])


def arrange_kernel(at_ref, *refs):
    z, p = at_ref[0], at_ref[1]
    wqkv_ref, wout_ref, cols_ref = refs[-3:]
    lines, _, width = wout_ref.shape
    fb = width // PLANE
    for r in range(PLANE):
        wqkv_ref[p ^ r] = refs[r][...]
    for k in range(lines):
        rows = refs[PLANE + k][...]
        wout_ref[z ^ k] = rows
        for r in range(PLANE):
            cols_ref[p ^ r, z ^ k] = rows[:, r * fb : (r + 1) * fb]


def columns_kernel(at_ref, *refs):
    out_ref = refs[-1]
    for r in range(PLANE):
        for k in range(refs[r].shape[0]):
            out_ref[PLANE * k + (at_ref[1] ^ r)] = refs[r][k]


def load_both(core, mine_ref, other_ref, all_ref):
    for i in range(mine_ref.shape[0]):
        all_ref[2 * i + core] = mine_ref[i]
        all_ref[2 * i + 1 - core] = other_ref[i]


def heads_kernel(at_ref, mine_ref, other_ref, wqkv_ref, wout_ref, *refs, rows, cpd, kpd, packed):
    core = at_ref[3]
    outs, got_ref = refs[:-1], refs[-1]
    part_ref, normed_ref, place_ref = outs[:3]
    lines = part_ref.shape[0]
    load_both(core, mine_ref, other_ref, got_ref)
    n, per, width = got_ref.shape
    slots = n * per
    half = width // 2
    fb = half // PLANE
    got = got_ref[...].reshape(slots, width)
    valid = got[:, :1].astype(F32) < EMPTY / 2
    ones = jnp.broadcast_to(jnp.where(valid, 1.0, 0.0), (slots, 128)).astype(BF16)
    earlier = (iota((slots, slots), 1) < iota((slots, slots), 0)).astype(F32).astype(BF16)
    rank = dot(earlier, ones)[:, :1].astype(jnp.int32)
    rank = jnp.where(valid, rank, -1)
    place = (rank == iota((slots, rows), 1)).astype(F32).astype(BF16)
    place_ref[...] = place
    compact = dot(place, got, 0, 0).astype(BF16)
    grads = compact[:, half:]
    for r in range(PLANE):
        normed_ref[r] = compact[:, r * fb : (r + 1) * fb]
    wqkv = wqkv_ref[...].reshape(half, lines * (cpd + kpd))
    query = dot(compact[:, :half], wqkv[:, : lines * cpd])
    kv = dot(wqkv[:, lines * cpd :], compact[:, :half], 0, 1)
    grad_heads = dot(grads, wout_ref[...].reshape(lines * cpd, half), 1, 1)
    top = rows // 2
    beside = lambda m: jnp.concatenate([m[:top], m[top:]], axis=1)
    for k in range(lines):
        q_part = query[:, k * cpd : (k + 1) * cpd]
        kv_part = kv[k * kpd : (k + 1) * kpd]
        g_part = grad_heads[:, k * cpd : (k + 1) * cpd]
        if packed:
            part_ref[k, :top] = beside(q_part)
            part_ref[k, top : top + kpd] = kv_part[:, :top]
            part_ref[k, top + kpd : top + 2 * kpd] = kv_part[:, top:]
            part_ref[k, top + 2 * kpd :] = beside(g_part)
        else:
            part_ref[k, :, :cpd] = q_part
            outs[3][k] = kv_part
            part_ref[k, :, cpd:] = g_part


def sum_kernel(part_ref, q_ref, g_ref):
    total = (part_ref[0] + part_ref[1] + (part_ref[2] + part_ref[3])).astype(BF16)
    lead = q_ref.shape[1]
    for i in range(q_ref.shape[0]):
        q_ref[i] = total[:lead]
        g_ref[i] = total[lead:]


def load_kv(q_all, kv_ref, kpd, top):
    n = q_all.shape[0]
    for i in range(n):
        kv_ref[i * kpd : (i + 1) * kpd, :top] = q_all[i, top : top + kpd]
        kv_ref[i * kpd : (i + 1) * kpd, top:] = q_all[i, top + kpd : top + 2 * kpd]


def probabilities(q, kt):
    top = q.shape[0]
    scale = HEAD_SIZE**-0.5

    def soft(scores, start):
        allowed = iota(scores.shape, 1) <= iota(scores.shape, 0) + start
        scores = jnp.where(allowed, scores * scale, -jnp.inf)
        e = jnp.exp(scores - jnp.max(scores, axis=1, keepdims=True))
        return e / jnp.sum(e, axis=1, keepdims=True)

    zero = jnp.zeros_like(kt)
    low = soft(dot(q, jnp.concatenate([kt[:, :top], zero[:, :top]], axis=0)), 0)
    return low, soft(dot(q, jnp.concatenate([zero, kt], axis=0)), top)


def forward_kernel(at_ref, *refs, packed, kpd):
    sources, (cols_ref, place_ref, send_ref, kv_out_ref) = refs[:2], refs[2:6]
    probs_refs = refs[6:-2]
    q_all, mixed_ref = refs[-2:]
    heads, top = q_all.shape[0], mixed_ref.shape[0] // 2
    if packed:
        load_both(at_ref[3], *sources, q_all)
        load_kv(q_all, kv_out_ref, kpd, top)
    else:
        q_all[...] = sources[0][...]
        kv_out_ref[...] = sources[1][...]

    def one_head(head, group):
        kt = kv_out_ref[pl.ds(group * HEAD_SIZE, HEAD_SIZE), :]
        vt = kv_out_ref[pl.ds((KEY_VALUE_HEADS + group) * HEAD_SIZE, HEAD_SIZE), :]
        low, high = probabilities(q_all[head, :top], kt)
        for ref, value in zip(probs_refs, (low, high)):
            ref[head] = value
        return dot(low.astype(BF16), vt[:, :top], 1, 1), dot(high.astype(BF16), vt, 1, 1)

    def pair(j):
        group = j // (GROUP // 2)
        low0, high0 = one_head(2 * j, group)
        low1, high1 = one_head(2 * j + 1, group)
        lanes = pl.ds(j * 2 * HEAD_SIZE, 2 * HEAD_SIZE)
        mixed_ref[:top, lanes] = jnp.concatenate([low0, low1], axis=1).astype(BF16)
        mixed_ref[top:, lanes] = jnp.concatenate([high0, high1], axis=1).astype(BF16)

    if packed:
        for j in range(heads // 2):
            pair(j)
    else:
        pl.loop(0, heads // 2)(pair)
    n, slots, _ = send_ref.shape
    out = dot(mixed_ref[...], cols_ref[...].reshape(Q_WIDTH, cols_ref.shape[2])).astype(BF16)
    spread = dot(place_ref[...], out).astype(BF16)
    for d in range(n):
        send_ref[d] = spread[d * slots : (d + 1) * slots]


def backward_kernel(at_ref, *refs, packed, kpd):
    count = 4 if packed else 2
    sources = refs[:count]
    kv_ref, wq_ref, wkv_ref, gain_ref, normed_ref, place_ref = refs[count : count + 6]
    probs_refs = refs[count + 6 : -6]
    up_ref, kvg_ref = refs[-6:-4]
    q_all, g_all, gq_ref, gkv_ref = refs[-4:]
    heads, top = q_all.shape[0], gq_ref.shape[0] // 2
    for source, all_ref in ((sources[: count // 2], q_all), (sources[count // 2 :], g_all)):
        if packed:
            load_both(at_ref[3], *source, all_ref)
        else:
            all_ref[...] = source[0][...]
    scale = HEAD_SIZE**-0.5
    gkv_ref[...] = jnp.zeros(gkv_ref.shape, F32)

    def one_head(head, group):
        keys = pl.ds(group * HEAD_SIZE, HEAD_SIZE)
        values = pl.ds((KEY_VALUE_HEADS + group) * HEAD_SIZE, HEAD_SIZE)
        kt, vt = kv_ref[keys, :], kv_ref[values, :]
        q, g = q_all[head, :top], g_all[head]
        zero = jnp.zeros_like(vt)

        def back(probs, gp):
            inner = jnp.sum(probs * gp, axis=1, keepdims=True)
            return (probs * (gp - inner)).astype(BF16)

        low, high = [ref[head] for ref in probs_refs] or probabilities(q, kt)
        gs_low = back(low, dot(g, jnp.concatenate([vt[:, :top], zero[:, :top]], axis=0)))
        gs_high = back(high, dot(g, jnp.concatenate([zero, vt], axis=0)))
        gkv_ref[keys, :] += dot(q, gs_high, 0, 0)[HEAD_SIZE:] * scale
        gkv_ref[keys, :top] += dot(q, gs_low, 0, 0)[:HEAD_SIZE] * scale
        gkv_ref[values, :] += dot(g, high.astype(BF16), 0, 0)[HEAD_SIZE:]
        gkv_ref[values, :top] += dot(g, low.astype(BF16), 0, 0)[:HEAD_SIZE]
        return dot(gs_low, kt[:, :top], 1, 1) * scale, dot(gs_high, kt, 1, 1) * scale

    def pair(j):
        group = j // (GROUP // 2)
        low0, high0 = one_head(2 * j, group)
        low1, high1 = one_head(2 * j + 1, group)
        lanes = pl.ds(j * 2 * HEAD_SIZE, 2 * HEAD_SIZE)
        gq_ref[:top, lanes] = jnp.concatenate([low0, low1], axis=1).astype(BF16)
        gq_ref[top:, lanes] = jnp.concatenate([high0, high1], axis=1).astype(BF16)

    if packed:
        for j in range(heads // 2):
            pair(j)
    else:
        pl.loop(0, heads // 2)(pair)
    n, slots, _ = up_ref.shape
    gkv = gkv_ref[...].astype(BF16)
    up = (dot(gq_ref[...], wq_ref[...], 1, 1) + dot(gkv, wkv_ref[...], 0, 1)) * gain_ref[at_ref[2]]
    kvg_ref[...] = dot(normed_ref[at_ref[1]], gkv, 0, 1)
    spread = dot(place_ref[...], up.astype(BF16)).astype(BF16)
    for d in range(n):
        up_ref[d] = spread[d * slots : (d + 1) * slots]


def mix_kernel(x_ref, cot_ref, gate_ref, got_ref, up_ref, send_ref, mixed_ref, logit_ref):
    n, slots, fb = up_ref.shape
    out = jnp.concatenate([got_ref[d] for d in range(n)], axis=1).astype(F32)
    x, gate = x_ref[...].astype(F32), gate_ref[...]
    mixed_ref[...] = (x + gate * out).astype(BF16)
    through = jnp.sum(cot_ref[...].astype(F32) * out, axis=1, keepdims=True)
    grad_logit = through * gate * (1.0 - gate)
    logit_ref[...] = grad_logit
    part = jnp.sum(grad_logit * x, axis=0, keepdims=True)
    row = iota((send_ref.shape[1] - slots, 1), 0)
    high = part.astype(BF16).astype(F32)
    middle = (part - high).astype(BF16).astype(F32)
    low = part - high - middle
    rows = jnp.where(row == 0, high, jnp.where(row == 1, middle, jnp.where(row == 2, low, 0.0))).astype(BF16)
    for d in range(n):
        send_ref[d, :slots] = up_ref[d]
        send_ref[d, slots:] = rows[:, d * fb : (d + 1) * fb]


def place_rows(picks, rows, tokens):
    sel = selection(picks, rows.shape[0])
    taken = dot(sel, jnp.ones((rows.shape[0], 128), BF16), 0, 0)[:, :1] > 0.5
    return jnp.where(taken, dot(sel, rows, 0, 0), tokens.astype(F32)).astype(BF16)


def tokens_kernel(h_ref, picks_ref, mixed_ref, out_ref):
    out_ref[...] = place_rows(picks_ref[...], mixed_ref[...], h_ref[...])


def add_kernel(a_ref, b_ref, out_ref):
    out_ref[...] = a_ref[...] + b_ref[...]


def finish_kernel(c_ref, picks_ref, router_ref, logit_ref, x_ref, cot_ref, inv_ref, got_ref, grad_ref):
    n = got_ref.shape[0]
    slots = x_ref.shape[0]
    up = jnp.concatenate([got_ref[d, :slots] for d in range(n)], axis=1).astype(F32)
    x, inv = x_ref[...].astype(F32), inv_ref[...]
    grad_block = inv * up - x * inv**3 * jnp.mean(up * x, axis=1, keepdims=True)
    grad_block = grad_block.astype(BF16).astype(F32)
    rows = (cot_ref[...].astype(F32) + logit_ref[...] * router_ref[...] + grad_block).astype(BF16)
    grad_ref[...] = place_rows(picks_ref[...], rows, c_ref[...])


def exchange(x, axes):
    return lax.all_to_all(x, axes, 0, 0, tiled=True)


def swap(x, n, bit):
    return lax.ppermute(x, SEQ, [(i, i ^ bit) for i in range(n)])


def block(hidden, cotangent, picks, gain, router, w_query, w_kv, w_out):
    lines = lax.axis_size("zz")
    n = lines * PLANE
    dp = lax.axis_size("dp")
    z, core = lax.axis_index("zz"), lax.axis_index("cc")
    p = 2 * lax.axis_index("yy") + core
    me = PLANE * z + p
    where = jnp.stack([z, p, me, core]).astype(jnp.int32)
    hidden, cotangent = hidden[0], cotangent[0]
    tokens = hidden.shape[0]
    slots = tokens // 4
    rows = n * (tokens // 8)
    top = rows // 2
    fb = MODEL_WIDTH // n
    cpd = Q_WIDTH // n
    kpd = KV_WIDTH // n
    packed = cpd == HEAD_SIZE
    as_row = lambda v: v.reshape(1, -1)

    lines_apart = lines <= 4
    to_plane = [shaped((fb, lines * (cpd + kpd)), BF16)] * PLANE
    to_lines = [shaped((cpd, PLANE * fb), BF16)] * lines if lines_apart else [shaped((lines, cpd, PLANE * fb), BF16)]
    out = call(
        functools.partial(weights_kernel, lines=lines, cpd=cpd, kpd=kpd),
        tuple(to_plane + to_lines),
        w_query,
        w_kv,
        w_out,
        scalars=(where,),
    )
    to_plane, to_lines = out[:PLANE], out[PLANE:]
    if not lines_apart:
        to_lines = [to_lines[0][k] for k in range(lines)]
    wqkv = [to_plane[0]] + [swap(to_plane[r], n, r) for r in range(1, PLANE)]
    wout = [to_lines[0]] + [swap(to_lines[k], n, PLANE * k) for k in range(1, lines)]
    wqkv, wout, cols = call(
        arrange_kernel,
        (
            shaped((PLANE, fb, lines * (cpd + kpd)), BF16),
            shaped((lines, cpd, PLANE * fb), BF16),
            shaped((PLANE, lines, cpd, fb), BF16),
        ),
        *wqkv,
        *wout,
        scalars=(where,),
    )

    send, x, cot, inv, gate = call(
        pick_kernel,
        (
            shaped((2 * lines, slots, 2 * PLANE * fb), BF16),
            shaped((slots, MODEL_WIDTH), BF16),
            shaped((slots, MODEL_WIDTH), BF16),
            shaped((slots, 1), F32),
            shaped((slots, 1), F32),
        ),
        hidden,
        cotangent,
        picks,
        as_row(gain),
        as_row(router),
    )
    mine = exchange(send, LINES)
    other = swap(mine, n, 1)

    part = (lines, top + 2 * kpd + top, 2 * cpd) if packed else (lines, rows, 2 * cpd)
    outs = [
        shaped(part, F32),
        shaped((PLANE, rows, fb), BF16),
        shaped((n * slots, rows), BF16),
    ]
    if not packed:
        outs += [shaped((lines, kpd, rows), F32)]
    part, normed, place, *kv_part = call(
        functools.partial(heads_kernel, rows=rows, cpd=cpd, kpd=kpd, packed=packed),
        tuple(outs),
        mine,
        other,
        wqkv,
        wout,
        scalars=(where,),
        scratch=(pltpu.VMEM((n, slots, 2 * PLANE * fb), BF16),),
    )
    cols = [cols[0]] + [swap(cols[r], n, r) for r in range(1, PLANE)]
    cols = call(columns_kernel, shaped((n, cpd, fb), BF16), *cols, scalars=(where,))
    part = exchange(part, "zz")
    if packed:
        lead = top + 2 * kpd
        q_pack, g_pack = call(
            sum_kernel, (shaped((2 * lines, lead, 2 * cpd), BF16), shaped((2 * lines, top, 2 * cpd), BF16)), part
        )
        q_refs = exchange(q_pack, LINES)
        q_refs = (q_refs, swap(q_refs, n, 1))
        g_refs = exchange(g_pack, LINES)
        g_refs = (g_refs, swap(g_refs, n, 1))
        kv_refs = ()
    else:
        per = HEAD_SIZE // cpd
        everything = jnp.sum(part, axis=0).astype(BF16)
        everything = lax.all_gather(everything, SEQ, axis=0).reshape(QUERY_HEADS, per, 2, top, 2, cpd)
        everything = everything.transpose(4, 0, 3, 2, 1, 5).reshape(2, QUERY_HEADS, top, 2 * HEAD_SIZE)
        q_refs, g_refs = (everything[0],), (everything[1],)
        kv_part = jnp.sum(lax.all_to_all(kv_part[0], "zz", 0, 0, tiled=True), axis=0).astype(BF16)
        kv_refs = (lax.all_gather(kv_part, SEQ, axis=0, tiled=True),)
    q_scratch = pltpu.VMEM((QUERY_HEADS, top + (2 * kpd if packed else 0), 2 * HEAD_SIZE), BF16)

    probs = (shaped((QUERY_HEADS, top, top), F32), shaped((QUERY_HEADS, top, rows), F32)) if packed else ()
    send, kv_all, *probs = call(
        functools.partial(forward_kernel, packed=packed, kpd=kpd),
        (
            shaped((n, slots, fb), BF16),
            shaped((KV_WIDTH, rows), BF16),
            *probs,
        ),
        *q_refs,
        *kv_refs,
        cols,
        place,
        scalars=(where,),
        scratch=(q_scratch, pltpu.VMEM((rows, Q_WIDTH), BF16)),
    )
    got = exchange(send, SEQ)
    up, kv_part = call(
        functools.partial(backward_kernel, packed=packed, kpd=kpd),
        (shaped((n, slots, fb), BF16), shaped((fb, KV_WIDTH), F32)),
        *q_refs,
        *g_refs,
        kv_all,
        w_query,
        w_kv,
        gain.reshape(n, 1, fb),
        normed,
        place,
        *probs,
        scalars=(where,),
        scratch=(
            q_scratch,
            pltpu.VMEM((QUERY_HEADS, top, 2 * HEAD_SIZE), BF16),
            pltpu.VMEM((rows, Q_WIDTH), BF16),
            pltpu.VMEM((KV_WIDTH, rows), F32),
        ),
    )
    send, mixed_rows, grad_logit = call(
        mix_kernel,
        (
            shaped((n, slots + 16, fb), BF16),
            shaped((slots, MODEL_WIDTH), BF16),
            shaped((slots, 1), F32),
        ),
        x,
        cot,
        gate,
        got,
        up,
    )
    got = exchange(send, SEQ)
    mixed = call(tokens_kernel, shaped((tokens, MODEL_WIDTH), BF16), hidden, picks, mixed_rows)

    def add_over_dp(v):
        if dp != 2:
            return lax.psum(v, "dp")
        other = lax.ppermute(v, "dp", [(0, 1), (1, 0)])
        return call(add_kernel, shaped(v.shape, F32), v, other)

    kv_grad = add_over_dp(kv_part)
    router_grad = jnp.sum(got[:, slots : slots + 3].astype(F32), axis=(0, 1)).reshape(1, fb)
    router_grad = add_over_dp(router_grad).reshape(fb)
    input_grad = call(
        finish_kernel,
        shaped((tokens, MODEL_WIDTH), BF16),
        cotangent,
        picks,
        as_row(router),
        grad_logit,
        x,
        cot,
        inv,
        got,
    )
    return mixed[None], input_grad[None], kv_grad, router_grad


def solution(mesh):
    dp, n = mesh.shape["dp"], mesh.shape["seq"]
    split = Mesh(mesh.devices.reshape(dp, n // PLANE, PLANE // 2, 2), ("dp",) + SEQ)
    rows = P("dp", SEQ, None)
    return jax.shard_map(
        block,
        mesh=split,
        in_specs=(rows, rows, P("dp", SEQ), P(), P(), P(SEQ, None), P(SEQ, None), P(SEQ, None)),
        out_specs=(rows, rows, P(SEQ, None), P(SEQ)),
        check_vma=False,
    )
```

time: 150 us -> 146 us (0.973)
  waiting for transfers between devices: 77.7 us -> 21.3 us
  blocking collectives: 0 us -> 53.9 us
  Pallas kernels: 21.1 us -> 37.4 us
  starting transfers between devices: 33.6 us -> 24.7 us
  local copies, waits for them, and re-layouts: 11.7 us -> 6.1 us
  other arithmetic: 4.1 us -> 0.79 us
    all_to_all x0 -> x3, blocking collectives: none -> 53.9 us  [exchange(): return lax.all_to_all(x, axes, 0, 0, tiled=True)]
    all_to_all x6 -> x3, waiting for transfers between devices: 57.8 us -> 12.8 us  [exchange(): return lax.all_to_all(x, axes, 0, 0, tiled=True)]
    pallas_call x4 -> x13, Pallas kernels: 21.1 us -> 37.4 us  [call(): pl.pallas_call(body, out_shape=out_shape, in_specs=[smem] * len(scalars)...]
    ppermute x9 -> x12, waiting for transfers between devices: 19.9 us -> 8.52 us  [swap(): return lax.ppermute(x, SEQ, [(i, i ^ bit) for i in range(n)])]
    all_to_all x6 -> x3, starting transfers between devices: 24.2 us -> 13.9 us  [exchange(): return lax.all_to_all(x, axes, 0, 0, tiled=True)]
    reshape x5 -> x0, local copies, waits for them, and re-layouts: 4.03 us -> none  [the longest x2 1.96 us: local(): w_out.reshape(cpd, lines, PLANE, fb).transpose(2, 0, 1, 3)]
    unnamed x18 -> x42, local copies, waits for them, and re-layouts: 2.74 us -> 5.45 us
    add x3 -> x0, other arithmetic: 2.43 us -> none  [the longest x1 0.99 us: local(): keep = keep + swap(away, n, 1)]
  transfers between devices with their start and end apart: 16 -> 17, of which waited for: 12 -> 5; matrix products, arithmetic and copies ran while one was open for 7% -> 1% of each run, Pallas kernels for 4% -> 18%
where the time goes in v2:
time: 146 us; the launch traced here: 145 us
  blocking collectives  53.9 us (37%)
  Pallas kernels  37.4 us (26%)
  starting transfers between devices  24.7 us (17%)
  waiting for transfers between devices  21.3 us (15%)
  local copies, waits for them, and re-layouts  6.1 us (4%)
    all_to_all x3, blocking collectives, exchange(): return lax.all_to_all(x, axes, 0, 0, tiled=True)  53.9 us
    pallas_call x13, Pallas kernels, call(): pl.pallas_call(body, out_shape=out_shape, in_specs=[smem] * len(scalars)...  37.4 us
    all_to_all x3, starting transfers between devices, exchange(): return lax.all_to_all(x, axes, 0, 0, tiled=True)  13.9 us
    all_to_all x3, waiting for transfers between devices, exchange(): return lax.all_to_all(x, axes, 0, 0, tiled=True)  12.8 us
    ppermute x12, waiting for transfers between devices, swap(): return lax.ppermute(x, SEQ, [(i, i ^ bit) for i in range(n)])  8.52 us
    ppermute x12, starting transfers between devices, swap(): return lax.ppermute(x, SEQ, [(i, i ^ bit) for i in range(n)])  7.69 us
    unnamed x42, local copies, waits for them, and re-layouts  5.45 us
    ppermute x2, starting transfers between devices, add_over_dp(): other = lax.ppermute(v, 'dp', [(0, 1), (1, 0)])  3.12 us
  transfers between devices with their start and end apart: 17, of which 5 were waited for; matrix products, arithmetic and copies ran while one was open for 1% of the time, Pallas kernels for 18%

profile of v2, /device:TPU:0, one launch (start us, length us, event | category | flops | bytes accessed | tf_op | source)
XLA Modules:
  0.0 145.1 jit_solution(14068561948342120810)
XLA Ops:
  0.6 2.5 %shard_map.111 = (bf16[8,32,1024]{2,1,0:T(8,128)(2,1)}, bf16[32,2048]{1,0:T(8,128)(2,1)}, bf16[32,2048]{1,0:T(8,128)(2,1)}, f32[32,1]{1,0:T(8,128)}, f32[32,1]{1,0:T(8,128)}) custom-call(bf16[128,2048]{1,0:T(8,128)(2,1)} %bitcast.21, bf16[128,2048]{1,0:T(8,128)(2,1)} %bitcast.23, s32[1,128]{1,0:T(1,128)} %picks_ref.5, f32[1,2048]{1,0:T(1,128)} %bitcast.27, ...), custom_call_target="tpu_custom_call" | custom-call | tf_op jit(solution)/shard_map/pallas_call | solution.py:39
  3.1 21.8 %all_to_all.30.mine_ref = bf16[8,32,1024]{2,1,0:T(8,128)(2,1)S(1)} all-to-all(bf16[8,32,1024]{2,1,0:T(8,128)(2,1)} %get-tuple-element.37), channel_id=1, replica_groups=mesh['dp'=2,'zz'=4,'yy'=2,'cc'=2] {'zz','yy'}, dimensions={0} | all-to-all | bytes 1048576 | tf_op jit(solution)/shard_map/all_to_all | solution.py:350
  25.0 0.8 pad_add_fusion.at_ref
  25.7 2.5 %shard_map.112 = (bf16[128,320]{1,0:T(8,128)(2,1)}, bf16[128,320]{1,0:T(8,128)(2,1)}, bf16[128,320]{1,0:T(8,128)(2,1)}, bf16[128,320]{1,0:T(8,128)(2,1)}, bf16[6...) custom-call(s32[4]{0:T(128)} %pad_add_fusion.at_ref, ...), custom_call_target="tpu_custom_call" | custom-call | tf_op jit(solution)/shard_map/pallas_call | solution.py:39
  28.2 1.1 collective-permute-start.4
  29.9 1.7 %collective-permute-start.2 = (bf16[128,320]{1,0:T(8,128)(2,1)}, bf16[128,320]{1,0:T(8,128)(2,1)S(1)}, u32[]{:S(2)}, u32[]{:S(2)}) collective-permute-start(bf16[128,320]{1,0:T(8,128)(2,1)} %get-tuple-element.40), channel_id=1, source_target_pairs={{0,2},{1,3},{2,0},{3,1},{4,6},{5,7},{6,4},{7,5},{8,10},{9,11},{10,... | collective-permute-start | bytes 245768 | tf_op jit(solution)/shard_map/ppermute | solution.py:354
  31.7 1.2 collective-permute-done.4.refs_5_
  33.4 2.5 %collective-permute-done.5.refs_6_ = bf16[64,512]{1,0:T(8,128)(2,1)S(1)} collective-permute-done((bf16[64,512]{1,0:T(8,128)(2,1)}, bf16[64,512]{1,0:T(8,128)(2,1)S(1)}, u32[]{:S(2)}, u32[]{:S(2)}) %collective-permute-start.5) | collective-permute-done | bytes 65568 | tf_op jit(solution)/shard_map/ppermute | solution.py:354
  35.9 1.5 %collective-permute-start.6 = (bf16[64,512]{1,0:T(8,128)(2,1)}, bf16[64,512]{1,0:T(8,128)(2,1)S(1)}, u32[]{:S(2)}, u32[]{:S(2)}) collective-permute-start(bf16[64,512]{1,0:T(8,128)(2,1)} %get-tuple-element.45), channel_id=1, source_target_pairs={{0,12},{1,13},{2,14},{3,15},{4,8},{5,9},{6,10},{7,11},{8,4},{9,5},... | collective-permute-start | bytes 196616 | tf_op jit(solution)/shard_map/ppermute | solution.py:354
  37.4 4.8 %collective-permute-done.6.refs_7_ = bf16[64,512]{1,0:T(8,128)(2,1)S(1)} collective-permute-done((bf16[64,512]{1,0:T(8,128)(2,1)}, bf16[64,512]{1,0:T(8,128)(2,1)S(1)}, u32[]{:S(2)}, u32[]{:S(2)}) %collective-permute-start.6) | collective-permute-done | bytes 65568 | tf_op jit(solution)/shard_map/ppermute | solution.py:354
  42.9 2.2 %shard_map.113 = (bf16[4,128,320]{2,1,0:T(8,128)(2,1)}, bf16[4,64,512]{2,1,0:T(8,128)(2,1)}, bf16[4,4,64,128]{3,2,1,0:T(8,128)(2,1)}) custom-call(s32[4]{0:T(128)} %pad_add_fusion.at_ref, bf16[128,320]{1,0:T(8,128)(2,1)} %get-tuple-element.38.refs_0_, bf16[128,320]{1,0:T(8,128)(2,1)} %copy-done.10, bf16[128,320]{1,0:T(8,128)(2,1)} %copy-done.11, ...), custom_call_target="tpu_custom_call" | custom-call | tf_op jit(solution)/shard_map/pallas_call | solution.py:39
  45.1 0.8 copy-done.5
  45.9 3.6 %shard_map.114 = (f32[4,288,128]{2,1,0:T(8,128)}, bf16[4,256,128]{2,1,0:T(8,128)(2,1)}, bf16[512,256]{1,0:T(8,128)(2,1)}) custom-call(s32[4]{0:T(128)} %pad_add_fusion.at_ref, bf16[8,32,1024]{2,1,0:T(8,128)(2,1)} %copy-done.1, bf16[8,32,1024]{2,1,0:T(8,128)(2,1)} %copy-done.5, bf16[4,128,320]{2,1,0:T(8,128)(2,1)} %get-tuple-element.46.wqkv_ref, ...), custom_call_target="tpu_custom_call" | custom-call | tf_op jit(solution)/shard_map/pallas_call | solution.py:39
  49.5 19.0 %all_to_all.31.part_ref = f32[4,288,128]{2,1,0:T(8,128)} all-to-all(f32[4,288,128]{2,1,0:T(8,128)} %get-tuple-element.48), channel_id=1, replica_groups=mesh['dp'=2,'zz'=4,'yy'=2,'cc'=2] {'zz'}, dimensions={0} | all-to-all | bytes 1179648 | tf_op jit(solution)/shard_map/all_to_all | solution.py:350
  68.5 1.9 %shard_map.115 = (bf16[8,160,128]{2,1,0:T(8,128)(2,1)}, bf16[8,128,128]{2,1,0:T(8,128)(2,1)}) custom-call(f32[4,288,128]{2,1,0:T(8,128)} %all_to_all.31.part_ref), custom_call_target="tpu_custom_call" | custom-call | tf_op jit(solution)/shard_map/pallas_call | solution.py:39
  70.4 13.1 %all_to_all.32.refs_0_ = bf16[8,160,128]{2,1,0:T(8,128)(2,1)S(1)} all-to-all(bf16[8,160,128]{2,1,0:T(8,128)(2,1)} %get-tuple-element.49), channel_id=1, replica_groups=mesh['dp'=2,'zz'=4,'yy'=2,'cc'=2] {'zz','yy'}, dimensions={0} | all-to-all | bytes 655360 | tf_op jit(solution)/shard_map/all_to_all | solution.py:350
  83.5 3.4 %all-to-all-start.4 = ((bf16[8,128,128]{2,1,0:T(8,128)(2,1)}), bf16[8,128,128]{2,1,0:T(8,128)(2,1)S(1)}, u32[]{:S(2)}, u32[]{:S(2)}) async-start(bf16[8,128,128]{2,1,0:T(8,128)(2,1)} %get-tuple-element.53), calls=%async_computation.4 | async-start | bytes 524288 | tf_op jit(solution)/shard_map/all_to_all | solution.py:350
  87.6 1.9 %collective-permute-start.10 = (bf16[4,64,128]{2,1,0:T(8,128)(2,1)S(1)}, bf16[4,64,128]{2,1,0:T(8,128)(2,1)S(1)}, u32[]{:S(2)}, u32[]{:S(2)}) collective-permute-start(bf16[4,64,128]{2,1,0:T(8,128)(2,1)S(1)} %get-tuple-element.64), channel_id=1, source_target_pairs={{0,3},{1,2},{2,1},{3,0},{4,7},{5,6},{6,5},{7,4},{8,11},{9,10},{10,... | collective-permute-start | bytes 196616 | tf_op jit(solution)/shard_map/ppermute | solution.py:354
  89.8 5.4 %all-to-all-done.4.refs_2_ = bf16[8,128,128]{2,1,0:T(8,128)(2,1)S(1)} async-done(((bf16[8,128,128]{2,1,0:T(8,128)(2,1)}), bf16[8,128,128]{2,1,0:T(8,128)(2,1)S(1)}, u32[]{:S(2)}, u32[]{:S(2)}) %all-to-all-start.4) | async-done | bytes 262176 | tf_op jit(solution)/shard_map/all_to_all | solution.py:350
  95.9 1.7 %shard_map.116.refs_2_ = bf16[16,64,128]{2,1,0:T(8,128)(2,1)} custom-call(s32[4]{0:T(128)} %pad_add_fusion.at_ref, bf16[4,64,128]{2,1,0:T(8,128)(2,1)} %get-tuple-element.67.refs_0_, bf16[4,64,128]{2,1,0:T(8,128)(2,1)} %copy-done.18, bf16[4,64,128]{2,1,0:T(8,128)(2,1)} %copy-done.16, bf16[4,64,128]{2,1,0:T(8,128)(2,1)} %copy-done.15), custom_call_target="tpu_custom_call" | custom-call | tf_op jit(solution)/shard_map/pallas_call | solution.py:39
  98.3 4.7 %shard_map.117 = (bf16[16,32,128]{2,1,0:T(8,128)(2,1)}, bf16[256,256]{1,0:T(8,128)(2,1)}, f32[16,128,128]{2,1,0:T(8,128)}, f32[16,128,256]{2,1,0:T(8,128)}) custom-call(s32[4]{0:T(128)} %pad_add_fusion.at_ref, bf16[8,160,128]{2,1,0:T(8,128)(2,1)} %copy-done, bf16[8,160,128]{2,1,0:T(8,128)(2,1)} %copy-done.2, bf16[16,64,128]{2,1,0:T(8,128)(2,1)} %shard_map.116.refs_2_, ...), custom_call_target="tpu_custom_call" | custom-call | tf_op jit(solution)/shard_map/pallas_call | solution.py:39
  103.0 4.5 %all-to-all-start.3 = ((bf16[16,32,128]{2,1,0:T(8,128)(2,1)}), bf16[16,32,128]{2,1,0:T(8,128)(2,1)S(1)}, u32[]{:S(2)}, u32[]{:S(2)}) async-start(bf16[16,32,128]{2,1,0:T(8,128)(2,1)} %get-tuple-element.52), calls=%async_computation.3 | async-start | bytes 262144 | tf_op jit(solution)/shard_map/all_to_all | solution.py:350
  108.3 8.5 %shard_map.118 = (bf16[16,32,128]{2,1,0:T(8,128)(2,1)}, f32[128,256]{1,0:T(8,128)}) custom-call(s32[4]{0:T(128)} %pad_add_fusion.at_ref, bf16[8,160,128]{2,1,0:T(8,128)(2,1)} %copy-done, bf16[8,160,128]{2,1,0:T(8,128)(2,1)} %copy-done.2, bf16[8,128,128]{2,1,0:T(8,128)(2,1)} %copy-done.3, bf16[8,128,128]{2,1,0:T(8,128)(2,1)} %copy-done.7, ...), custom_call_target="tpu_custom_call" | custom-call | tf_op jit(solution)/shard_map/pallas_call | solution.py:39
  117.4 2.1 %shard_map.119 = (bf16[16,48,128]{2,1,0:T(8,128)(2,1)}, bf16[32,2048]{1,0:T(8,128)(2,1)}, f32[32,1]{1,0:T(8,128)}) custom-call(bf16[32,2048]{1,0:T(8,128)(2,1)} %get-tuple-element.34.x_ref, bf16[32,2048]{1,0:T(8,128)(2,1)} %get-tuple-element.35.cot_ref, f32[32,1]{1,0:T(8,128)} %get-tuple-element.36.gate_ref, bf16[16,32,128]{2,1,0:T(8,128)(2,1)} %copy-done.6, ...), custom_call_target="tpu_custom_call" | custom-call | tf_op jit(solution)/shard_map/pallas_call | solution.py:39
  119.5 6.0 %all-to-all-start.5 = ((bf16[16,48,128]{2,1,0:T(8,128)(2,1)}), bf16[16,48,128]{2,1,0:T(8,128)(2,1)S(1)}, u32[]{:S(2)}, u32[]{:S(2)}) async-start(bf16[16,48,128]{2,1,0:T(8,128)(2,1)} %get-tuple-element.62), calls=%async_computation.5 | async-start | bytes 393216 | tf_op jit(solution)/shard_map/all_to_all | solution.py:350
  125.5 1.6 %collective-permute-start.12 = (f32[128,256]{1,0:T(8,128)}, f32[128,256]{1,0:T(8,128)S(1)}, u32[]{:S(2)}, u32[]{:S(2)}) collective-permute-start(f32[128,256]{1,0:T(8,128)} %get-tuple-element.63.a_ref), channel_id=1, source_target_pairs={{0,16},{16,0},{1,17},{17,1},{2,18},{18,2},{3,19},{19,3},{4,20},{20... | collective-permute-start | bytes 393224 | tf_op jit(solution)/shard_map/ppermute | solution.py:518
  127.1 7.4 %all-to-all-done.5.got_ref = bf16[16,48,128]{2,1,0:T(8,128)(2,1)S(1)} async-done(((bf16[16,48,128]{2,1,0:T(8,128)(2,1)}), bf16[16,48,128]{2,1,0:T(8,128)(2,1)S(1)}, u32[]{:S(2)}, u32[]{:S(2)}) %all-to-all-start.5) | async-done | bytes 196640 | tf_op jit(solution)/shard_map/all_to_all | solution.py:350
  134.5 1.6 %collective-permute-start.13 = (f32[1,128]{1,0:T(1,128)S(1)}, f32[1,128]{1,0:T(1,128)S(1)}, u32[]{:S(2)}, u32[]{:S(2)}) collective-permute-start(f32[1,128]{1,0:T(1,128)S(1)} %bitcast.31), channel_id=1, source_target_pairs={{0,16},{16,0},{1,17},{17,1},{2,18},{18,2},{3,19},{19,3},{4,20},{20... | collective-permute-start | bytes 1544 | tf_op jit(solution)/shard_map/ppermute | solution.py:518
  136.8 1.6 %shard_map.122 = f32[128,256]{1,0:T(8,128)} custom-call(f32[128,256]{1,0:T(8,128)} %get-tuple-element.63.a_ref, f32[128,256]{1,0:T(8,128)} %copy-done.9), custom_call_target="tpu_custom_call" | custom-call | tf_op jit(solution)/shard_map/pallas_call | solution.py:39
  138.4 2.4 %shard_map.120 = bf16[128,2048]{1,0:T(8,128)(2,1)} custom-call(bf16[128,2048]{1,0:T(8,128)(2,1)} %bitcast.22, s32[1,128]{1,0:T(1,128)} %picks_ref.5, bf16[32,2048]{1,0:T(8,128)(2,1)} %get-tuple-element.59.mixed_ref), custom_call_target="tpu_custom_call" | custom-call | tf_op jit(solution)/shard_map/pallas_call | solution.py:39
  140.8 2.5 %shard_map.121 = bf16[128,2048]{1,0:T(8,128)(2,1)} custom-call(bf16[128,2048]{1,0:T(8,128)(2,1)} %bitcast.24, s32[1,128]{1,0:T(1,128)} %picks_ref.5, f32[1,2048]{1,0:T(1,128)} %bitcast.30, f32[32,1]{1,0:T(8,128)} %get-tuple-element.60.logit_ref, bf16[32,2048]{1,0:T(8,128)(2,1)} %get-tuple-element.34.x_ref, bf16[32,2048]{1,0:T(8,128)(2,1)} %get-tuple-element.35.cot_ref, ...), custom_call_target="tpu_custom_call" | custom-call | tf_op jit(solution)/shard_map/pallas_call | solution.py:39
  143.9 1.2 shard_map.123
  (63 shorter events, 6.9 us)
Async XLA Ops:
  25.0 20.2 %copy-start.1 = (bf16[8,32,1024]{2,1,0:T(8,128)(2,1)}, bf16[8,32,1024]{2,1,0:T(8,128)(2,1)S(1)}, u32[]{:S(2)}) copy-start(bf16[8,32,1024]{2,1,0:T(8,128)(2,1)S(1)} %all_to_all.30.mine_ref) | copy-start | bytes 1572868
  25.0 20.1 %collective-permute-start = (bf16[8,32,1024]{2,1,0:T(8,128)(2,1)S(1)}, bf16[8,32,1024]{2,1,0:T(8,128)(2,1)S(1)}, u32[]{:S(2)}, u32[]{:S(2)}) collective-permute-start(bf16[8,32,1024]{2,1,0:T(8,128)(2,1)S(1)} %all_to_all.30.mine_ref), channel_id=1, source_target_pairs={{0,1},{1,0},{2,3},{3,2},{4,5},{5,4},{6,7},{7,6},{8,9},{9,8},{10,11... | collective-permute-start | bytes 1572872 | tf_op jit(solution)/shard_map/ppermute | solution.py:354
  28.2 4.6 %collective-permute-start.4 = (bf16[64,512]{1,0:T(8,128)(2,1)}, bf16[64,512]{1,0:T(8,128)(2,1)S(1)}, u32[]{:S(2)}, u32[]{:S(2)}) collective-permute-start(bf16[64,512]{1,0:T(8,128)(2,1)} %get-tuple-element.43), channel_id=1, source_target_pairs={{0,4},{1,5},{2,6},{3,7},{4,0},{5,1},{6,2},{7,3},{8,12},{9,13},{10,... | collective-permute-start | bytes 196616 | tf_op jit(solution)/shard_map/ppermute | solution.py:354
  29.3 6.7 %collective-permute-start.5 = (bf16[64,512]{1,0:T(8,128)(2,1)}, bf16[64,512]{1,0:T(8,128)(2,1)S(1)}, u32[]{:S(2)}, u32[]{:S(2)}) collective-permute-start(bf16[64,512]{1,0:T(8,128)(2,1)} %get-tuple-element.44), channel_id=1, source_target_pairs={{0,8},{1,9},{2,10},{3,11},{4,12},{5,13},{6,14},{7,15},{8,0},{9,1},... | collective-permute-start | bytes 196616 | tf_op jit(solution)/shard_map/ppermute | solution.py:354
  29.9 12.3 %collective-permute-start.1 = (bf16[128,320]{1,0:T(8,128)(2,1)}, bf16[128,320]{1,0:T(8,128)(2,1)S(1)}, u32[]{:S(2)}, u32[]{:S(2)}) collective-permute-start(bf16[128,320]{1,0:T(8,128)(2,1)} %get-tuple-element.39), channel_id=1, source_target_pairs={{0,1},{1,0},{2,3},{3,2},{4,5},{5,4},{6,7},{7,6},{8,9},{9,8},{10,11... | collective-permute-start | bytes 245768 | tf_op jit(solution)/shard_map/ppermute | solution.py:354
  29.9 12.3 %collective-permute-start.2 = (bf16[128,320]{1,0:T(8,128)(2,1)}, bf16[128,320]{1,0:T(8,128)(2,1)S(1)}, u32[]{:S(2)}, u32[]{:S(2)}) collective-permute-start(bf16[128,320]{1,0:T(8,128)(2,1)} %get-tuple-element.40), channel_id=1, source_target_pairs={{0,2},{1,3},{2,0},{3,1},{4,6},{5,7},{6,4},{7,5},{8,10},{9,11},{10,... | collective-permute-start | bytes 245768 | tf_op jit(solution)/shard_map/ppermute | solution.py:354
  32.8 9.4 %copy-start.13 = (bf16[64,512]{1,0:T(8,128)(2,1)}, bf16[64,512]{1,0:T(8,128)(2,1)S(1)}, u32[]{:S(2)}) copy-start(bf16[64,512]{1,0:T(8,128)(2,1)S(1)} %collective-permute-done.4.refs_5_) | copy-start | bytes 196612
  32.8 9.4 %collective-permute-start.3 = (bf16[128,320]{1,0:T(8,128)(2,1)}, bf16[128,320]{1,0:T(8,128)(2,1)S(1)}, u32[]{:S(2)}, u32[]{:S(2)}) collective-permute-start(bf16[128,320]{1,0:T(8,128)(2,1)} %get-tuple-element.41), channel_id=1, source_target_pairs={{0,3},{1,2},{2,1},{3,0},{4,7},{5,6},{6,5},{7,4},{8,11},{9,10},{10,... | collective-permute-start | bytes 245768 | tf_op jit(solution)/shard_map/ppermute | solution.py:354
  35.9 6.3 %copy-start.14 = (bf16[64,512]{1,0:T(8,128)(2,1)}, bf16[64,512]{1,0:T(8,128)(2,1)S(1)}, u32[]{:S(2)}) copy-start(bf16[64,512]{1,0:T(8,128)(2,1)S(1)} %collective-permute-done.5.refs_6_) | copy-start | bytes 196612
  35.9 6.3 %collective-permute-start.6 = (bf16[64,512]{1,0:T(8,128)(2,1)}, bf16[64,512]{1,0:T(8,128)(2,1)S(1)}, u32[]{:S(2)}, u32[]{:S(2)}) collective-permute-start(bf16[64,512]{1,0:T(8,128)(2,1)} %get-tuple-element.45), channel_id=1, source_target_pairs={{0,12},{1,13},{2,14},{3,15},{4,8},{5,9},{6,10},{7,11},{8,4},{9,5},... | collective-permute-start | bytes 196616 | tf_op jit(solution)/shard_map/ppermute | solution.py:354
  42.2 0.7 copy-start.11
  42.2 0.7 copy-start.12
  45.1 0.8 copy-start.5
  45.9 41.1 %copy-start.8 = (bf16[4,4,64,128]{3,2,1,0:T(8,128)(2,1)S(1)}, bf16[4,4,64,128]{3,2,1,0:T(8,128)(2,1)}, u32[]{:S(2)}) copy-start(bf16[4,4,64,128]{3,2,1,0:T(8,128)(2,1)} %get-tuple-element.50) | copy-start | bytes 786436
  83.5 14.1 %copy-start = (bf16[8,160,128]{2,1,0:T(8,128)(2,1)}, bf16[8,160,128]{2,1,0:T(8,128)(2,1)S(1)}, u32[]{:S(2)}) copy-start(bf16[8,160,128]{2,1,0:T(8,128)(2,1)S(1)} %all_to_all.32.refs_0_) | copy-start | bytes 983044
  83.5 11.7 %all-to-all-start.4 = ((bf16[8,128,128]{2,1,0:T(8,128)(2,1)}), bf16[8,128,128]{2,1,0:T(8,128)(2,1)S(1)}, u32[]{:S(2)}, u32[]{:S(2)}) async-start(bf16[8,128,128]{2,1,0:T(8,128)(2,1)} %get-tuple-element.53), calls=%async_computation.4 | async-start | bytes 524288 | tf_op jit(solution)/shard_map/all_to_all | solution.py:350
  86.9 10.7 %collective-permute-start.7 = (bf16[8,160,128]{2,1,0:T(8,128)(2,1)S(1)}, bf16[8,160,128]{2,1,0:T(8,128)(2,1)S(1)}, u32[]{:S(2)}, u32[]{:S(2)}) collective-permute-start(bf16[8,160,128]{2,1,0:T(8,128)(2,1)S(1)} %all_to_all.32.refs_0_), channel_id=1, source_target_pairs={{0,1},{1,0},{2,3},{3,2},{4,5},{5,4},{6,7},{7,6},{8,9},{9,8},{10,11... | collective-permute-start | bytes 983048 | tf_op jit(solution)/shard_map/ppermute | solution.py:354
  87.6 7.5 %collective-permute-start.10 = (bf16[4,64,128]{2,1,0:T(8,128)(2,1)S(1)}, bf16[4,64,128]{2,1,0:T(8,128)(2,1)S(1)}, u32[]{:S(2)}, u32[]{:S(2)}) collective-permute-start(bf16[4,64,128]{2,1,0:T(8,128)(2,1)S(1)} %get-tuple-element.64), channel_id=1, source_target_pairs={{0,3},{1,2},{2,1},{3,0},{4,7},{5,6},{6,5},{7,4},{8,11},{9,10},{10,... | collective-permute-start | bytes 196616 | tf_op jit(solution)/shard_map/ppermute | solution.py:354
  89.6 5.6 %collective-permute-start.9 = (bf16[4,64,128]{2,1,0:T(8,128)(2,1)S(1)}, bf16[4,64,128]{2,1,0:T(8,128)(2,1)S(1)}, u32[]{:S(2)}, u32[]{:S(2)}) collective-permute-start(bf16[4,64,128]{2,1,0:T(8,128)(2,1)S(1)} %get-tuple-element.65), channel_id=1, source_target_pairs={{0,2},{1,3},{2,0},{3,1},{4,6},{5,7},{6,4},{7,5},{8,10},{9,11},{10,... | collective-permute-start | bytes 196616 | tf_op jit(solution)/shard_map/ppermute | solution.py:354
  89.8 5.4 %collective-permute-start.8 = (bf16[4,64,128]{2,1,0:T(8,128)(2,1)S(1)}, bf16[4,64,128]{2,1,0:T(8,128)(2,1)S(1)}, u32[]{:S(2)}, u32[]{:S(2)}) collective-permute-start(bf16[4,64,128]{2,1,0:T(8,128)(2,1)S(1)} %get-tuple-element.66), channel_id=1, source_target_pairs={{0,1},{1,0},{2,3},{3,2},{4,5},{5,4},{6,7},{7,6},{8,9},{9,8},{10,11... | collective-permute-start | bytes 196616 | tf_op jit(solution)/shard_map/ppermute | solution.py:354
  95.1 12.4 %copy-start.3 = (bf16[8,128,128]{2,1,0:T(8,128)(2,1)}, bf16[8,128,128]{2,1,0:T(8,128)(2,1)S(1)}, u32[]{:S(2)}) copy-start(bf16[8,128,128]{2,1,0:T(8,128)(2,1)S(1)} %all-to-all-done.4.refs_2_) | copy-start | bytes 786436
  95.1 12.4 %collective-permute-start.11 = (bf16[8,128,128]{2,1,0:T(8,128)(2,1)S(1)}, bf16[8,128,128]{2,1,0:T(8,128)(2,1)S(1)}, u32[]{:S(2)}, u32[]{:S(2)}) collective-permute-start(bf16[8,128,128]{2,1,0:T(8,128)(2,1)S(1)} %all-to-all-done.4.refs_2_), channel_id=1, source_target_pairs={{0,1},{1,0},{2,3},{3,2},{4,5},{5,4},{6,7},{7,6},{8,9},{9,8},{10,11... | collective-permute-start | bytes 786440 | tf_op jit(solution)/shard_map/ppermute | solution.py:354
  95.2 0.7 copy-start.16
  95.2 0.7 copy-start.18
  97.6 0.7 copy-start.2
  103.0 13.8 %all-to-all-start.3 = ((bf16[16,32,128]{2,1,0:T(8,128)(2,1)}), bf16[16,32,128]{2,1,0:T(8,128)(2,1)S(1)}, u32[]{:S(2)}, u32[]{:S(2)}) async-start(bf16[16,32,128]{2,1,0:T(8,128)(2,1)} %get-tuple-element.52), calls=%async_computation.3 | async-start | bytes 262144 | tf_op jit(solution)/shard_map/all_to_all | solution.py:350
  107.5 0.7 copy-start.7
  119.5 15.0 %all-to-all-start.5 = ((bf16[16,48,128]{2,1,0:T(8,128)(2,1)}), bf16[16,48,128]{2,1,0:T(8,128)(2,1)S(1)}, u32[]{:S(2)}, u32[]{:S(2)}) async-start(bf16[16,48,128]{2,1,0:T(8,128)(2,1)} %get-tuple-element.62), calls=%async_computation.5 | async-start | bytes 393216 | tf_op jit(solution)/shard_map/all_to_all | solution.py:350
  125.5 10.6 %collective-permute-start.12 = (f32[128,256]{1,0:T(8,128)}, f32[128,256]{1,0:T(8,128)S(1)}, u32[]{:S(2)}, u32[]{:S(2)}) collective-permute-start(f32[128,256]{1,0:T(8,128)} %get-tuple-element.63.a_ref), channel_id=1, source_target_pairs={{0,16},{16,0},{1,17},{17,1},{2,18},{18,2},{3,19},{19,3},{4,20},{20... | collective-permute-start | bytes 393224 | tf_op jit(solution)/shard_map/ppermute | solution.py:518
  134.5 6.3 %copy-start.4 = (bf16[16,48,128]{2,1,0:T(8,128)(2,1)}, bf16[16,48,128]{2,1,0:T(8,128)(2,1)S(1)}, u32[]{:S(2)}) copy-start(bf16[16,48,128]{2,1,0:T(8,128)(2,1)S(1)} %all-to-all-done.5.got_ref) | copy-start | bytes 589828
  134.5 8.8 %copy-start.19 = (f32[128]{0:T(128)}, f32[128]{0:T(128)S(1)}, u32[]{:S(2)}) copy-start(f32[128]{0:T(128)S(1)} %convert_reduce_fusion) | copy-start | bytes 1540
  134.5 8.8 %collective-permute-start.13 = (f32[1,128]{1,0:T(1,128)S(1)}, f32[1,128]{1,0:T(1,128)S(1)}, u32[]{:S(2)}, u32[]{:S(2)}) collective-permute-start(f32[1,128]{1,0:T(1,128)S(1)} %bitcast.31), channel_id=1, source_target_pairs={{0,16},{16,0},{1,17},{17,1},{2,18},{18,2},{3,19},{19,3},{4,20},{20... | collective-permute-start | bytes 1544 | tf_op jit(solution)/shard_map/ppermute | solution.py:518
  (6 other events, 3.8 us)

commit v3 on v2

v3 whole, which is shorter than its diff:
```python
import functools

import jax
import jax.numpy as jnp
from jax import lax
from jax.experimental import pallas as pl
from jax.experimental.pallas import tpu as pltpu
from jax.sharding import Mesh, PartitionSpec as P


MODEL_WIDTH = 2048
QUERY_HEADS = 16
KEY_VALUE_HEADS = 2
HEAD_SIZE = 64
GROUP = QUERY_HEADS // KEY_VALUE_HEADS
KV_WIDTH = 2 * KEY_VALUE_HEADS * HEAD_SIZE
Q_WIDTH = QUERY_HEADS * HEAD_SIZE
EPSILON = 1e-05
PLANE = 4
LANES = 128
LINES = ("zz", "yy")
SEQ = LINES + ("cc",)

F32 = jnp.float32
BF16 = jnp.bfloat16


def dot(a, b, ca=1, cb=0, precision=None):
    return lax.dot_general(a, b, (((ca,), (cb,)), ((), ())), precision=precision, preferred_element_type=F32)


def pieces(v):
    high = v.astype(BF16).astype(F32)
    middle = (v - high).astype(BF16).astype(F32)
    return high, middle, v - high - middle


def iota(shape, dim):
    return lax.broadcasted_iota(jnp.int32, shape, dim)


def call(body, out_shape, *args, scalars=(), scratch=()):
    vmem = pl.BlockSpec(memory_space=pltpu.VMEM)
    smem = pl.BlockSpec(memory_space=pltpu.SMEM)
    return pl.pallas_call(
        body,
        out_shape=out_shape,
        in_specs=[smem] * len(scalars) + [vmem] * len(args),
        out_specs=jax.tree.map(lambda _: vmem, out_shape),
        scratch_shapes=list(scratch),
    )(*scalars, *args)


def shaped(shape, dtype):
    return jax.ShapeDtypeStruct(shape, dtype)


def selection(picks, slots):
    tokens = picks.shape[1]
    picked = jnp.broadcast_to(picks.astype(F32), (8, tokens)).astype(BF16)
    before = (iota((tokens, tokens), 0) < iota((tokens, tokens), 1)).astype(F32).astype(BF16)
    rank = dot(picked, before)[:1].astype(jnp.int32)
    hit = (iota((slots, tokens), 0) == rank) & (picks > 0)
    return hit.astype(F32).astype(BF16)


def pick_kernel(h_ref, c_ref, picks_ref, router_ref, send_ref, x_ref, cot_ref, inv_ref, gate_ref):
    lines, slots = send_ref.shape[0] // 2, send_ref.shape[1]
    width = MODEL_WIDTH // lines
    picks = picks_ref[...]
    sel = selection(picks, slots)
    x = dot(sel, h_ref[...])
    cot = dot(sel, c_ref[...])
    gate = 1.0 / (1.0 + jnp.exp(-jnp.sum(x * router_ref[...], axis=1, keepdims=True)))
    inv = lax.rsqrt(jnp.mean(x * x, axis=1, keepdims=True) + EPSILON)
    inv_ref[...] = inv
    gate_ref[...] = gate
    lane = iota((slots, LANES), 1)
    extra = jnp.where((lane == 6) & (iota((slots, 1), 0) < jnp.sum(picks)), 1.0, 0.0)
    for k, piece in enumerate(pieces(gate) + pieces(inv)):
        extra = jnp.where(lane == k, piece, extra)
    extra = extra.astype(BF16)
    x, cot = x.astype(BF16), cot.astype(BF16)
    x_ref[...] = x
    cot_ref[...] = cot
    for z in range(lines):
        cols = slice(z * width, (z + 1) * width)
        part = jnp.concatenate([x[:, cols], cot[:, cols], extra], axis=1)
        send_ref[2 * z] = part
        send_ref[2 * z + 1] = part


def put(refs, at, value):
    if len(refs) == 1:
        refs[0][at] = value
        return
    for k, ref in enumerate(refs):

        @pl.when(at == k)
        def _(ref=ref):
            ref[...] = value


def weights_kernel(at_ref, wq_ref, wkv_ref, wo_ref, *outs, lines, cpd, kpd):
    z, p = at_ref[0], at_ref[1]
    to_plane, to_lines = outs[:PLANE], outs[PLANE:]
    width = wo_ref.shape[1] // lines
    for r in range(PLANE):
        places = [PLANE * k + r for k in range(lines)]
        columns = [wq_ref[:, i * cpd : (i + 1) * cpd] for i in places]
        columns += [wkv_ref[:, i * kpd : (i + 1) * kpd] for i in places]
        put(to_plane, p ^ r, jnp.concatenate(columns, axis=1))
    for k in range(lines):
        put(to_lines, z ^ k, wo_ref[:, k * width : (k + 1) * width])


def arrange_kernel(at_ref, *refs):
    z, p = at_ref[0], at_ref[1]
    wqkv_ref, wout_ref, cols_ref = refs[-3:]
    lines, _, width = wout_ref.shape
    fb = width // PLANE
    for r in range(PLANE):
        wqkv_ref[p ^ r] = refs[r][...]
    for k in range(lines):
        rows = refs[PLANE + k][...]
        wout_ref[z ^ k] = rows
        for r in range(PLANE):
            cols_ref[p ^ r, z ^ k] = rows[:, r * fb : (r + 1) * fb]


def columns_kernel(at_ref, *refs):
    out_ref = refs[-1]
    for r in range(PLANE):
        for k in range(refs[r].shape[0]):
            out_ref[PLANE * k + (at_ref[1] ^ r)] = refs[r][k]


def load_both(core, mine_ref, other_ref, all_ref):
    for i in range(mine_ref.shape[0]):
        all_ref[2 * i + core] = mine_ref[i]
        all_ref[2 * i + 1 - core] = other_ref[i]


def heads_kernel(at_ref, mine_ref, other_ref, wqkv_ref, wout_ref, gain_ref, *refs, rows, cpd, kpd, packed):
    core = at_ref[3]
    outs, got_ref = refs[:-1], refs[-1]
    part_ref, place_ref, gate_ref, normed_ref, x_ref, cot_ref = outs[:6]
    lines = part_ref.shape[0]
    load_both(core, mine_ref, other_ref, got_ref)
    n, per, width = got_ref.shape
    slots = n * per
    half = (width - LANES) // 2
    fb = half // PLANE
    got = got_ref[...].reshape(slots, width)
    valid = got[:, 2 * half + 6 : 2 * half + 7].astype(F32) > 0.5
    ones = jnp.broadcast_to(jnp.where(valid, 1.0, 0.0), (slots, 128)).astype(BF16)
    earlier = (iota((slots, slots), 1) < iota((slots, slots), 0)).astype(F32).astype(BF16)
    rank = dot(earlier, ones)[:, :1].astype(jnp.int32)
    rank = jnp.where(valid, rank, -1)
    place = (rank == iota((slots, rows), 1)).astype(F32).astype(BF16)
    place_ref[...] = place
    compact = dot(place, got, 0, 0)
    extra = compact[:, 2 * half :]
    x, cot = compact[:, :half], compact[:, half : 2 * half]
    add_up = lambda k: extra[:, k : k + 1] + extra[:, k + 1 : k + 2] + extra[:, k + 2 : k + 3]
    gate, inv = add_up(0), add_up(3)
    normed = (x * inv * gain_ref[at_ref[0]]).astype(BF16)
    grads = (gate * cot).astype(BF16)
    three = jnp.where(iota((8, LANES), 1) < 3, 1.0, 0.0).astype(BF16)
    gate_ref[...] = dot(three, extra.astype(BF16), 1, 1)
    for r in range(PLANE):
        cols = slice(r * fb, (r + 1) * fb)

        @pl.when(at_ref[1] == r)
        def _(cols=cols):
            normed_ref[...] = normed[:, cols]
            x_ref[...] = x[:, cols].astype(BF16)
            cot_ref[...] = cot[:, cols].astype(BF16)

    wqkv = wqkv_ref[...].reshape(half, lines * (cpd + kpd))
    query = dot(normed, wqkv[:, : lines * cpd])
    kv = dot(wqkv[:, lines * cpd :], normed, 0, 1)
    grad_heads = dot(grads, wout_ref[...].reshape(lines * cpd, half), 1, 1)
    top = rows // 2
    beside = lambda m: jnp.concatenate([m[:top], m[top:]], axis=1)
    for k in range(lines):
        q_part = query[:, k * cpd : (k + 1) * cpd]
        kv_part = kv[k * kpd : (k + 1) * kpd]
        g_part = grad_heads[:, k * cpd : (k + 1) * cpd]
        if packed:
            part_ref[k, :top] = beside(q_part)
            part_ref[k, top : top + kpd] = kv_part[:, :top]
            part_ref[k, top + kpd : top + 2 * kpd] = kv_part[:, top:]
            part_ref[k, top + 2 * kpd :] = beside(g_part)
        else:
            part_ref[k, :, :cpd] = q_part
            outs[6][k] = kv_part
            part_ref[k, :, cpd:] = g_part


def sum_kernel(part_ref, q_ref, g_ref):
    total = sum(part_ref[k] for k in range(part_ref.shape[0])).astype(BF16)
    lead = q_ref.shape[1]
    for i in range(q_ref.shape[0]):
        q_ref[i] = total[:lead]
        g_ref[i] = total[lead:]


def load_kv(q_all, kv_ref, kpd, top):
    n = q_all.shape[0]
    for i in range(n):
        kv_ref[i * kpd : (i + 1) * kpd, :top] = q_all[i, top : top + kpd]
        kv_ref[i * kpd : (i + 1) * kpd, top:] = q_all[i, top + kpd : top + 2 * kpd]


def probabilities(q, kt):
    heads, top, lanes = q.shape
    scale = HEAD_SIZE**-0.5

    def soft(padded, start):
        scores = dot(q.reshape(heads * top, lanes), padded).reshape(heads, top, padded.shape[1])
        allowed = iota(scores.shape, 2) <= iota(scores.shape, 1) + start
        scores = jnp.where(allowed, scores * scale, -jnp.inf)
        e = jnp.exp(scores - jnp.max(scores, axis=2, keepdims=True))
        return e / jnp.sum(e, axis=2, keepdims=True)

    zero = jnp.zeros_like(kt)
    low = soft(jnp.concatenate([kt[:, :top], zero[:, :top]], axis=0), 0)
    return low, soft(jnp.concatenate([zero, kt], axis=0), top)


def flat(x):
    return x.reshape(x.shape[0] * x.shape[1], x.shape[2])


def by_lanes(ref, first, low, high):
    top = ref.shape[0] // 2
    for start, part in ((0, low), (top, high)):
        for i in range(0, part.shape[0] // top, 2):
            both = [part[(i + j) * top : (i + j + 1) * top] for j in range(2)]
            lanes = pl.ds(pl.multiple_of((first + i) * HEAD_SIZE, 2 * HEAD_SIZE), 2 * HEAD_SIZE)
            ref[start : start + top, lanes] = jnp.concatenate(both, axis=1).astype(BF16)


def over_heads(body, heads, packed):
    if packed:
        for group in range(KEY_VALUE_HEADS):
            body(group * GROUP, GROUP, group)
    else:

        @pl.loop(0, heads // 2)
        def _(j):
            body(2 * j, 2, j // (GROUP // 2))


def forward_kernel(at_ref, *refs, packed, kpd):
    sources, (cols_ref, place_ref, cot_ref, send_ref, kv_out_ref, through_ref) = refs[:2], refs[2:8]
    probs_refs = refs[8:-2]
    q_all, mixed_ref = refs[-2:]
    heads, top = q_all.shape[0], mixed_ref.shape[0] // 2
    if packed:
        load_both(at_ref[3], *sources, q_all)
        load_kv(q_all, kv_out_ref, kpd, top)
    else:
        q_all[...] = sources[0][...]
        kv_out_ref[...] = sources[1][...]

    def some_heads(first, count, group):
        kt = kv_out_ref[pl.ds(group * HEAD_SIZE, HEAD_SIZE), :]
        vt = kv_out_ref[pl.ds((KEY_VALUE_HEADS + group) * HEAD_SIZE, HEAD_SIZE), :]
        low, high = probabilities(q_all[pl.ds(first, count), :top], kt)
        for ref, value in zip(probs_refs, (low, high)):
            ref[pl.ds(first, count)] = value
        low, high = flat(low).astype(BF16), flat(high).astype(BF16)
        by_lanes(mixed_ref, first, dot(low, vt[:, :top], 1, 1), dot(high, vt, 1, 1))

    over_heads(some_heads, heads, packed)
    n, slots, _ = send_ref.shape
    out = dot(mixed_ref[...], cols_ref[...].reshape(Q_WIDTH, cols_ref.shape[2])).astype(BF16)
    terms = cot_ref[...].astype(F32) * out.astype(F32)
    through_ref[...] = dot(jnp.ones((8, terms.shape[1]), F32), terms, 1, 1, lax.Precision.HIGHEST)
    spread = dot(place_ref[...], out).astype(BF16)
    for d in range(n):
        send_ref[d] = spread[d * slots : (d + 1) * slots]


def backward_kernel(at_ref, *refs, packed, kpd):
    count = 4 if packed else 2
    sources = refs[:count]
    kv_ref, wq_ref, wkv_ref, gain_ref, normed_ref, place_ref, out_ref = refs[count : count + 7]
    probs_refs = refs[count + 7 : -6]
    send_ref, kv_grad_ref = refs[-6:-4]
    q_all, g_all, gq_ref, gkv_ref = refs[-4:]
    heads, top = q_all.shape[0], gq_ref.shape[0] // 2
    for source, all_ref in ((sources[: count // 2], q_all), (sources[count // 2 :], g_all)):
        if packed:
            load_both(at_ref[3], *source, all_ref)
        else:
            all_ref[...] = source[0][...]
    scale = HEAD_SIZE**-0.5
    gkv_ref[...] = jnp.zeros(gkv_ref.shape, F32)

    def some_heads(first, count, group):
        some = pl.ds(first, count)
        keys = pl.ds(group * HEAD_SIZE, HEAD_SIZE)
        values = pl.ds((KEY_VALUE_HEADS + group) * HEAD_SIZE, HEAD_SIZE)
        kt, vt = kv_ref[keys, :], kv_ref[values, :]
        q, g = q_all[some, :top], flat(g_all[some])
        low, high = [ref[some] for ref in probs_refs] or probabilities(q, kt)
        q = flat(q)
        zero = jnp.zeros_like(vt)

        def back(probs, padded):
            gp = dot(g, padded).reshape(probs.shape)
            inner = jnp.sum(probs * gp, axis=2, keepdims=True)
            return flat((probs * (gp - inner)).astype(BF16))

        gs_low = back(low, jnp.concatenate([vt[:, :top], zero[:, :top]], axis=0))
        gs_high = back(high, jnp.concatenate([zero, vt], axis=0))
        low, high = flat(low).astype(BF16), flat(high).astype(BF16)
        gkv_ref[keys, :] += dot(q, gs_high, 0, 0)[HEAD_SIZE:] * scale
        gkv_ref[keys, :top] += dot(q, gs_low, 0, 0)[:HEAD_SIZE] * scale
        gkv_ref[values, :] += dot(g, high, 0, 0)[HEAD_SIZE:]
        gkv_ref[values, :top] += dot(g, low, 0, 0)[:HEAD_SIZE]
        by_lanes(gq_ref, first, dot(gs_low, kt[:, :top], 1, 1) * scale, dot(gs_high, kt, 1, 1) * scale)

    over_heads(some_heads, heads, packed)
    n, slots, fb = out_ref.shape
    gkv = gkv_ref[...].astype(BF16)
    up = (dot(gq_ref[...], wq_ref[...], 1, 1) + dot(gkv, wkv_ref[...], 0, 1)) * gain_ref[at_ref[2]]
    spread = dot(place_ref[...], up.astype(BF16)).astype(BF16)
    for d in range(n):
        send_ref[d, :, :fb] = out_ref[d]
        send_ref[d, :, fb:] = spread[d * slots : (d + 1) * slots]
    kv_grad_ref[...] = dot(normed_ref[...], gkv, 0, 1)


def router_kernel(x_ref, gate_ref, *refs):
    gate, out_ref = gate_ref[...], refs[-1]
    grad_logit = sum(ref[...] for ref in refs[:-1]) * gate * (1.0 - gate)
    out_ref[...] = dot(grad_logit, x_ref[...].astype(F32), 1, 0, lax.Precision.HIGHEST)


def place_rows(picks, rows, tokens):
    sel = selection(picks, rows.shape[0])
    taken = dot(sel, jnp.ones((rows.shape[0], 128), BF16), 0, 0)[:, :1] > 0.5
    return jnp.where(taken, dot(sel, rows, 0, 0), tokens.astype(F32)).astype(BF16)


def add_kernel(a_ref, b_ref, out_ref):
    out_ref[...] = a_ref[...] + b_ref[...]


def finish_kernel(
    h_ref, c_ref, picks_ref, router_ref, gate_ref, x_ref, cot_ref, inv_ref, got_ref, part_ref, other_ref,
    mixed_ref, grad_ref, router_grad_ref
):
    router_grad_ref[...] = part_ref[:1] + other_ref[:1]
    n, _, width = got_ref.shape
    fb = width // 2
    take = lambda k: jnp.concatenate([got_ref[d, :, k * fb : (k + 1) * fb] for d in range(n)], axis=1).astype(F32)
    out, up = take(0), take(1)
    x, inv, gate = x_ref[...].astype(F32), inv_ref[...], gate_ref[...]
    picks = picks_ref[...]
    mixed_ref[...] = place_rows(picks, (x + gate * out).astype(BF16), h_ref[...])
    cot = cot_ref[...].astype(F32)
    grad_logit = jnp.sum(cot * out, axis=1, keepdims=True) * gate * (1.0 - gate)
    grad_block = inv * up - x * inv**3 * jnp.mean(up * x, axis=1, keepdims=True)
    grad_block = grad_block.astype(BF16).astype(F32)
    rows = (cot + grad_logit * router_ref[...] + grad_block).astype(BF16)
    grad_ref[...] = place_rows(picks, rows, c_ref[...])


def exchange(x, axes):
    return lax.all_to_all(x, axes, 0, 0, tiled=True)


def swap(x, n, bit):
    return lax.ppermute(x, SEQ, [(i, i ^ bit) for i in range(n)])


def block(hidden, cotangent, picks, gain, router, w_query, w_kv, w_out):
    lines = lax.axis_size("zz")
    n = lines * PLANE
    dp = lax.axis_size("dp")
    z, core = lax.axis_index("zz"), lax.axis_index("cc")
    p = 2 * lax.axis_index("yy") + core
    me = PLANE * z + p
    where = jnp.stack([z, p, me, core]).astype(jnp.int32)
    hidden, cotangent = hidden[0], cotangent[0]
    tokens = hidden.shape[0]
    slots = tokens // 4
    rows = n * (tokens // 8)
    top = rows // 2
    fb = MODEL_WIDTH // n
    cpd = Q_WIDTH // n
    kpd = KV_WIDTH // n
    packed = cpd == HEAD_SIZE
    as_row = lambda v: v.reshape(1, -1)

    lines_apart = lines <= 4
    to_plane = [shaped((fb, lines * (cpd + kpd)), BF16)] * PLANE
    to_lines = [shaped((cpd, PLANE * fb), BF16)] * lines if lines_apart else [shaped((lines, cpd, PLANE * fb), BF16)]
    out = call(
        functools.partial(weights_kernel, lines=lines, cpd=cpd, kpd=kpd),
        tuple(to_plane + to_lines),
        w_query,
        w_kv,
        w_out,
        scalars=(where,),
    )
    to_plane, to_lines = out[:PLANE], out[PLANE:]
    if not lines_apart:
        to_lines = [to_lines[0][k] for k in range(lines)]
    wqkv = [to_plane[0]] + [swap(to_plane[r], n, r) for r in range(1, PLANE)]
    wout = [to_lines[0]] + [swap(to_lines[k], n, PLANE * k) for k in range(1, lines)]
    wqkv, wout, cols = call(
        arrange_kernel,
        (
            shaped((PLANE, fb, lines * (cpd + kpd)), BF16),
            shaped((lines, cpd, PLANE * fb), BF16),
            shaped((PLANE, lines, cpd, fb), BF16),
        ),
        *wqkv,
        *wout,
        scalars=(where,),
    )

    send, x, cot, inv, gate = call(
        pick_kernel,
        (
            shaped((2 * lines, slots, 2 * PLANE * fb + LANES), BF16),
            shaped((slots, MODEL_WIDTH), BF16),
            shaped((slots, MODEL_WIDTH), BF16),
            shaped((slots, 1), F32),
            shaped((slots, 1), F32),
        ),
        hidden,
        cotangent,
        picks,
        as_row(router),
    )
    mine = exchange(send, LINES)
    other = swap(mine, n, 1)

    part = (lines, top + 2 * kpd + top, 2 * cpd) if packed else (lines, rows, 2 * cpd)
    outs = [
        shaped(part, F32),
        shaped((n * slots, rows), BF16),
        shaped((8, rows), F32),
    ]
    outs += [shaped((rows, fb), BF16)] * 3
    if not packed:
        outs += [shaped((lines, kpd, rows), F32)]
    part, place, gate_rows, normed, own_x, own_cot, *kv_part = call(
        functools.partial(heads_kernel, rows=rows, cpd=cpd, kpd=kpd, packed=packed),
        tuple(outs),
        mine,
        other,
        wqkv,
        wout,
        gain.reshape(lines, 1, PLANE * fb),
        scalars=(where,),
        scratch=(pltpu.VMEM((n, slots, 2 * PLANE * fb + LANES), BF16),),
    )
    cols = [cols[0]] + [swap(cols[r], n, r) for r in range(1, PLANE)]
    cols = call(columns_kernel, shaped((n, cpd, fb), BF16), *cols, scalars=(where,))
    part = exchange(part, "zz")
    if packed:
        lead = top + 2 * kpd
        q_pack, g_pack = call(
            sum_kernel, (shaped((2 * lines, lead, 2 * cpd), BF16), shaped((2 * lines, top, 2 * cpd), BF16)), part
        )
        q_refs = exchange(q_pack, LINES)
        q_refs = (q_refs, swap(q_refs, n, 1))
        g_refs = exchange(g_pack, LINES)
        g_refs = (g_refs, swap(g_refs, n, 1))
        kv_refs = ()
    else:
        per = HEAD_SIZE // cpd
        everything = jnp.sum(part, axis=0).astype(BF16)
        everything = lax.all_gather(everything, SEQ, axis=0).reshape(QUERY_HEADS, per, 2, top, 2, cpd)
        everything = everything.transpose(4, 0, 3, 2, 1, 5).reshape(2, QUERY_HEADS, top, 2 * HEAD_SIZE)
        q_refs, g_refs = (everything[0],), (everything[1],)
        kv_part = lax.all_to_all(kv_part[0], "zz", 0, 0, tiled=True)
        kv_part = jnp.sum(kv_part, axis=0).astype(BF16)
        kv_refs = (lax.all_gather(kv_part, SEQ, axis=0, tiled=True),)
    q_scratch = pltpu.VMEM((QUERY_HEADS, top + (2 * kpd if packed else 0), 2 * HEAD_SIZE), BF16)

    probs = (shaped((QUERY_HEADS, top, top), F32), shaped((QUERY_HEADS, top, rows), F32)) if packed else ()
    out, kv_all, through, *probs = call(
        functools.partial(forward_kernel, packed=packed, kpd=kpd),
        (
            shaped((n, slots, fb), BF16),
            shaped((KV_WIDTH, rows), BF16),
            shaped((8, rows), F32),
            *probs,
        ),
        *q_refs,
        *kv_refs,
        cols,
        place,
        own_cot,
        scalars=(where,),
        scratch=(q_scratch, pltpu.VMEM((rows, Q_WIDTH), BF16)),
    )
    through = [through] + [swap(through, n, r) for r in range(1, PLANE)]
    send, kv_part = call(
        functools.partial(backward_kernel, packed=packed, kpd=kpd),
        (shaped((n, slots, 2 * fb), BF16), shaped((fb, KV_WIDTH), F32)),
        *q_refs,
        *g_refs,
        kv_all,
        w_query,
        w_kv,
        gain.reshape(n, 1, fb),
        normed,
        place,
        out,
        *probs,
        scalars=(where,),
        scratch=(
            q_scratch,
            pltpu.VMEM((QUERY_HEADS, top, 2 * HEAD_SIZE), BF16),
            pltpu.VMEM((rows, Q_WIDTH), BF16),
            pltpu.VMEM((KV_WIDTH, rows), F32),
        ),
    )
    got = exchange(send, SEQ)
    through = sum(through[1:], through[0])
    through = [through] + [swap(through, n, PLANE * k) for k in range(1, lines)]
    router_part = call(router_kernel, shaped((8, fb), F32), own_x, gate_rows, *through)
    if dp == 2:
        pair = [(0, 1), (1, 0)]
        other = lax.ppermute(kv_part, "dp", pair)
        kv_grad = call(add_kernel, shaped((fb, KV_WIDTH), F32), kv_part, other)
        router_other = lax.ppermute(router_part, "dp", pair)
    else:
        kv_grad, router_part = lax.psum(kv_part, "dp"), lax.psum(router_part, "dp")
        router_other = jnp.zeros_like(router_part)
    mixed, input_grad, router_grad = call(
        finish_kernel,
        (
            shaped((tokens, MODEL_WIDTH), BF16),
            shaped((tokens, MODEL_WIDTH), BF16),
            shaped((1, fb), F32),
        ),
        hidden,
        cotangent,
        picks,
        as_row(router),
        gate,
        x,
        cot,
        inv,
        got,
        router_part,
        router_other,
    )
    return mixed[None], input_grad[None], kv_grad, router_grad.reshape(fb)


def solution(mesh):
    dp, n = mesh.shape["dp"], mesh.shape["seq"]
    split = Mesh(mesh.devices.reshape(dp, n // PLANE, PLANE // 2, 2), ("dp",) + SEQ)
    rows = P("dp", SEQ, None)
    return jax.shard_map(
        block,
        mesh=split,
        in_specs=(rows, rows, P("dp", SEQ), P(), P(), P(SEQ, None), P(SEQ, None), P(SEQ, None)),
        out_specs=(rows, rows, P(SEQ, None), P(SEQ)),
        check_vma=False,
    )
```

time: 146 us -> 146 us (level)
  waiting for transfers between devices: 21.3 us -> 26.5 us
  Pallas kernels: 37.4 us -> 32.4 us
  starting transfers between devices: 24.7 us -> 22.9 us
  blocking collectives: 53.9 us -> 55.4 us
    ppermute x12 -> x18, waiting for transfers between devices: 8.52 us -> 18.4 us  [swap(): return lax.ppermute(x, SEQ, [(i, i ^ bit) for i in range(n)])]
    all_to_all x3 -> x2, starting transfers between devices: 13.9 us -> 6.94 us  [exchange(): return lax.all_to_all(x, axes, 0, 0, tiled=True)]
    ppermute x12 -> x18, starting transfers between devices: 7.69 us -> 13 us  [swap(): return lax.ppermute(x, SEQ, [(i, i ^ bit) for i in range(n)])]
    pallas_call x13 -> x11, Pallas kernels: 37.4 us -> 32.4 us  [call(): pl.pallas_call(body, out_shape=out_shape, in_specs=[smem] * len(scalars)...]
    all_to_all x3 -> x2, waiting for transfers between devices: 12.8 us -> 8.08 us  [exchange(): return lax.all_to_all(x, axes, 0, 0, tiled=True)]
    all_to_all x3, blocking collectives: 53.9 us -> 55.4 us  [exchange(): return lax.all_to_all(x, axes, 0, 0, tiled=True)]
    unnamed x42 -> x48, local copies, waits for them, and re-layouts: 5.45 us -> 5.55 us
  transfers between devices with their start and end apart: 17 -> 22, of which waited for: 5 -> 9; matrix products, arithmetic and copies ran while one was open for 1% -> 1% of each run, Pallas kernels for 18% -> 10%
where the time goes in v3:
time: 146 us; the launch traced here: 145 us
  blocking collectives  55.4 us (38%)
  Pallas kernels  32.4 us (22%)
  waiting for transfers between devices  26.5 us (18%)
  starting transfers between devices  22.9 us (16%)
  local copies, waits for them, and re-layouts  6.26 us (4%)
    all_to_all x3, blocking collectives, exchange(): return lax.all_to_all(x, axes, 0, 0, tiled=True)  55.4 us
    pallas_call x11, Pallas kernels, call(): pl.pallas_call(body, out_shape=out_shape, in_specs=[smem] * len(scalars)...  32.4 us
    ppermute x18, waiting for transfers between devices, swap(): return lax.ppermute(x, SEQ, [(i, i ^ bit) for i in range(n)])  18.4 us
    ppermute x18, starting transfers between devices, swap(): return lax.ppermute(x, SEQ, [(i, i ^ bit) for i in range(n)])  13 us
    all_to_all x2, waiting for transfers between devices, exchange(): return lax.all_to_all(x, axes, 0, 0, tiled=True)  8.08 us
    all_to_all x2, starting transfers between devices, exchange(): return lax.all_to_all(x, axes, 0, 0, tiled=True)  6.94 us
    unnamed x48, local copies, waits for them, and re-layouts  5.55 us
  transfers between devices with their start and end apart: 22, of which 9 were waited for; matrix products, arithmetic and copies ran while one was open for 1% of the time, Pallas kernels for 10%

profile of v3, /device:TPU:0, one launch (start us, length us, event | category | flops | bytes accessed | tf_op | source)
XLA Modules:
  0.0 145.1 jit_solution(13313435327625189641)
XLA Ops:
  0.6 2.5 %shard_map.111 = (bf16[8,32,1152]{2,1,0:T(8,128)(2,1)}, bf16[32,2048]{1,0:T(8,128)(2,1)}, bf16[32,2048]{1,0:T(8,128)(2,1)}, f32[32,1]{1,0:T(8,128)}, f32[32,1]{1,0:T(8,128)}) custom-call(bf16[128,2048]{1,0:T(8,128)(2,1)} %bitcast.20, bf16[128,2048]{1,0:T(8,128)(2,1)} %bitcast.22, s32[1,128]{1,0:T(1,128)} %picks_ref.3, f32[1,2048]{1,0:T(1,128)} %bitcast.26), custom_call_target="tpu_custom_call" | custom-call | tf_op jit(solution)/shard_map/pallas_call | solution.py:45
  3.1 23.8 %all_to_all.25.mine_ref = bf16[8,32,1152]{2,1,0:T(8,128)(2,1)S(1)} all-to-all(bf16[8,32,1152]{2,1,0:T(8,128)(2,1)} %get-tuple-element.42), channel_id=1, replica_groups=mesh['dp'=2,'zz'=4,'yy'=2,'cc'=2] {'zz','yy'}, dimensions={0} | all-to-all | bytes 1179648 | tf_op jit(solution)/shard_map/all_to_all | solution.py:375
  27.7 2.5 %shard_map.112 = (bf16[128,320]{1,0:T(8,128)(2,1)}, bf16[128,320]{1,0:T(8,128)(2,1)}, bf16[128,320]{1,0:T(8,128)(2,1)}, bf16[128,320]{1,0:T(8,128)(2,1)}, bf16[6...) custom-call(s32[4]{0:T(128)} %pad_add_fusion.at_ref, ...), custom_call_target="tpu_custom_call" | custom-call | tf_op jit(solution)/shard_map/pallas_call | solution.py:45
  30.9 1.3 collective-permute-start.5
  33.0 1.8 %collective-permute-done.4.refs_5_ = bf16[64,512]{1,0:T(8,128)(2,1)S(1)} collective-permute-done((bf16[64,512]{1,0:T(8,128)(2,1)}, bf16[64,512]{1,0:T(8,128)(2,1)S(1)}, u32[]{:S(2)}, u32[]{:S(2)}) %collective-permute-start.4) | collective-permute-done | bytes 65568 | tf_op jit(solution)/shard_map/ppermute | solution.py:379
  34.8 2.8 %collective-permute-done.5.refs_6_ = bf16[64,512]{1,0:T(8,128)(2,1)S(1)} collective-permute-done((bf16[64,512]{1,0:T(8,128)(2,1)}, bf16[64,512]{1,0:T(8,128)(2,1)S(1)}, u32[]{:S(2)}, u32[]{:S(2)}) %collective-permute-start.5) | collective-permute-done | bytes 65568 | tf_op jit(solution)/shard_map/ppermute | solution.py:379
  37.6 1.5 %collective-permute-start.6 = (bf16[64,512]{1,0:T(8,128)(2,1)}, bf16[64,512]{1,0:T(8,128)(2,1)S(1)}, u32[]{:S(2)}, u32[]{:S(2)}) collective-permute-start(bf16[64,512]{1,0:T(8,128)(2,1)} %get-tuple-element.50), channel_id=1, source_target_pairs={{0,12},{1,13},{2,14},{3,15},{4,8},{5,9},{6,10},{7,11},{8,4},{9,5},... | collective-permute-start | bytes 196616 | tf_op jit(solution)/shard_map/ppermute | solution.py:379
  39.1 4.8 %collective-permute-done.6.refs_7_ = bf16[64,512]{1,0:T(8,128)(2,1)S(1)} collective-permute-done((bf16[64,512]{1,0:T(8,128)(2,1)}, bf16[64,512]{1,0:T(8,128)(2,1)S(1)}, u32[]{:S(2)}, u32[]{:S(2)}) %collective-permute-start.6) | collective-permute-done | bytes 65568 | tf_op jit(solution)/shard_map/ppermute | solution.py:379
  44.6 2.1 %shard_map.113 = (bf16[4,128,320]{2,1,0:T(8,128)(2,1)}, bf16[4,64,512]{2,1,0:T(8,128)(2,1)}, bf16[4,4,64,128]{3,2,1,0:T(8,128)(2,1)}) custom-call(s32[4]{0:T(128)} %pad_add_fusion.at_ref, bf16[128,320]{1,0:T(8,128)(2,1)} %get-tuple-element.43.refs_0_, bf16[128,320]{1,0:T(8,128)(2,1)} %copy-done.9, bf16[128,320]{1,0:T(8,128)(2,1)} %copy-done.10, ...), custom_call_target="tpu_custom_call" | custom-call | tf_op jit(solution)/shard_map/pallas_call | solution.py:45
  47.6 4.3 %shard_map.114 = (f32[4,288,128]{2,1,0:T(8,128)}, bf16[512,256]{1,0:T(8,128)(2,1)}, f32[8,256]{1,0:T(8,128)}, bf16[256,128]{1,0:T(8,128)(2,1)}, bf16[256,128]{1,0:T(8,128)(2,1)}, /*index=5*/bf16[256,128]{1,0:T(8,128)(2,1)}) custom-call(s32[4]{0:T(128)} %pad_add_fusion.at_ref, bf16[8,32,1152]{2,1,0:T(8,128)(2,1)} %copy-done.1, ...), custom_call_target="tpu_custom_call" | custom-call | tf_op jit(solution)/shard_map/pallas_call | solution.py:45
  51.9 18.7 %all_to_all.26.part_ref = f32[4,288,128]{2,1,0:T(8,128)} all-to-all(f32[4,288,128]{2,1,0:T(8,128)} %get-tuple-element.53), channel_id=1, replica_groups=mesh['dp'=2,'zz'=4,'yy'=2,'cc'=2] {'zz'}, dimensions={0} | all-to-all | bytes 1179648 | tf_op jit(solution)/shard_map/all_to_all | solution.py:375
  70.6 1.9 %shard_map.115 = (bf16[8,160,128]{2,1,0:T(8,128)(2,1)}, bf16[8,128,128]{2,1,0:T(8,128)(2,1)}) custom-call(f32[4,288,128]{2,1,0:T(8,128)} %all_to_all.26.part_ref), custom_call_target="tpu_custom_call" | custom-call | tf_op jit(solution)/shard_map/pallas_call | solution.py:45
  72.5 12.9 %all_to_all.27.refs_0_ = bf16[8,160,128]{2,1,0:T(8,128)(2,1)S(1)} all-to-all(bf16[8,160,128]{2,1,0:T(8,128)(2,1)} %get-tuple-element.54), channel_id=1, replica_groups=mesh['dp'=2,'zz'=4,'yy'=2,'cc'=2] {'zz','yy'}, dimensions={0} | all-to-all | bytes 655360 | tf_op jit(solution)/shard_map/all_to_all | solution.py:375
  85.4 3.4 %all-to-all-start.3 = ((bf16[8,128,128]{2,1,0:T(8,128)(2,1)}), bf16[8,128,128]{2,1,0:T(8,128)(2,1)S(1)}, u32[]{:S(2)}, u32[]{:S(2)}) async-start(bf16[8,128,128]{2,1,0:T(8,128)(2,1)} %get-tuple-element.55), calls=%async_computation.3 | async-start | bytes 524288 | tf_op jit(solution)/shard_map/all_to_all | solution.py:375
  88.9 8.1 %all-to-all-done.3.refs_2_ = bf16[8,128,128]{2,1,0:T(8,128)(2,1)S(1)} async-done(((bf16[8,128,128]{2,1,0:T(8,128)(2,1)}), bf16[8,128,128]{2,1,0:T(8,128)(2,1)S(1)}, u32[]{:S(2)}, u32[]{:S(2)}) %all-to-all-start.3) | async-done | bytes 262176 | tf_op jit(solution)/shard_map/all_to_all | solution.py:375
  97.7 1.3 collective-permute-start.11
  99.8 1.7 %collective-permute-done.11.refs_3_ = bf16[4,64,128]{2,1,0:T(8,128)(2,1)S(1)} collective-permute-done((bf16[4,64,128]{2,1,0:T(8,128)(2,1)S(1)}, bf16[4,64,128]{2,1,0:T(8,128)(2,1)S(1)}, u32[]{:S(2)}, u32[]{:S(2)}) %collective-permute-start.11) | collective-permute-done | bytes 65568 | tf_op jit(solution)/shard_map/ppermute | solution.py:379
  101.5 2.0 %collective-permute-done.10.refs_2_ = bf16[4,64,128]{2,1,0:T(8,128)(2,1)S(1)} collective-permute-done((bf16[4,64,128]{2,1,0:T(8,128)(2,1)S(1)}, bf16[4,64,128]{2,1,0:T(8,128)(2,1)S(1)}, u32[]{:S(2)}, u32[]{:S(2)}) %collective-permute-start.10) | collective-permute-done | bytes 65568 | tf_op jit(solution)/shard_map/ppermute | solution.py:379
  104.1 1.7 %shard_map.116.refs_2_ = bf16[16,64,128]{2,1,0:T(8,128)(2,1)} custom-call(s32[4]{0:T(128)} %pad_add_fusion.at_ref, bf16[4,64,128]{2,1,0:T(8,128)(2,1)} %get-tuple-element.75.refs_0_, bf16[4,64,128]{2,1,0:T(8,128)(2,1)} %copy-done.17, bf16[4,64,128]{2,1,0:T(8,128)(2,1)} %copy-done.16, bf16[4,64,128]{2,1,0:T(8,128)(2,1)} %copy-done.15), custom_call_target="tpu_custom_call" | custom-call | tf_op jit(solution)/shard_map/pallas_call | solution.py:45
  106.6 5.0 %shard_map.117 = (bf16[16,32,128]{2,1,0:T(8,128)(2,1)}, bf16[256,256]{1,0:T(8,128)(2,1)}, f32[8,256]{1,0:T(8,128)}, f32[16,128,128]{2,1,0:T(8,128)}, f32[16,128,256]{2,1,0:T(8,128)}) custom-call(s32[4]{0:T(128)} %pad_add_fusion.at_ref, bf16[8,160,128]{2,1,0:T(8,128)(2,1)} %copy-done, bf16[8,160,128]{2,1,0:T(8,128)(2,1)} %copy-done.2, ...), custom_call_target="tpu_custom_call" | custom-call | tf_op jit(solution)/shard_map/pallas_call | solution.py:45
  112.3 6.2 %shard_map.118 = (bf16[16,32,256]{2,1,0:T(8,128)(2,1)}, f32[128,256]{1,0:T(8,128)}) custom-call(s32[4]{0:T(128)} %pad_add_fusion.at_ref, bf16[8,160,128]{2,1,0:T(8,128)(2,1)} %copy-done, bf16[8,160,128]{2,1,0:T(8,128)(2,1)} %copy-done.2, bf16[8,128,128]{2,1,0:T(8,128)(2,1)} %copy-done.4, bf16[8,128,128]{2,1,0:T(8,128)(2,1)} %copy-done.7, ...), custom_call_target="tpu_custom_call" | custom-call | tf_op jit(solution)/shard_map/pallas_call | solution.py:45
  118.5 3.5 %all-to-all-start.4 = ((bf16[16,32,256]{2,1,0:T(8,128)(2,1)}), bf16[16,32,256]{2,1,0:T(8,128)(2,1)S(1)}, u32[]{:S(2)}, u32[]{:S(2)}) async-start(bf16[16,32,256]{2,1,0:T(8,128)(2,1)} %get-tuple-element.64), calls=%async_computation.4 | async-start | bytes 524288 | tf_op jit(solution)/shard_map/all_to_all | solution.py:375
  122.0 1.6 %collective-permute-start.14 = (f32[8,256]{1,0:T(8,128)S(1)}, f32[8,256]{1,0:T(8,128)S(1)}, u32[]{:S(2)}, u32[]{:S(2)}) collective-permute-start(f32[8,256]{1,0:T(8,128)S(1)} %copy-done.19), channel_id=1, source_target_pairs={{0,3},{1,2},{2,1},{3,0},{4,7},{5,6},{6,5},{7,4},{8,11},{9,10},{10,... | collective-permute-start | bytes 24584 | tf_op jit(solution)/shard_map/ppermute | solution.py:379
  124.0 1.5 %collective-permute-start.19 = (f32[128,256]{1,0:T(8,128)}, f32[128,256]{1,0:T(8,128)S(1)}, u32[]{:S(2)}, u32[]{:S(2)}) collective-permute-start(f32[128,256]{1,0:T(8,128)} %get-tuple-element.70.a_ref), channel_id=1, source_target_pairs={{0,16},{16,0},{1,17},{17,1},{2,18},{18,2},{3,19},{19,3},{4,20},{20... | collective-permute-start | bytes 393224 | tf_op jit(solution)/shard_map/ppermute | solution.py:535
  125.5 1.8 %collective-permute-done.13 = f32[8,256]{1,0:T(8,128)S(1)} collective-permute-done((f32[8,256]{1,0:T(8,128)S(1)}, f32[8,256]{1,0:T(8,128)S(1)}, u32[]{:S(2)}, u32[]{:S(2)}) %collective-permute-start.13) | collective-permute-done | bytes 8224 | tf_op jit(solution)/shard_map/ppermute | solution.py:379
  127.3 3.5 %collective-permute-start.17 = (f32[8,256]{1,0:T(8,128)S(1)}, f32[8,256]{1,0:T(8,128)S(1)}, u32[]{:S(2)}, u32[]{:S(2)}) collective-permute-start(f32[8,256]{1,0:T(8,128)S(1)} %add_add_fusion.refs_0_), channel_id=1, source_target_pairs={{0,12},{1,13},{2,14},{3,15},{4,8},{5,9},{6,10},{7,11},{8,4},{9,5},... | collective-permute-start | bytes 24584 | tf_op jit(solution)/shard_map/ppermute | solution.py:379
  131.8 1.1 collective-permute-done.17.refs_3_
  132.8 2.6 %collective-permute-done.16.refs_2_ = f32[8,256]{1,0:T(8,128)S(1)} collective-permute-done((f32[8,256]{1,0:T(8,128)S(1)}, f32[8,256]{1,0:T(8,128)S(1)}, u32[]{:S(2)}, u32[]{:S(2)}) %collective-permute-start.16) | collective-permute-done | bytes 8224 | tf_op jit(solution)/shard_map/ppermute | solution.py:379
  136.0 1.7 %shard_map.119.part_ref = f32[8,128]{1,0:T(8,128)} custom-call(bf16[256,128]{1,0:T(8,128)(2,1)} %get-tuple-element.65.x_ref, f32[8,256]{1,0:T(8,128)} %get-tuple-element.66.gate_ref, f32[8,256]{1,0:T(8,128)} %copy-done.18, f32[8,256]{1,0:T(8,128)} %copy-done.22, f32[8,256]{1,0:T(8,128)} %copy-done.21, f32[8,256]{1,0:T(8,128)} %copy-done.20), custom_call_target="tpu_custom_call" | custom-call | tf_op jit(solution)/shard_map/pallas_call | solution.py:45
  137.6 1.5 %collective-permute-start.18 = (f32[8,128]{1,0:T(8,128)}, f32[8,128]{1,0:T(8,128)S(1)}, u32[]{:S(2)}, u32[]{:S(2)}) collective-permute-start(f32[8,128]{1,0:T(8,128)} %shard_map.119.part_ref), channel_id=1, source_target_pairs={{0,16},{16,0},{1,17},{17,1},{2,18},{18,2},{3,19},{19,3},{4,20},{20... | collective-permute-start | bytes 12296 | tf_op jit(solution)/shard_map/ppermute | solution.py:537
  139.8 1.6 %shard_map.121 = f32[128,256]{1,0:T(8,128)} custom-call(f32[128,256]{1,0:T(8,128)} %get-tuple-element.70.a_ref, f32[128,256]{1,0:T(8,128)} %copy-done.8), custom_call_target="tpu_custom_call" | custom-call | tf_op jit(solution)/shard_map/pallas_call | solution.py:45
  142.2 2.9 %shard_map.120 = (bf16[128,2048]{1,0:T(8,128)(2,1)}, bf16[128,2048]{1,0:T(8,128)(2,1)}, f32[1,128]{1,0:T(1,128)}) custom-call(bf16[128,2048]{1,0:T(8,128)(2,1)} %bitcast.21, bf16[128,2048]{1,0:T(8,128)(2,1)} %bitcast.23, s32[1,128]{1,0:T(1,128)} %picks_ref.3, f32[1,2048]{1,0:T(1,128)} %bitcast.27, f32[32,1]{1,0:T(8,128)} %get-tuple-element.38.gate_ref, ...), custom_call_target="tpu_custom_call" | custom-call | tf_op jit(solution)/shard_map/pallas_call | solution.py:45
  (77 shorter events, 10.8 us)
Async XLA Ops:
  27.0 19.8 %copy-start.1 = (bf16[8,32,1152]{2,1,0:T(8,128)(2,1)}, bf16[8,32,1152]{2,1,0:T(8,128)(2,1)S(1)}, u32[]{:S(2)}) copy-start(bf16[8,32,1152]{2,1,0:T(8,128)(2,1)S(1)} %all_to_all.25.mine_ref) | copy-start | bytes 1769476
  27.0 19.8 %collective-permute-start = (bf16[8,32,1152]{2,1,0:T(8,128)(2,1)S(1)}, bf16[8,32,1152]{2,1,0:T(8,128)(2,1)S(1)}, u32[]{:S(2)}, u32[]{:S(2)}) collective-permute-start(bf16[8,32,1152]{2,1,0:T(8,128)(2,1)S(1)} %all_to_all.25.mine_ref), channel_id=1, source_target_pairs={{0,1},{1,0},{2,3},{3,2},{4,5},{5,4},{6,7},{7,6},{8,9},{9,8},{10,11... | collective-permute-start | bytes 1769480 | tf_op jit(solution)/shard_map/ppermute | solution.py:379
  30.2 4.6 %collective-permute-start.4 = (bf16[64,512]{1,0:T(8,128)(2,1)}, bf16[64,512]{1,0:T(8,128)(2,1)S(1)}, u32[]{:S(2)}, u32[]{:S(2)}) collective-permute-start(bf16[64,512]{1,0:T(8,128)(2,1)} %get-tuple-element.48), channel_id=1, source_target_pairs={{0,4},{1,5},{2,6},{3,7},{4,0},{5,1},{6,2},{7,3},{8,12},{9,13},{10,... | collective-permute-start | bytes 196616 | tf_op jit(solution)/shard_map/ppermute | solution.py:379
  30.9 6.7 %collective-permute-start.5 = (bf16[64,512]{1,0:T(8,128)(2,1)}, bf16[64,512]{1,0:T(8,128)(2,1)S(1)}, u32[]{:S(2)}, u32[]{:S(2)}) collective-permute-start(bf16[64,512]{1,0:T(8,128)(2,1)} %get-tuple-element.49), channel_id=1, source_target_pairs={{0,8},{1,9},{2,10},{3,11},{4,12},{5,13},{6,14},{7,15},{8,0},{9,1},... | collective-permute-start | bytes 196616 | tf_op jit(solution)/shard_map/ppermute | solution.py:379
  32.2 11.7 %collective-permute-start.1 = (bf16[128,320]{1,0:T(8,128)(2,1)}, bf16[128,320]{1,0:T(8,128)(2,1)S(1)}, u32[]{:S(2)}, u32[]{:S(2)}) collective-permute-start(bf16[128,320]{1,0:T(8,128)(2,1)} %get-tuple-element.44), channel_id=1, source_target_pairs={{0,1},{1,0},{2,3},{3,2},{4,5},{5,4},{6,7},{7,6},{8,9},{9,8},{10,11... | collective-permute-start | bytes 245768 | tf_op jit(solution)/shard_map/ppermute | solution.py:379
  32.2 11.7 %collective-permute-start.2 = (bf16[128,320]{1,0:T(8,128)(2,1)}, bf16[128,320]{1,0:T(8,128)(2,1)S(1)}, u32[]{:S(2)}, u32[]{:S(2)}) collective-permute-start(bf16[128,320]{1,0:T(8,128)(2,1)} %get-tuple-element.45), channel_id=1, source_target_pairs={{0,2},{1,3},{2,0},{3,1},{4,6},{5,7},{6,4},{7,5},{8,10},{9,11},{10,... | collective-permute-start | bytes 245768 | tf_op jit(solution)/shard_map/ppermute | solution.py:379
  34.8 9.1 %copy-start.12 = (bf16[64,512]{1,0:T(8,128)(2,1)}, bf16[64,512]{1,0:T(8,128)(2,1)S(1)}, u32[]{:S(2)}) copy-start(bf16[64,512]{1,0:T(8,128)(2,1)S(1)} %collective-permute-done.4.refs_5_) | copy-start | bytes 196612
  34.8 9.1 %collective-permute-start.3 = (bf16[128,320]{1,0:T(8,128)(2,1)}, bf16[128,320]{1,0:T(8,128)(2,1)S(1)}, u32[]{:S(2)}, u32[]{:S(2)}) collective-permute-start(bf16[128,320]{1,0:T(8,128)(2,1)} %get-tuple-element.46), channel_id=1, source_target_pairs={{0,3},{1,2},{2,1},{3,0},{4,7},{5,6},{6,5},{7,4},{8,11},{9,10},{10,... | collective-permute-start | bytes 245768 | tf_op jit(solution)/shard_map/ppermute | solution.py:379
  37.6 6.3 %copy-start.13 = (bf16[64,512]{1,0:T(8,128)(2,1)}, bf16[64,512]{1,0:T(8,128)(2,1)S(1)}, u32[]{:S(2)}) copy-start(bf16[64,512]{1,0:T(8,128)(2,1)S(1)} %collective-permute-done.5.refs_6_) | copy-start | bytes 196612
  37.6 6.3 %collective-permute-start.6 = (bf16[64,512]{1,0:T(8,128)(2,1)}, bf16[64,512]{1,0:T(8,128)(2,1)S(1)}, u32[]{:S(2)}, u32[]{:S(2)}) collective-permute-start(bf16[64,512]{1,0:T(8,128)(2,1)} %get-tuple-element.50), channel_id=1, source_target_pairs={{0,12},{1,13},{2,14},{3,15},{4,8},{5,9},{6,10},{7,11},{8,4},{9,5},... | collective-permute-start | bytes 196616 | tf_op jit(solution)/shard_map/ppermute | solution.py:379
  47.6 49.4 %copy-start.6 = (bf16[4,4,64,128]{3,2,1,0:T(8,128)(2,1)S(1)}, bf16[4,4,64,128]{3,2,1,0:T(8,128)(2,1)}, u32[]{:S(2)}) copy-start(bf16[4,4,64,128]{3,2,1,0:T(8,128)(2,1)} %get-tuple-element.56) | copy-start | bytes 786436
  85.4 20.5 %copy-start = (bf16[8,160,128]{2,1,0:T(8,128)(2,1)}, bf16[8,160,128]{2,1,0:T(8,128)(2,1)S(1)}, u32[]{:S(2)}) copy-start(bf16[8,160,128]{2,1,0:T(8,128)(2,1)S(1)} %all_to_all.27.refs_0_) | copy-start | bytes 983044
  85.4 11.6 %all-to-all-start.3 = ((bf16[8,128,128]{2,1,0:T(8,128)(2,1)}), bf16[8,128,128]{2,1,0:T(8,128)(2,1)S(1)}, u32[]{:S(2)}, u32[]{:S(2)}) async-start(bf16[8,128,128]{2,1,0:T(8,128)(2,1)} %get-tuple-element.55), calls=%async_computation.3 | async-start | bytes 524288 | tf_op jit(solution)/shard_map/all_to_all | solution.py:375
  88.8 17.0 %collective-permute-start.7 = (bf16[8,160,128]{2,1,0:T(8,128)(2,1)S(1)}, bf16[8,160,128]{2,1,0:T(8,128)(2,1)S(1)}, u32[]{:S(2)}, u32[]{:S(2)}) collective-permute-start(bf16[8,160,128]{2,1,0:T(8,128)(2,1)S(1)} %all_to_all.27.refs_0_), channel_id=1, source_target_pairs={{0,1},{1,0},{2,3},{3,2},{4,5},{5,4},{6,7},{7,6},{8,9},{9,8},{10,11... | collective-permute-start | bytes 983048 | tf_op jit(solution)/shard_map/ppermute | solution.py:379
  97.0 14.6 %copy-start.4 = (bf16[8,128,128]{2,1,0:T(8,128)(2,1)}, bf16[8,128,128]{2,1,0:T(8,128)(2,1)S(1)}, u32[]{:S(2)}) copy-start(bf16[8,128,128]{2,1,0:T(8,128)(2,1)S(1)} %all-to-all-done.3.refs_2_) | copy-start | bytes 786436
  97.0 14.6 %collective-permute-start.8 = (bf16[8,128,128]{2,1,0:T(8,128)(2,1)S(1)}, bf16[8,128,128]{2,1,0:T(8,128)(2,1)S(1)}, u32[]{:S(2)}, u32[]{:S(2)}) collective-permute-start(bf16[8,128,128]{2,1,0:T(8,128)(2,1)S(1)} %all-to-all-done.3.refs_2_), channel_id=1, source_target_pairs={{0,1},{1,0},{2,3},{3,2},{4,5},{5,4},{6,7},{7,6},{8,9},{9,8},{10,11... | collective-permute-start | bytes 786440 | tf_op jit(solution)/shard_map/ppermute | solution.py:379
  97.7 3.8 %collective-permute-start.11 = (bf16[4,64,128]{2,1,0:T(8,128)(2,1)S(1)}, bf16[4,64,128]{2,1,0:T(8,128)(2,1)S(1)}, u32[]{:S(2)}, u32[]{:S(2)}) collective-permute-start(bf16[4,64,128]{2,1,0:T(8,128)(2,1)S(1)} %get-tuple-element.72), channel_id=1, source_target_pairs={{0,3},{1,2},{2,1},{3,0},{4,7},{5,6},{6,5},{7,4},{8,11},{9,10},{10,... | collective-permute-start | bytes 196616 | tf_op jit(solution)/shard_map/ppermute | solution.py:379
  99.0 4.5 %collective-permute-start.10 = (bf16[4,64,128]{2,1,0:T(8,128)(2,1)S(1)}, bf16[4,64,128]{2,1,0:T(8,128)(2,1)S(1)}, u32[]{:S(2)}, u32[]{:S(2)}) collective-permute-start(bf16[4,64,128]{2,1,0:T(8,128)(2,1)S(1)} %get-tuple-element.73), channel_id=1, source_target_pairs={{0,2},{1,3},{2,0},{3,1},{4,6},{5,7},{6,4},{7,5},{8,10},{9,11},{10,... | collective-permute-start | bytes 196616 | tf_op jit(solution)/shard_map/ppermute | solution.py:379
  99.8 3.7 %collective-permute-start.9 = (bf16[4,64,128]{2,1,0:T(8,128)(2,1)S(1)}, bf16[4,64,128]{2,1,0:T(8,128)(2,1)S(1)}, u32[]{:S(2)}, u32[]{:S(2)}) collective-permute-start(bf16[4,64,128]{2,1,0:T(8,128)(2,1)S(1)} %get-tuple-element.74), channel_id=1, source_target_pairs={{0,1},{1,0},{2,3},{3,2},{4,5},{5,4},{6,7},{7,6},{8,9},{9,8},{10,11... | collective-permute-start | bytes 196616 | tf_op jit(solution)/shard_map/ppermute | solution.py:379
  101.5 2.0 %copy-start.15 = (bf16[4,64,128]{2,1,0:T(8,128)(2,1)}, bf16[4,64,128]{2,1,0:T(8,128)(2,1)S(1)}, u32[]{:S(2)}) copy-start(bf16[4,64,128]{2,1,0:T(8,128)(2,1)S(1)} %collective-permute-done.11.refs_3_) | copy-start | bytes 196612
  112.3 9.8 %copy-start.19 = (f32[8,256]{1,0:T(8,128)S(1)}, f32[8,256]{1,0:T(8,128)}, u32[]{:S(2)}) copy-start(f32[8,256]{1,0:T(8,128)} %get-tuple-element.67) | copy-start | bytes 24580
  118.5 23.0 %all-to-all-start.4 = ((bf16[16,32,256]{2,1,0:T(8,128)(2,1)}), bf16[16,32,256]{2,1,0:T(8,128)(2,1)S(1)}, u32[]{:S(2)}, u32[]{:S(2)}) async-start(bf16[16,32,256]{2,1,0:T(8,128)(2,1)} %get-tuple-element.64), calls=%async_computation.4 | async-start | bytes 524288 | tf_op jit(solution)/shard_map/all_to_all | solution.py:375
  122.0 3.5 %collective-permute-start.14 = (f32[8,256]{1,0:T(8,128)S(1)}, f32[8,256]{1,0:T(8,128)S(1)}, u32[]{:S(2)}, u32[]{:S(2)}) collective-permute-start(f32[8,256]{1,0:T(8,128)S(1)} %copy-done.19), channel_id=1, source_target_pairs={{0,3},{1,2},{2,1},{3,0},{4,7},{5,6},{6,5},{7,4},{8,11},{9,10},{10,... | collective-permute-start | bytes 24584 | tf_op jit(solution)/shard_map/ppermute | solution.py:379
  123.6 3.7 %collective-permute-start.13 = (f32[8,256]{1,0:T(8,128)S(1)}, f32[8,256]{1,0:T(8,128)S(1)}, u32[]{:S(2)}, u32[]{:S(2)}) collective-permute-start(f32[8,256]{1,0:T(8,128)S(1)} %copy-done.19), channel_id=1, source_target_pairs={{0,2},{1,3},{2,0},{3,1},{4,6},{5,7},{6,4},{7,5},{8,10},{9,11},{10,... | collective-permute-start | bytes 24584 | tf_op jit(solution)/shard_map/ppermute | solution.py:379
  124.0 3.3 %collective-permute-start.12 = (f32[8,256]{1,0:T(8,128)S(1)}, f32[8,256]{1,0:T(8,128)S(1)}, u32[]{:S(2)}, u32[]{:S(2)}) collective-permute-start(f32[8,256]{1,0:T(8,128)S(1)} %copy-done.19), channel_id=1, source_target_pairs={{0,1},{1,0},{2,3},{3,2},{4,5},{5,4},{6,7},{7,6},{8,9},{9,8},{10,11... | collective-permute-start | bytes 24584 | tf_op jit(solution)/shard_map/ppermute | solution.py:379
  124.0 15.1 %collective-permute-start.19 = (f32[128,256]{1,0:T(8,128)}, f32[128,256]{1,0:T(8,128)S(1)}, u32[]{:S(2)}, u32[]{:S(2)}) collective-permute-start(f32[128,256]{1,0:T(8,128)} %get-tuple-element.70.a_ref), channel_id=1, source_target_pairs={{0,16},{16,0},{1,17},{17,1},{2,18},{18,2},{3,19},{19,3},{4,20},{20... | collective-permute-start | bytes 393224 | tf_op jit(solution)/shard_map/ppermute | solution.py:535
  127.3 8.1 %copy-start.18 = (f32[8,256]{1,0:T(8,128)}, f32[8,256]{1,0:T(8,128)S(1)}, u32[]{:S(2)}) copy-start(f32[8,256]{1,0:T(8,128)S(1)} %add_add_fusion.refs_0_) | copy-start | bytes 24580
  127.3 5.5 %collective-permute-start.17 = (f32[8,256]{1,0:T(8,128)S(1)}, f32[8,256]{1,0:T(8,128)S(1)}, u32[]{:S(2)}, u32[]{:S(2)}) collective-permute-start(f32[8,256]{1,0:T(8,128)S(1)} %add_add_fusion.refs_0_), channel_id=1, source_target_pairs={{0,12},{1,13},{2,14},{3,15},{4,8},{5,9},{6,10},{7,11},{8,4},{9,5},... | collective-permute-start | bytes 24584 | tf_op jit(solution)/shard_map/ppermute | solution.py:379
  130.8 4.5 %collective-permute-start.16 = (f32[8,256]{1,0:T(8,128)S(1)}, f32[8,256]{1,0:T(8,128)S(1)}, u32[]{:S(2)}, u32[]{:S(2)}) collective-permute-start(f32[8,256]{1,0:T(8,128)S(1)} %add_add_fusion.refs_0_), channel_id=1, source_target_pairs={{0,8},{1,9},{2,10},{3,11},{4,12},{5,13},{6,14},{7,15},{8,0},{9,1},... | collective-permute-start | bytes 24584 | tf_op jit(solution)/shard_map/ppermute | solution.py:379
  130.8 4.6 %collective-permute-start.15 = (f32[8,256]{1,0:T(8,128)S(1)}, f32[8,256]{1,0:T(8,128)S(1)}, u32[]{:S(2)}, u32[]{:S(2)}) collective-permute-start(f32[8,256]{1,0:T(8,128)S(1)} %add_add_fusion.refs_0_), channel_id=1, source_target_pairs={{0,4},{1,5},{2,6},{3,7},{4,0},{5,1},{6,2},{7,3},{8,12},{9,13},{10,... | collective-permute-start | bytes 24584 | tf_op jit(solution)/shard_map/ppermute | solution.py:379
  132.8 2.6 %copy-start.20 = (f32[8,256]{1,0:T(8,128)}, f32[8,256]{1,0:T(8,128)S(1)}, u32[]{:S(2)}) copy-start(f32[8,256]{1,0:T(8,128)S(1)} %collective-permute-done.17.refs_3_) | copy-start | bytes 24580
  137.6 3.8 %collective-permute-start.18 = (f32[8,128]{1,0:T(8,128)}, f32[8,128]{1,0:T(8,128)S(1)}, u32[]{:S(2)}, u32[]{:S(2)}) collective-permute-start(f32[8,128]{1,0:T(8,128)} %shard_map.119.part_ref), channel_id=1, source_target_pairs={{0,16},{16,0},{1,17},{17,1},{2,18},{18,2},{3,19},{19,3},{4,20},{20... | collective-permute-start | bytes 12296 | tf_op jit(solution)/shard_map/ppermute | solution.py:537
  (14 other events, 9.4 us)

commit v4 on v3

--- a/solution.py
+++ b/solution.py
@@ -16,6 +16,7 @@
 KV_WIDTH = 2 * KEY_VALUE_HEADS * HEAD_SIZE
 Q_WIDTH = QUERY_HEADS * HEAD_SIZE
 EPSILON = 1e-05
+
 PLANE = 4
 LANES = 128
 LINES = ("zz", "yy")
@@ -143,9 +144,10 @@
 
 def heads_kernel(at_ref, mine_ref, other_ref, wqkv_ref, wout_ref, gain_ref, *refs, rows, cpd, kpd, packed):
     core = at_ref[3]
-    outs, got_ref = refs[:-1], refs[-1]
-    part_ref, place_ref, gate_ref, normed_ref, x_ref, cot_ref = outs[:6]
-    lines = part_ref.shape[0]
+    parts = wout_ref.shape[0] if packed else 1
+    part_refs, outs, got_ref = refs[:parts], refs[parts:-1], refs[-1]
+    place_ref, gate_ref, normed_ref, x_ref, cot_ref = outs[:5]
+    lines = wout_ref.shape[0]
     load_both(core, mine_ref, other_ref, got_ref)
     n, per, width = got_ref.shape
     slots = n * per
@@ -188,18 +190,16 @@
         kv_part = kv[k * kpd : (k + 1) * kpd]
         g_part = grad_heads[:, k * cpd : (k + 1) * cpd]
         if packed:
-            part_ref[k, :top] = beside(q_part)
-            part_ref[k, top : top + kpd] = kv_part[:, :top]
-            part_ref[k, top + kpd : top + 2 * kpd] = kv_part[:, top:]
-            part_ref[k, top + 2 * kpd :] = beside(g_part)
+            halves = [kv_part[:, :top], kv_part[:, top:]]
+            put(part_refs, at_ref[0] ^ k, jnp.concatenate([beside(q_part)] + halves + [beside(g_part)], axis=0))
         else:
-            part_ref[k, :, :cpd] = q_part
-            outs[6][k] = kv_part
-            part_ref[k, :, cpd:] = g_part
-
-
-def sum_kernel(part_ref, q_ref, g_ref):
-    total = sum(part_ref[k] for k in range(part_ref.shape[0])).astype(BF16)
+            part_refs[0][k] = jnp.concatenate([q_part, g_part], axis=1)
+            outs[5][k] = kv_part
+
+
+def sum_kernel(*refs):
+    q_ref, g_ref = refs[-2:]
+    total = sum(ref[...] for ref in refs[:-2]).astype(BF16)
     lead = q_ref.shape[1]
     for i in range(q_ref.shape[0]):
         q_ref[i] = total[:lead]
@@ -443,16 +443,15 @@
     mine = exchange(send, LINES)
     other = swap(mine, n, 1)
 
-    part = (lines, top + 2 * kpd + top, 2 * cpd) if packed else (lines, rows, 2 * cpd)
-    outs = [
-        shaped(part, F32),
+    parts = [(top + 2 * kpd + top, 2 * cpd)] * lines if packed else [(lines, rows, 2 * cpd)]
+    outs = [shaped(part, F32) for part in parts] + [
         shaped((n * slots, rows), BF16),
         shaped((8, rows), F32),
     ]
     outs += [shaped((rows, fb), BF16)] * 3
     if not packed:
         outs += [shaped((lines, kpd, rows), F32)]
-    part, place, gate_rows, normed, own_x, own_cot, *kv_part = call(
+    out = call(
         functools.partial(heads_kernel, rows=rows, cpd=cpd, kpd=kpd, packed=packed),
         tuple(outs),
         mine,
@@ -463,13 +462,14 @@
         scalars=(where,),
         scratch=(pltpu.VMEM((n, slots, 2 * PLANE * fb + LANES), BF16),),
     )
+    parts, (place, gate_rows, normed, own_x, own_cot, *kv_part) = out[: len(parts)], out[len(parts) :]
     cols = [cols[0]] + [swap(cols[r], n, r) for r in range(1, PLANE)]
     cols = call(columns_kernel, shaped((n, cpd, fb), BF16), *cols, scalars=(where,))
-    part = exchange(part, "zz")
     if packed:
+        parts = [parts[0]] + [swap(parts[k], n, PLANE * k) for k in range(1, lines)]
         lead = top + 2 * kpd
         q_pack, g_pack = call(
-            sum_kernel, (shaped((2 * lines, lead, 2 * cpd), BF16), shaped((2 * lines, top, 2 * cpd), BF16)), part
+            sum_kernel, (shaped((2 * lines, lead, 2 * cpd), BF16), shaped((2 * lines, top, 2 * cpd), BF16)), *parts
         )
         q_refs = exchange(q_pack, LINES)
         q_refs = (q_refs, swap(q_refs, n, 1))
@@ -478,7 +478,7 @@
         kv_refs = ()
     else:
         per = HEAD_SIZE // cpd
-        everything = jnp.sum(part, axis=0).astype(BF16)
+        everything = jnp.sum(exchange(parts[0], "zz"), axis=0).astype(BF16)
         everything = lax.all_gather(everything, SEQ, axis=0).reshape(QUERY_HEADS, per, 2, top, 2, cpd)
         everything = everything.transpose(4, 0, 3, 2, 1, 5).reshape(2, QUERY_HEADS, top, 2 * HEAD_SIZE)
         q_refs, g_refs = (everything[0],), (everything[1],)

time: 146 us -> 142 us (0.973)
  blocking collectives: 55.4 us -> 36.9 us
  waiting for transfers between devices: 26.5 us -> 35.2 us
  starting transfers between devices: 22.9 us -> 27.3 us
    all_to_all x3 -> x2, blocking collectives: 55.4 us -> 36.9 us  [exchange(): return lax.all_to_all(x, axes, 0, 0, tiled=True)]
    ppermute x18 -> x21, waiting for transfers between devices: 18.4 us -> 27.1 us  [swap(): return lax.ppermute(x, SEQ, [(i, i ^ bit) for i in range(n)])]
    ppermute x18 -> x21, starting transfers between devices: 13 us -> 17.3 us  [swap(): return lax.ppermute(x, SEQ, [(i, i ^ bit) for i in range(n)])]
    unnamed x48 -> x54, local copies, waits for them, and re-layouts: 5.55 us -> 6.29 us
  transfers between devices with their start and end apart: 22 -> 25, of which waited for: 9 -> 11; matrix products, arithmetic and copies ran while one was open for 1% -> 1% of each run, Pallas kernels for 10% -> 10%
where the time goes in v4:
time: 142 us; the launch traced here: 141 us
  blocking collectives  36.9 us (26%)
  waiting for transfers between devices  35.2 us (25%)
  Pallas kernels  32.9 us (23%)
  starting transfers between devices  27.3 us (19%)
  local copies, waits for them, and re-layouts  7.02 us (5%)
    all_to_all x2, blocking collectives, exchange(): return lax.all_to_all(x, axes, 0, 0, tiled=True)  36.9 us
    pallas_call x11, Pallas kernels, call(): pl.pallas_call(body, out_shape=out_shape, in_specs=[smem] * len(scalars)...  32.9 us
    ppermute x21, waiting for transfers between devices, swap(): return lax.ppermute(x, SEQ, [(i, i ^ bit) for i in range(n)])  27.1 us
    ppermute x21, starting transfers between devices, swap(): return lax.ppermute(x, SEQ, [(i, i ^ bit) for i in range(n)])  17.3 us
    all_to_all x2, waiting for transfers between devices, exchange(): return lax.all_to_all(x, axes, 0, 0, tiled=True)  8.08 us
    all_to_all x2, starting transfers between devices, exchange(): return lax.all_to_all(x, axes, 0, 0, tiled=True)  6.94 us
    unnamed x54, local copies, waits for them, and re-layouts  6.29 us
  transfers between devices with their start and end apart: 25, of which 11 were waited for; matrix products, arithmetic and copies ran while one was open for 1% of the time, Pallas kernels for 10%

profile of v4, /device:TPU:0, one launch (start us, length us, event | category | flops | bytes accessed | tf_op | source)
XLA Modules:
  0.0 140.8 jit_solution(17497825070668689587)
XLA Ops:
  0.6 2.5 %shard_map.111 = (bf16[8,32,1152]{2,1,0:T(8,128)(2,1)}, bf16[32,2048]{1,0:T(8,128)(2,1)}, bf16[32,2048]{1,0:T(8,128)(2,1)}, f32[32,1]{1,0:T(8,128)}, f32[32,1]{1,0:T(8,128)}) custom-call(bf16[128,2048]{1,0:T(8,128)(2,1)} %bitcast.20, bf16[128,2048]{1,0:T(8,128)(2,1)} %bitcast.22, s32[1,128]{1,0:T(1,128)} %picks_ref.3, f32[1,2048]{1,0:T(1,128)} %bitcast.26), custom_call_target="tpu_custom_call" | custom-call | tf_op jit(solution)/shard_map/pallas_call | solution.py:46
  3.1 23.8 %all_to_all.20.mine_ref = bf16[8,32,1152]{2,1,0:T(8,128)(2,1)S(1)} all-to-all(bf16[8,32,1152]{2,1,0:T(8,128)(2,1)} %get-tuple-element.45), channel_id=1, replica_groups=mesh['dp'=2,'zz'=4,'yy'=2,'cc'=2] {'zz','yy'}, dimensions={0} | all-to-all | bytes 1179648 | tf_op jit(solution)/shard_map/all_to_all | solution.py:375
  27.7 2.5 %shard_map.112 = (bf16[128,320]{1,0:T(8,128)(2,1)}, bf16[128,320]{1,0:T(8,128)(2,1)}, bf16[128,320]{1,0:T(8,128)(2,1)}, bf16[128,320]{1,0:T(8,128)(2,1)}, bf16[6...) custom-call(s32[4]{0:T(128)} %pad_add_fusion.at_ref, ...), custom_call_target="tpu_custom_call" | custom-call | tf_op jit(solution)/shard_map/pallas_call | solution.py:46
  33.0 1.8 %collective-permute-done.4.refs_5_ = bf16[64,512]{1,0:T(8,128)(2,1)S(1)} collective-permute-done((bf16[64,512]{1,0:T(8,128)(2,1)}, bf16[64,512]{1,0:T(8,128)(2,1)S(1)}, u32[]{:S(2)}, u32[]{:S(2)}) %collective-permute-start.4) | collective-permute-done | bytes 65568 | tf_op jit(solution)/shard_map/ppermute | solution.py:379
  34.8 2.8 %collective-permute-done.5.refs_6_ = bf16[64,512]{1,0:T(8,128)(2,1)S(1)} collective-permute-done((bf16[64,512]{1,0:T(8,128)(2,1)}, bf16[64,512]{1,0:T(8,128)(2,1)S(1)}, u32[]{:S(2)}, u32[]{:S(2)}) %collective-permute-start.5) | collective-permute-done | bytes 65568 | tf_op jit(solution)/shard_map/ppermute | solution.py:379
  37.6 1.5 %collective-permute-start.6 = (bf16[64,512]{1,0:T(8,128)(2,1)}, bf16[64,512]{1,0:T(8,128)(2,1)S(1)}, u32[]{:S(2)}, u32[]{:S(2)}) collective-permute-start(bf16[64,512]{1,0:T(8,128)(2,1)} %get-tuple-element.53), channel_id=1, source_target_pairs={{0,12},{1,13},{2,14},{3,15},{4,8},{5,9},{6,10},{7,11},{8,4},{9,5},... | collective-permute-start | bytes 196616 | tf_op jit(solution)/shard_map/ppermute | solution.py:379
  39.1 4.8 %collective-permute-done.6.refs_7_ = bf16[64,512]{1,0:T(8,128)(2,1)S(1)} collective-permute-done((bf16[64,512]{1,0:T(8,128)(2,1)}, bf16[64,512]{1,0:T(8,128)(2,1)S(1)}, u32[]{:S(2)}, u32[]{:S(2)}) %collective-permute-start.6) | collective-permute-done | bytes 65568 | tf_op jit(solution)/shard_map/ppermute | solution.py:379
  44.6 2.1 %shard_map.113 = (bf16[4,128,320]{2,1,0:T(8,128)(2,1)}, bf16[4,64,512]{2,1,0:T(8,128)(2,1)}, bf16[4,4,64,128]{3,2,1,0:T(8,128)(2,1)}) custom-call(s32[4]{0:T(128)} %pad_add_fusion.at_ref, bf16[128,320]{1,0:T(8,128)(2,1)} %get-tuple-element.46.refs_0_, bf16[128,320]{1,0:T(8,128)(2,1)} %copy-done.12, bf16[128,320]{1,0:T(8,128)(2,1)} %copy-done.13, ...), custom_call_target="tpu_custom_call" | custom-call | tf_op jit(solution)/shard_map/pallas_call | solution.py:46
  47.6 4.8 %shard_map.114 = (f32[288,128]{1,0:T(8,128)}, f32[288,128]{1,0:T(8,128)}, f32[288,128]{1,0:T(8,128)}, f32[288,128]{1,0:T(8,128)}, bf16[512,256]{1,0:T(8,128)(2,1...) custom-call(s32[4]{0:T(128)} %pad_add_fusion.at_ref, ...), custom_call_target="tpu_custom_call" | custom-call | tf_op jit(solution)/shard_map/pallas_call | solution.py:46
  52.3 2.1 %collective-permute-start.8 = (f32[288,128]{1,0:T(8,128)}, f32[288,128]{1,0:T(8,128)S(1)}, u32[]{:S(2)}, u32[]{:S(2)}) collective-permute-start(f32[288,128]{1,0:T(8,128)} %get-tuple-element.58), channel_id=1, source_target_pairs={{0,8},{1,9},{2,10},{3,11},{4,12},{5,13},{6,14},{7,15},{8,0},{9,1},... | collective-permute-start | bytes 442376 | tf_op jit(solution)/shard_map/ppermute | solution.py:379
  54.4 2.3 %collective-permute-start.9 = (f32[288,128]{1,0:T(8,128)}, f32[288,128]{1,0:T(8,128)S(1)}, u32[]{:S(2)}, u32[]{:S(2)}) collective-permute-start(f32[288,128]{1,0:T(8,128)} %get-tuple-element.59), channel_id=1, source_target_pairs={{0,12},{1,13},{2,14},{3,15},{4,8},{5,9},{6,10},{7,11},{8,4},{9,5},... | collective-permute-start | bytes 442376 | tf_op jit(solution)/shard_map/ppermute | solution.py:379
  56.7 1.6 %collective-permute-done.7.refs_1_ = f32[288,128]{1,0:T(8,128)S(1)} collective-permute-done((f32[288,128]{1,0:T(8,128)}, f32[288,128]{1,0:T(8,128)S(1)}, u32[]{:S(2)}, u32[]{:S(2)}) %collective-permute-start.7) | collective-permute-done | bytes 147488 | tf_op jit(solution)/shard_map/ppermute | solution.py:379
  58.3 7.0 %collective-permute-done.8.refs_2_ = f32[288,128]{1,0:T(8,128)S(1)} collective-permute-done((f32[288,128]{1,0:T(8,128)}, f32[288,128]{1,0:T(8,128)S(1)}, u32[]{:S(2)}, u32[]{:S(2)}) %collective-permute-start.8) | collective-permute-done | bytes 147488 | tf_op jit(solution)/shard_map/ppermute | solution.py:379
  66.1 2.0 %shard_map.115 = (bf16[8,160,128]{2,1,0:T(8,128)(2,1)}, bf16[8,128,128]{2,1,0:T(8,128)(2,1)}) custom-call(f32[288,128]{1,0:T(8,128)} %get-tuple-element.56.refs_0_, f32[288,128]{1,0:T(8,128)} %copy-done.8, f32[288,128]{1,0:T(8,128)} %copy-done.9, f32[288,128]{1,0:T(8,128)} %copy-done.10), custom_call_target="tpu_custom_call" | custom-call | tf_op jit(solution)/shard_map/pallas_call | solution.py:46
  68.0 13.1 %all_to_all.21.refs_0_ = bf16[8,160,128]{2,1,0:T(8,128)(2,1)S(1)} all-to-all(bf16[8,160,128]{2,1,0:T(8,128)(2,1)} %get-tuple-element.60), channel_id=1, replica_groups=mesh['dp'=2,'zz'=4,'yy'=2,'cc'=2] {'zz','yy'}, dimensions={0} | all-to-all | bytes 655360 | tf_op jit(solution)/shard_map/all_to_all | solution.py:375
  81.1 3.4 %all-to-all-start.2 = ((bf16[8,128,128]{2,1,0:T(8,128)(2,1)}), bf16[8,128,128]{2,1,0:T(8,128)(2,1)S(1)}, u32[]{:S(2)}, u32[]{:S(2)}) async-start(bf16[8,128,128]{2,1,0:T(8,128)(2,1)} %get-tuple-element.61), calls=%async_computation.2 | async-start | bytes 524288 | tf_op jit(solution)/shard_map/all_to_all | solution.py:375
  84.6 8.1 %all-to-all-done.2.refs_2_ = bf16[8,128,128]{2,1,0:T(8,128)(2,1)S(1)} async-done(((bf16[8,128,128]{2,1,0:T(8,128)(2,1)}), bf16[8,128,128]{2,1,0:T(8,128)(2,1)S(1)}, u32[]{:S(2)}, u32[]{:S(2)}) %all-to-all-start.2) | async-done | bytes 262176 | tf_op jit(solution)/shard_map/all_to_all | solution.py:375
  95.5 1.7 %collective-permute-done.14.refs_3_ = bf16[4,64,128]{2,1,0:T(8,128)(2,1)S(1)} collective-permute-done((bf16[4,64,128]{2,1,0:T(8,128)(2,1)S(1)}, bf16[4,64,128]{2,1,0:T(8,128)(2,1)S(1)}, u32[]{:S(2)}, u32[]{:S(2)}) %collective-permute-start.14) | collective-permute-done | bytes 65568 | tf_op jit(solution)/shard_map/ppermute | solution.py:379
  97.2 2.0 %collective-permute-done.13.refs_2_ = bf16[4,64,128]{2,1,0:T(8,128)(2,1)S(1)} collective-permute-done((bf16[4,64,128]{2,1,0:T(8,128)(2,1)S(1)}, bf16[4,64,128]{2,1,0:T(8,128)(2,1)S(1)}, u32[]{:S(2)}, u32[]{:S(2)}) %collective-permute-start.13) | collective-permute-done | bytes 65568 | tf_op jit(solution)/shard_map/ppermute | solution.py:379
  99.9 1.7 %shard_map.116.refs_2_ = bf16[16,64,128]{2,1,0:T(8,128)(2,1)} custom-call(s32[4]{0:T(128)} %pad_add_fusion.at_ref, bf16[4,64,128]{2,1,0:T(8,128)(2,1)} %get-tuple-element.81.refs_0_, bf16[4,64,128]{2,1,0:T(8,128)(2,1)} %copy-done.20, bf16[4,64,128]{2,1,0:T(8,128)(2,1)} %copy-done.19, bf16[4,64,128]{2,1,0:T(8,128)(2,1)} %copy-done.18), custom_call_target="tpu_custom_call" | custom-call | tf_op jit(solution)/shard_map/pallas_call | solution.py:46
  102.3 5.0 %shard_map.117 = (bf16[16,32,128]{2,1,0:T(8,128)(2,1)}, bf16[256,256]{1,0:T(8,128)(2,1)}, f32[8,256]{1,0:T(8,128)}, f32[16,128,128]{2,1,0:T(8,128)}, f32[16,128,256]{2,1,0:T(8,128)}) custom-call(s32[4]{0:T(128)} %pad_add_fusion.at_ref, bf16[8,160,128]{2,1,0:T(8,128)(2,1)} %copy-done, bf16[8,160,128]{2,1,0:T(8,128)(2,1)} %copy-done.2, ...), custom_call_target="tpu_custom_call" | custom-call | tf_op jit(solution)/shard_map/pallas_call | solution.py:46
  108.0 6.2 %shard_map.118 = (bf16[16,32,256]{2,1,0:T(8,128)(2,1)}, f32[128,256]{1,0:T(8,128)}) custom-call(s32[4]{0:T(128)} %pad_add_fusion.at_ref, bf16[8,160,128]{2,1,0:T(8,128)(2,1)} %copy-done, bf16[8,160,128]{2,1,0:T(8,128)(2,1)} %copy-done.2, bf16[8,128,128]{2,1,0:T(8,128)(2,1)} %copy-done.4, bf16[8,128,128]{2,1,0:T(8,128)(2,1)} %copy-done.7, ...), custom_call_target="tpu_custom_call" | custom-call | tf_op jit(solution)/shard_map/pallas_call | solution.py:46
  114.2 3.5 %all-to-all-start.3 = ((bf16[16,32,256]{2,1,0:T(8,128)(2,1)}), bf16[16,32,256]{2,1,0:T(8,128)(2,1)S(1)}, u32[]{:S(2)}, u32[]{:S(2)}) async-start(bf16[16,32,256]{2,1,0:T(8,128)(2,1)} %get-tuple-element.70), calls=%async_computation.3 | async-start | bytes 524288 | tf_op jit(solution)/shard_map/all_to_all | solution.py:375
  117.7 1.6 %collective-permute-start.17 = (f32[8,256]{1,0:T(8,128)S(1)}, f32[8,256]{1,0:T(8,128)S(1)}, u32[]{:S(2)}, u32[]{:S(2)}) collective-permute-start(f32[8,256]{1,0:T(8,128)S(1)} %copy-done.22), channel_id=1, source_target_pairs={{0,3},{1,2},{2,1},{3,0},{4,7},{5,6},{6,5},{7,4},{8,11},{9,10},{10,... | collective-permute-start | bytes 24584 | tf_op jit(solution)/shard_map/ppermute | solution.py:379
  119.7 1.5 %collective-permute-start.22 = (f32[128,256]{1,0:T(8,128)}, f32[128,256]{1,0:T(8,128)S(1)}, u32[]{:S(2)}, u32[]{:S(2)}) collective-permute-start(f32[128,256]{1,0:T(8,128)} %get-tuple-element.76.a_ref), channel_id=1, source_target_pairs={{0,16},{16,0},{1,17},{17,1},{2,18},{18,2},{3,19},{19,3},{4,20},{20... | collective-permute-start | bytes 393224 | tf_op jit(solution)/shard_map/ppermute | solution.py:535
  121.2 1.7 %collective-permute-done.16 = f32[8,256]{1,0:T(8,128)S(1)} collective-permute-done((f32[8,256]{1,0:T(8,128)S(1)}, f32[8,256]{1,0:T(8,128)S(1)}, u32[]{:S(2)}, u32[]{:S(2)}) %collective-permute-start.16) | collective-permute-done | bytes 8224 | tf_op jit(solution)/shard_map/ppermute | solution.py:379
  123.0 3.5 %collective-permute-start.20 = (f32[8,256]{1,0:T(8,128)S(1)}, f32[8,256]{1,0:T(8,128)S(1)}, u32[]{:S(2)}, u32[]{:S(2)}) collective-permute-start(f32[8,256]{1,0:T(8,128)S(1)} %add_add_fusion.refs_0_), channel_id=1, source_target_pairs={{0,12},{1,13},{2,14},{3,15},{4,8},{5,9},{6,10},{7,11},{8,4},{9,5},... | collective-permute-start | bytes 24584 | tf_op jit(solution)/shard_map/ppermute | solution.py:379
  128.5 2.6 %collective-permute-done.19.refs_2_ = f32[8,256]{1,0:T(8,128)S(1)} collective-permute-done((f32[8,256]{1,0:T(8,128)S(1)}, f32[8,256]{1,0:T(8,128)S(1)}, u32[]{:S(2)}, u32[]{:S(2)}) %collective-permute-start.19) | collective-permute-done | bytes 8224 | tf_op jit(solution)/shard_map/ppermute | solution.py:379
  131.7 1.7 %shard_map.119.part_ref = f32[8,128]{1,0:T(8,128)} custom-call(bf16[256,128]{1,0:T(8,128)(2,1)} %get-tuple-element.71.x_ref, f32[8,256]{1,0:T(8,128)} %get-tuple-element.72.gate_ref, f32[8,256]{1,0:T(8,128)} %copy-done.21, f32[8,256]{1,0:T(8,128)} %copy-done.25, f32[8,256]{1,0:T(8,128)} %copy-done.24, f32[8,256]{1,0:T(8,128)} %copy-done.23), custom_call_target="tpu_custom_call" | custom-call | tf_op jit(solution)/shard_map/pallas_call | solution.py:46
  133.4 1.5 %collective-permute-start.21 = (f32[8,128]{1,0:T(8,128)}, f32[8,128]{1,0:T(8,128)S(1)}, u32[]{:S(2)}, u32[]{:S(2)}) collective-permute-start(f32[8,128]{1,0:T(8,128)} %shard_map.119.part_ref), channel_id=1, source_target_pairs={{0,16},{16,0},{1,17},{17,1},{2,18},{18,2},{3,19},{19,3},{4,20},{20... | collective-permute-start | bytes 12296 | tf_op jit(solution)/shard_map/ppermute | solution.py:537
  135.5 1.6 %shard_map.121 = f32[128,256]{1,0:T(8,128)} custom-call(f32[128,256]{1,0:T(8,128)} %get-tuple-element.76.a_ref, f32[128,256]{1,0:T(8,128)} %copy-done.11), custom_call_target="tpu_custom_call" | custom-call | tf_op jit(solution)/shard_map/pallas_call | solution.py:46
  137.9 2.9 %shard_map.120 = (bf16[128,2048]{1,0:T(8,128)(2,1)}, bf16[128,2048]{1,0:T(8,128)(2,1)}, f32[1,128]{1,0:T(1,128)}) custom-call(bf16[128,2048]{1,0:T(8,128)(2,1)} %bitcast.21, bf16[128,2048]{1,0:T(8,128)(2,1)} %bitcast.23, s32[1,128]{1,0:T(1,128)} %picks_ref.3, f32[1,2048]{1,0:T(1,128)} %bitcast.27, f32[32,1]{1,0:T(8,128)} %get-tuple-element.41.gate_ref, ...), custom_call_target="tpu_custom_call" | custom-call | tf_op jit(solution)/shard_map/pallas_call | solution.py:46
  (88 shorter events, 15.1 us)
Async XLA Ops:
  27.0 19.8 %copy-start.1 = (bf16[8,32,1152]{2,1,0:T(8,128)(2,1)}, bf16[8,32,1152]{2,1,0:T(8,128)(2,1)S(1)}, u32[]{:S(2)}) copy-start(bf16[8,32,1152]{2,1,0:T(8,128)(2,1)S(1)} %all_to_all.20.mine_ref) | copy-start | bytes 1769476
  27.0 19.8 %collective-permute-start = (bf16[8,32,1152]{2,1,0:T(8,128)(2,1)S(1)}, bf16[8,32,1152]{2,1,0:T(8,128)(2,1)S(1)}, u32[]{:S(2)}, u32[]{:S(2)}) collective-permute-start(bf16[8,32,1152]{2,1,0:T(8,128)(2,1)S(1)} %all_to_all.20.mine_ref), channel_id=1, source_target_pairs={{0,1},{1,0},{2,3},{3,2},{4,5},{5,4},{6,7},{7,6},{8,9},{9,8},{10,11... | collective-permute-start | bytes 1769480 | tf_op jit(solution)/shard_map/ppermute | solution.py:379
  30.2 4.6 %collective-permute-start.4 = (bf16[64,512]{1,0:T(8,128)(2,1)}, bf16[64,512]{1,0:T(8,128)(2,1)S(1)}, u32[]{:S(2)}, u32[]{:S(2)}) collective-permute-start(bf16[64,512]{1,0:T(8,128)(2,1)} %get-tuple-element.51), channel_id=1, source_target_pairs={{0,4},{1,5},{2,6},{3,7},{4,0},{5,1},{6,2},{7,3},{8,12},{9,13},{10,... | collective-permute-start | bytes 196616 | tf_op jit(solution)/shard_map/ppermute | solution.py:379
  30.9 6.7 %collective-permute-start.5 = (bf16[64,512]{1,0:T(8,128)(2,1)}, bf16[64,512]{1,0:T(8,128)(2,1)S(1)}, u32[]{:S(2)}, u32[]{:S(2)}) collective-permute-start(bf16[64,512]{1,0:T(8,128)(2,1)} %get-tuple-element.52), channel_id=1, source_target_pairs={{0,8},{1,9},{2,10},{3,11},{4,12},{5,13},{6,14},{7,15},{8,0},{9,1},... | collective-permute-start | bytes 196616 | tf_op jit(solution)/shard_map/ppermute | solution.py:379
  32.2 11.7 %collective-permute-start.1 = (bf16[128,320]{1,0:T(8,128)(2,1)}, bf16[128,320]{1,0:T(8,128)(2,1)S(1)}, u32[]{:S(2)}, u32[]{:S(2)}) collective-permute-start(bf16[128,320]{1,0:T(8,128)(2,1)} %get-tuple-element.47), channel_id=1, source_target_pairs={{0,1},{1,0},{2,3},{3,2},{4,5},{5,4},{6,7},{7,6},{8,9},{9,8},{10,11... | collective-permute-start | bytes 245768 | tf_op jit(solution)/shard_map/ppermute | solution.py:379
  32.2 11.7 %collective-permute-start.2 = (bf16[128,320]{1,0:T(8,128)(2,1)}, bf16[128,320]{1,0:T(8,128)(2,1)S(1)}, u32[]{:S(2)}, u32[]{:S(2)}) collective-permute-start(bf16[128,320]{1,0:T(8,128)(2,1)} %get-tuple-element.48), channel_id=1, source_target_pairs={{0,2},{1,3},{2,0},{3,1},{4,6},{5,7},{6,4},{7,5},{8,10},{9,11},{10,... | collective-permute-start | bytes 245768 | tf_op jit(solution)/shard_map/ppermute | solution.py:379
  34.8 9.1 %copy-start.15 = (bf16[64,512]{1,0:T(8,128)(2,1)}, bf16[64,512]{1,0:T(8,128)(2,1)S(1)}, u32[]{:S(2)}) copy-start(bf16[64,512]{1,0:T(8,128)(2,1)S(1)} %collective-permute-done.4.refs_5_) | copy-start | bytes 196612
  34.8 9.1 %collective-permute-start.3 = (bf16[128,320]{1,0:T(8,128)(2,1)}, bf16[128,320]{1,0:T(8,128)(2,1)S(1)}, u32[]{:S(2)}, u32[]{:S(2)}) collective-permute-start(bf16[128,320]{1,0:T(8,128)(2,1)} %get-tuple-element.49), channel_id=1, source_target_pairs={{0,3},{1,2},{2,1},{3,0},{4,7},{5,6},{6,5},{7,4},{8,11},{9,10},{10,... | collective-permute-start | bytes 245768 | tf_op jit(solution)/shard_map/ppermute | solution.py:379
  37.6 6.3 %collective-permute-start.6 = (bf16[64,512]{1,0:T(8,128)(2,1)}, bf16[64,512]{1,0:T(8,128)(2,1)S(1)}, u32[]{:S(2)}, u32[]{:S(2)}) collective-permute-start(bf16[64,512]{1,0:T(8,128)(2,1)} %get-tuple-element.53), channel_id=1, source_target_pairs={{0,12},{1,13},{2,14},{3,15},{4,8},{5,9},{6,10},{7,11},{8,4},{9,5},... | collective-permute-start | bytes 196616 | tf_op jit(solution)/shard_map/ppermute | solution.py:379
  46.7 46.0 %copy-start.6 = (bf16[4,4,64,128]{3,2,1,0:T(8,128)(2,1)S(1)}, bf16[4,4,64,128]{3,2,1,0:T(8,128)(2,1)}, u32[]{:S(2)}) copy-start(bf16[4,4,64,128]{3,2,1,0:T(8,128)(2,1)} %get-tuple-element.62) | copy-start | bytes 786436
  52.3 6.0 %collective-permute-start.7 = (f32[288,128]{1,0:T(8,128)}, f32[288,128]{1,0:T(8,128)S(1)}, u32[]{:S(2)}, u32[]{:S(2)}) collective-permute-start(f32[288,128]{1,0:T(8,128)} %get-tuple-element.57), channel_id=1, source_target_pairs={{0,4},{1,5},{2,6},{3,7},{4,0},{5,1},{6,2},{7,3},{8,12},{9,13},{10,... | collective-permute-start | bytes 442376 | tf_op jit(solution)/shard_map/ppermute | solution.py:379
  52.3 13.0 %collective-permute-start.8 = (f32[288,128]{1,0:T(8,128)}, f32[288,128]{1,0:T(8,128)S(1)}, u32[]{:S(2)}, u32[]{:S(2)}) collective-permute-start(f32[288,128]{1,0:T(8,128)} %get-tuple-element.58), channel_id=1, source_target_pairs={{0,8},{1,9},{2,10},{3,11},{4,12},{5,13},{6,14},{7,15},{8,0},{9,1},... | collective-permute-start | bytes 442376 | tf_op jit(solution)/shard_map/ppermute | solution.py:379
  54.4 10.9 %collective-permute-start.9 = (f32[288,128]{1,0:T(8,128)}, f32[288,128]{1,0:T(8,128)S(1)}, u32[]{:S(2)}, u32[]{:S(2)}) collective-permute-start(f32[288,128]{1,0:T(8,128)} %get-tuple-element.59), channel_id=1, source_target_pairs={{0,12},{1,13},{2,14},{3,15},{4,8},{5,9},{6,10},{7,11},{8,4},{9,5},... | collective-permute-start | bytes 442376 | tf_op jit(solution)/shard_map/ppermute | solution.py:379
  81.1 20.5 %copy-start = (bf16[8,160,128]{2,1,0:T(8,128)(2,1)}, bf16[8,160,128]{2,1,0:T(8,128)(2,1)S(1)}, u32[]{:S(2)}) copy-start(bf16[8,160,128]{2,1,0:T(8,128)(2,1)S(1)} %all_to_all.21.refs_0_) | copy-start | bytes 983044
  81.1 11.6 %all-to-all-start.2 = ((bf16[8,128,128]{2,1,0:T(8,128)(2,1)}), bf16[8,128,128]{2,1,0:T(8,128)(2,1)S(1)}, u32[]{:S(2)}, u32[]{:S(2)}) async-start(bf16[8,128,128]{2,1,0:T(8,128)(2,1)} %get-tuple-element.61), calls=%async_computation.2 | async-start | bytes 524288 | tf_op jit(solution)/shard_map/all_to_all | solution.py:375
  84.5 17.0 %collective-permute-start.10 = (bf16[8,160,128]{2,1,0:T(8,128)(2,1)S(1)}, bf16[8,160,128]{2,1,0:T(8,128)(2,1)S(1)}, u32[]{:S(2)}, u32[]{:S(2)}) collective-permute-start(bf16[8,160,128]{2,1,0:T(8,128)(2,1)S(1)} %all_to_all.21.refs_0_), channel_id=1, source_target_pairs={{0,1},{1,0},{2,3},{3,2},{4,5},{5,4},{6,7},{7,6},{8,9},{9,8},{10,11... | collective-permute-start | bytes 983048 | tf_op jit(solution)/shard_map/ppermute | solution.py:379
  92.7 14.6 %copy-start.4 = (bf16[8,128,128]{2,1,0:T(8,128)(2,1)}, bf16[8,128,128]{2,1,0:T(8,128)(2,1)S(1)}, u32[]{:S(2)}) copy-start(bf16[8,128,128]{2,1,0:T(8,128)(2,1)S(1)} %all-to-all-done.2.refs_2_) | copy-start | bytes 786436
  92.7 14.6 %collective-permute-start.11 = (bf16[8,128,128]{2,1,0:T(8,128)(2,1)S(1)}, bf16[8,128,128]{2,1,0:T(8,128)(2,1)S(1)}, u32[]{:S(2)}, u32[]{:S(2)}) collective-permute-start(bf16[8,128,128]{2,1,0:T(8,128)(2,1)S(1)} %all-to-all-done.2.refs_2_), channel_id=1, source_target_pairs={{0,1},{1,0},{2,3},{3,2},{4,5},{5,4},{6,7},{7,6},{8,9},{9,8},{10,11... | collective-permute-start | bytes 786440 | tf_op jit(solution)/shard_map/ppermute | solution.py:379
  93.4 3.8 %collective-permute-start.14 = (bf16[4,64,128]{2,1,0:T(8,128)(2,1)S(1)}, bf16[4,64,128]{2,1,0:T(8,128)(2,1)S(1)}, u32[]{:S(2)}, u32[]{:S(2)}) collective-permute-start(bf16[4,64,128]{2,1,0:T(8,128)(2,1)S(1)} %get-tuple-element.78), channel_id=1, source_target_pairs={{0,3},{1,2},{2,1},{3,0},{4,7},{5,6},{6,5},{7,4},{8,11},{9,10},{10,... | collective-permute-start | bytes 196616 | tf_op jit(solution)/shard_map/ppermute | solution.py:379
  94.7 4.5 %collective-permute-start.13 = (bf16[4,64,128]{2,1,0:T(8,128)(2,1)S(1)}, bf16[4,64,128]{2,1,0:T(8,128)(2,1)S(1)}, u32[]{:S(2)}, u32[]{:S(2)}) collective-permute-start(bf16[4,64,128]{2,1,0:T(8,128)(2,1)S(1)} %get-tuple-element.79), channel_id=1, source_target_pairs={{0,2},{1,3},{2,0},{3,1},{4,6},{5,7},{6,4},{7,5},{8,10},{9,11},{10,... | collective-permute-start | bytes 196616 | tf_op jit(solution)/shard_map/ppermute | solution.py:379
  95.5 3.7 %collective-permute-start.12 = (bf16[4,64,128]{2,1,0:T(8,128)(2,1)S(1)}, bf16[4,64,128]{2,1,0:T(8,128)(2,1)S(1)}, u32[]{:S(2)}, u32[]{:S(2)}) collective-permute-start(bf16[4,64,128]{2,1,0:T(8,128)(2,1)S(1)} %get-tuple-element.80), channel_id=1, source_target_pairs={{0,1},{1,0},{2,3},{3,2},{4,5},{5,4},{6,7},{7,6},{8,9},{9,8},{10,11... | collective-permute-start | bytes 196616 | tf_op jit(solution)/shard_map/ppermute | solution.py:379
  108.0 9.7 %copy-start.22 = (f32[8,256]{1,0:T(8,128)S(1)}, f32[8,256]{1,0:T(8,128)}, u32[]{:S(2)}) copy-start(f32[8,256]{1,0:T(8,128)} %get-tuple-element.73) | copy-start | bytes 24580
  114.2 23.0 %all-to-all-start.3 = ((bf16[16,32,256]{2,1,0:T(8,128)(2,1)}), bf16[16,32,256]{2,1,0:T(8,128)(2,1)S(1)}, u32[]{:S(2)}, u32[]{:S(2)}) async-start(bf16[16,32,256]{2,1,0:T(8,128)(2,1)} %get-tuple-element.70), calls=%async_computation.3 | async-start | bytes 524288 | tf_op jit(solution)/shard_map/all_to_all | solution.py:375
  117.7 3.5 %collective-permute-start.17 = (f32[8,256]{1,0:T(8,128)S(1)}, f32[8,256]{1,0:T(8,128)S(1)}, u32[]{:S(2)}, u32[]{:S(2)}) collective-permute-start(f32[8,256]{1,0:T(8,128)S(1)} %copy-done.22), channel_id=1, source_target_pairs={{0,3},{1,2},{2,1},{3,0},{4,7},{5,6},{6,5},{7,4},{8,11},{9,10},{10,... | collective-permute-start | bytes 24584 | tf_op jit(solution)/shard_map/ppermute | solution.py:379
  119.3 3.7 %collective-permute-start.16 = (f32[8,256]{1,0:T(8,128)S(1)}, f32[8,256]{1,0:T(8,128)S(1)}, u32[]{:S(2)}, u32[]{:S(2)}) collective-permute-start(f32[8,256]{1,0:T(8,128)S(1)} %copy-done.22), channel_id=1, source_target_pairs={{0,2},{1,3},{2,0},{3,1},{4,6},{5,7},{6,4},{7,5},{8,10},{9,11},{10,... | collective-permute-start | bytes 24584 | tf_op jit(solution)/shard_map/ppermute | solution.py:379
  119.7 3.3 %collective-permute-start.15 = (f32[8,256]{1,0:T(8,128)S(1)}, f32[8,256]{1,0:T(8,128)S(1)}, u32[]{:S(2)}, u32[]{:S(2)}) collective-permute-start(f32[8,256]{1,0:T(8,128)S(1)} %copy-done.22), channel_id=1, source_target_pairs={{0,1},{1,0},{2,3},{3,2},{4,5},{5,4},{6,7},{7,6},{8,9},{9,8},{10,11... | collective-permute-start | bytes 24584 | tf_op jit(solution)/shard_map/ppermute | solution.py:379
  119.7 15.1 %collective-permute-start.22 = (f32[128,256]{1,0:T(8,128)}, f32[128,256]{1,0:T(8,128)S(1)}, u32[]{:S(2)}, u32[]{:S(2)}) collective-permute-start(f32[128,256]{1,0:T(8,128)} %get-tuple-element.76.a_ref), channel_id=1, source_target_pairs={{0,16},{16,0},{1,17},{17,1},{2,18},{18,2},{3,19},{19,3},{4,20},{20... | collective-permute-start | bytes 393224 | tf_op jit(solution)/shard_map/ppermute | solution.py:535
  123.0 8.1 %copy-start.21 = (f32[8,256]{1,0:T(8,128)}, f32[8,256]{1,0:T(8,128)S(1)}, u32[]{:S(2)}) copy-start(f32[8,256]{1,0:T(8,128)S(1)} %add_add_fusion.refs_0_) | copy-start | bytes 24580
  123.0 5.5 %collective-permute-start.20 = (f32[8,256]{1,0:T(8,128)S(1)}, f32[8,256]{1,0:T(8,128)S(1)}, u32[]{:S(2)}, u32[]{:S(2)}) collective-permute-start(f32[8,256]{1,0:T(8,128)S(1)} %add_add_fusion.refs_0_), channel_id=1, source_target_pairs={{0,12},{1,13},{2,14},{3,15},{4,8},{5,9},{6,10},{7,11},{8,4},{9,5},... | collective-permute-start | bytes 24584 | tf_op jit(solution)/shard_map/ppermute | solution.py:379
  126.5 4.5 %collective-permute-start.19 = (f32[8,256]{1,0:T(8,128)S(1)}, f32[8,256]{1,0:T(8,128)S(1)}, u32[]{:S(2)}, u32[]{:S(2)}) collective-permute-start(f32[8,256]{1,0:T(8,128)S(1)} %add_add_fusion.refs_0_), channel_id=1, source_target_pairs={{0,8},{1,9},{2,10},{3,11},{4,12},{5,13},{6,14},{7,15},{8,0},{9,1},... | collective-permute-start | bytes 24584 | tf_op jit(solution)/shard_map/ppermute | solution.py:379
  126.5 4.6 %collective-permute-start.18 = (f32[8,256]{1,0:T(8,128)S(1)}, f32[8,256]{1,0:T(8,128)S(1)}, u32[]{:S(2)}, u32[]{:S(2)}) collective-permute-start(f32[8,256]{1,0:T(8,128)S(1)} %add_add_fusion.refs_0_), channel_id=1, source_target_pairs={{0,4},{1,5},{2,6},{3,7},{4,0},{5,1},{6,2},{7,3},{8,12},{9,13},{10,... | collective-permute-start | bytes 24584 | tf_op jit(solution)/shard_map/ppermute | solution.py:379
  133.4 3.8 %collective-permute-start.21 = (f32[8,128]{1,0:T(8,128)}, f32[8,128]{1,0:T(8,128)S(1)}, u32[]{:S(2)}, u32[]{:S(2)}) collective-permute-start(f32[8,128]{1,0:T(8,128)} %shard_map.119.part_ref), channel_id=1, source_target_pairs={{0,16},{16,0},{1,17},{17,1},{2,18},{18,2},{3,19},{19,3},{4,20},{20... | collective-permute-start | bytes 12296 | tf_op jit(solution)/shard_map/ppermute | solution.py:537
  (20 other events, 28.8 us)

commit v5 on v4

--- a/solution.py
+++ b/solution.py
@@ -116,14 +116,17 @@
 
 
 def arrange_kernel(at_ref, *refs):
+    for r in range(PLANE):
+        refs[-1][at_ref[1] ^ r] = refs[r][...]
+
+
+def arrange_out_kernel(at_ref, *refs):
     z, p = at_ref[0], at_ref[1]
-    wqkv_ref, wout_ref, cols_ref = refs[-3:]
+    wout_ref, cols_ref = refs[-2:]
     lines, _, width = wout_ref.shape
     fb = width // PLANE
-    for r in range(PLANE):
-        wqkv_ref[p ^ r] = refs[r][...]
     for k in range(lines):
-        rows = refs[PLANE + k][...]
+        rows = refs[k][...]
         wout_ref[z ^ k] = rows
         for r in range(PLANE):
             cols_ref[p ^ r, z ^ k] = rows[:, r * fb : (r + 1) * fb]
@@ -414,14 +417,10 @@
         to_lines = [to_lines[0][k] for k in range(lines)]
     wqkv = [to_plane[0]] + [swap(to_plane[r], n, r) for r in range(1, PLANE)]
     wout = [to_lines[0]] + [swap(to_lines[k], n, PLANE * k) for k in range(1, lines)]
-    wqkv, wout, cols = call(
-        arrange_kernel,
-        (
-            shaped((PLANE, fb, lines * (cpd + kpd)), BF16),
-            shaped((lines, cpd, PLANE * fb), BF16),
-            shaped((PLANE, lines, cpd, fb), BF16),
-        ),
-        *wqkv,
+    wqkv = call(arrange_kernel, shaped((PLANE, fb, lines * (cpd + kpd)), BF16), *wqkv, scalars=(where,))
+    wout, cols = call(
+        arrange_out_kernel,
+        (shaped((lines, cpd, PLANE * fb), BF16), shaped((PLANE, lines, cpd, fb), BF16)),
         *wout,
         scalars=(where,),
     )

time: 142 us -> 144 us (1.014)
  Pallas kernels: 32.9 us -> 34.4 us
    pallas_call x11 -> x12, Pallas kernels: 32.9 us -> 34.4 us  [call(): pl.pallas_call(body, out_shape=out_shape, in_specs=[smem] * len(scalars)...]
  transfers between devices with their start and end apart: 25 -> 25, of which waited for: 11 -> 11; matrix products, arithmetic and copies ran while one was open for 1% -> 1% of each run, Pallas kernels for 10% -> 11%
where the time goes in v5:
time: 144 us; the launch traced here: 143 us
  blocking collectives  36.9 us (26%)
  waiting for transfers between devices  35.2 us (24%)
  Pallas kernels  34.4 us (24%)
  starting transfers between devices  27.3 us (19%)
  local copies, waits for them, and re-layouts  7.67 us (5%)
    all_to_all x2, blocking collectives, exchange(): return lax.all_to_all(x, axes, 0, 0, tiled=True)  36.9 us
    pallas_call x12, Pallas kernels, call(): pl.pallas_call(body, out_shape=out_shape, in_specs=[smem] * len(scalars)...  34.4 us
    ppermute x21, waiting for transfers between devices, swap(): return lax.ppermute(x, SEQ, [(i, i ^ bit) for i in range(n)])  27.1 us
    ppermute x21, starting transfers between devices, swap(): return lax.ppermute(x, SEQ, [(i, i ^ bit) for i in range(n)])  17.3 us
    all_to_all x2, waiting for transfers between devices, exchange(): return lax.all_to_all(x, axes, 0, 0, tiled=True)  8.08 us
    all_to_all x2, starting transfers between devices, exchange(): return lax.all_to_all(x, axes, 0, 0, tiled=True)  6.94 us
    unnamed x54, local copies, waits for them, and re-layouts  6.94 us
  transfers between devices with their start and end apart: 25, of which 11 were waited for; matrix products, arithmetic and copies ran while one was open for 1% of the time, Pallas kernels for 11%

profile of v5, /device:TPU:0, one launch (start us, length us, event | category | flops | bytes accessed | tf_op | source)
XLA Modules:
  0.0 143.0 jit_solution(3936541922973786189)
XLA Ops:
  0.6 2.5 %shard_map.111 = (bf16[8,32,1152]{2,1,0:T(8,128)(2,1)}, bf16[32,2048]{1,0:T(8,128)(2,1)}, bf16[32,2048]{1,0:T(8,128)(2,1)}, f32[32,1]{1,0:T(8,128)}, f32[32,1]{1,0:T(8,128)}) custom-call(bf16[128,2048]{1,0:T(8,128)(2,1)} %bitcast.20, bf16[128,2048]{1,0:T(8,128)(2,1)} %bitcast.22, s32[1,128]{1,0:T(1,128)} %picks_ref.3, f32[1,2048]{1,0:T(1,128)} %bitcast.26), custom_call_target="tpu_custom_call" | custom-call | tf_op jit(solution)/shard_map/pallas_call | solution.py:46
  3.1 23.8 %all_to_all.20.mine_ref = bf16[8,32,1152]{2,1,0:T(8,128)(2,1)S(1)} all-to-all(bf16[8,32,1152]{2,1,0:T(8,128)(2,1)} %get-tuple-element.44), channel_id=1, replica_groups=mesh['dp'=2,'zz'=4,'yy'=2,'cc'=2] {'zz','yy'}, dimensions={0} | all-to-all | bytes 1179648 | tf_op jit(solution)/shard_map/all_to_all | solution.py:378
  27.7 2.5 %shard_map.112 = (bf16[128,320]{1,0:T(8,128)(2,1)}, bf16[128,320]{1,0:T(8,128)(2,1)}, bf16[128,320]{1,0:T(8,128)(2,1)}, bf16[128,320]{1,0:T(8,128)(2,1)}, bf16[6...) custom-call(s32[4]{0:T(128)} %pad_add_fusion.at_ref, ...), custom_call_target="tpu_custom_call" | custom-call | tf_op jit(solution)/shard_map/pallas_call | solution.py:46
  33.0 1.8 %collective-permute-done.4.refs_1_ = bf16[64,512]{1,0:T(8,128)(2,1)S(1)} collective-permute-done((bf16[64,512]{1,0:T(8,128)(2,1)}, bf16[64,512]{1,0:T(8,128)(2,1)S(1)}, u32[]{:S(2)}, u32[]{:S(2)}) %collective-permute-start.4) | collective-permute-done | bytes 65568 | tf_op jit(solution)/shard_map/ppermute | solution.py:382
  34.8 2.8 %collective-permute-done.5.refs_2_ = bf16[64,512]{1,0:T(8,128)(2,1)S(1)} collective-permute-done((bf16[64,512]{1,0:T(8,128)(2,1)}, bf16[64,512]{1,0:T(8,128)(2,1)S(1)}, u32[]{:S(2)}, u32[]{:S(2)}) %collective-permute-start.5) | collective-permute-done | bytes 65568 | tf_op jit(solution)/shard_map/ppermute | solution.py:382
  37.6 1.5 %collective-permute-start.6 = (bf16[64,512]{1,0:T(8,128)(2,1)}, bf16[64,512]{1,0:T(8,128)(2,1)S(1)}, u32[]{:S(2)}, u32[]{:S(2)}) collective-permute-start(bf16[64,512]{1,0:T(8,128)(2,1)} %get-tuple-element.52), channel_id=1, source_target_pairs={{0,12},{1,13},{2,14},{3,15},{4,8},{5,9},{6,10},{7,11},{8,4},{9,5},... | collective-permute-start | bytes 196616 | tf_op jit(solution)/shard_map/ppermute | solution.py:382
  39.1 4.8 %collective-permute-done.6.refs_3_ = bf16[64,512]{1,0:T(8,128)(2,1)S(1)} collective-permute-done((bf16[64,512]{1,0:T(8,128)(2,1)}, bf16[64,512]{1,0:T(8,128)(2,1)S(1)}, u32[]{:S(2)}, u32[]{:S(2)}) %collective-permute-start.6) | collective-permute-done | bytes 65568 | tf_op jit(solution)/shard_map/ppermute | solution.py:382
  44.5 1.8 %shard_map.114 = (bf16[4,64,512]{2,1,0:T(8,128)(2,1)}, bf16[4,4,64,128]{3,2,1,0:T(8,128)(2,1)}) custom-call(s32[4]{0:T(128)} %pad_add_fusion.at_ref, bf16[64,512]{1,0:T(8,128)(2,1)} %get-tuple-element.49.refs_0_, bf16[64,512]{1,0:T(8,128)(2,1)} %copy-done.18, bf16[64,512]{1,0:T(8,128)(2,1)} %copy-done.19, bf16[64,512]{1,0:T(8,128)(2,1)} %copy-done.20), custom_call_target="tpu_custom_call" | custom-call | tf_op jit(solution)/shard_map/pallas_call | solution.py:46
  47.0 1.9 %shard_map.113.wqkv_ref = bf16[4,128,320]{2,1,0:T(8,128)(2,1)} custom-call(s32[4]{0:T(128)} %pad_add_fusion.at_ref, bf16[128,320]{1,0:T(8,128)(2,1)} %get-tuple-element.45.refs_0_, bf16[128,320]{1,0:T(8,128)(2,1)} %copy-done.12, bf16[128,320]{1,0:T(8,128)(2,1)} %copy-done.13, bf16[128,320]{1,0:T(8,128)(2,1)} %copy-done.14), custom_call_target="tpu_custom_call" | custom-call | tf_op jit(solution)/shard_map/pallas_call | solution.py:46
  49.7 4.8 %shard_map.115 = (f32[288,128]{1,0:T(8,128)}, f32[288,128]{1,0:T(8,128)}, f32[288,128]{1,0:T(8,128)}, f32[288,128]{1,0:T(8,128)}, bf16[512,256]{1,0:T(8,128)(2,1...) custom-call(s32[4]{0:T(128)} %pad_add_fusion.at_ref, ...), custom_call_target="tpu_custom_call" | custom-call | tf_op jit(solution)/shard_map/pallas_call | solution.py:46
  54.5 2.1 %collective-permute-start.8 = (f32[288,128]{1,0:T(8,128)}, f32[288,128]{1,0:T(8,128)S(1)}, u32[]{:S(2)}, u32[]{:S(2)}) collective-permute-start(f32[288,128]{1,0:T(8,128)} %get-tuple-element.56), channel_id=1, source_target_pairs={{0,8},{1,9},{2,10},{3,11},{4,12},{5,13},{6,14},{7,15},{8,0},{9,1},... | collective-permute-start | bytes 442376 | tf_op jit(solution)/shard_map/ppermute | solution.py:382
  56.5 2.3 %collective-permute-start.9 = (f32[288,128]{1,0:T(8,128)}, f32[288,128]{1,0:T(8,128)S(1)}, u32[]{:S(2)}, u32[]{:S(2)}) collective-permute-start(f32[288,128]{1,0:T(8,128)} %get-tuple-element.57), channel_id=1, source_target_pairs={{0,12},{1,13},{2,14},{3,15},{4,8},{5,9},{6,10},{7,11},{8,4},{9,5},... | collective-permute-start | bytes 442376 | tf_op jit(solution)/shard_map/ppermute | solution.py:382
  58.9 1.6 %collective-permute-done.7.refs_1_ = f32[288,128]{1,0:T(8,128)S(1)} collective-permute-done((f32[288,128]{1,0:T(8,128)}, f32[288,128]{1,0:T(8,128)S(1)}, u32[]{:S(2)}, u32[]{:S(2)}) %collective-permute-start.7) | collective-permute-done | bytes 147488 | tf_op jit(solution)/shard_map/ppermute | solution.py:382
  60.5 7.0 %collective-permute-done.8.refs_2_ = f32[288,128]{1,0:T(8,128)S(1)} collective-permute-done((f32[288,128]{1,0:T(8,128)}, f32[288,128]{1,0:T(8,128)S(1)}, u32[]{:S(2)}, u32[]{:S(2)}) %collective-permute-start.8) | collective-permute-done | bytes 147488 | tf_op jit(solution)/shard_map/ppermute | solution.py:382
  68.2 2.0 %shard_map.116 = (bf16[8,160,128]{2,1,0:T(8,128)(2,1)}, bf16[8,128,128]{2,1,0:T(8,128)(2,1)}) custom-call(f32[288,128]{1,0:T(8,128)} %get-tuple-element.54.refs_0_, f32[288,128]{1,0:T(8,128)} %copy-done.8, f32[288,128]{1,0:T(8,128)} %copy-done.9, f32[288,128]{1,0:T(8,128)} %copy-done.10), custom_call_target="tpu_custom_call" | custom-call | tf_op jit(solution)/shard_map/pallas_call | solution.py:46
  70.2 13.1 %all_to_all.21.refs_0_ = bf16[8,160,128]{2,1,0:T(8,128)(2,1)S(1)} all-to-all(bf16[8,160,128]{2,1,0:T(8,128)(2,1)} %get-tuple-element.58), channel_id=1, replica_groups=mesh['dp'=2,'zz'=4,'yy'=2,'cc'=2] {'zz','yy'}, dimensions={0} | all-to-all | bytes 655360 | tf_op jit(solution)/shard_map/all_to_all | solution.py:378
  83.3 3.4 %all-to-all-start.2 = ((bf16[8,128,128]{2,1,0:T(8,128)(2,1)}), bf16[8,128,128]{2,1,0:T(8,128)(2,1)S(1)}, u32[]{:S(2)}, u32[]{:S(2)}) async-start(bf16[8,128,128]{2,1,0:T(8,128)(2,1)} %get-tuple-element.59), calls=%async_computation.2 | async-start | bytes 524288 | tf_op jit(solution)/shard_map/all_to_all | solution.py:378
  86.8 8.1 %all-to-all-done.2.refs_2_ = bf16[8,128,128]{2,1,0:T(8,128)(2,1)S(1)} async-done(((bf16[8,128,128]{2,1,0:T(8,128)(2,1)}), bf16[8,128,128]{2,1,0:T(8,128)(2,1)S(1)}, u32[]{:S(2)}, u32[]{:S(2)}) %all-to-all-start.2) | async-done | bytes 262176 | tf_op jit(solution)/shard_map/all_to_all | solution.py:378
  97.6 1.7 %collective-permute-done.14.refs_3_ = bf16[4,64,128]{2,1,0:T(8,128)(2,1)S(1)} collective-permute-done((bf16[4,64,128]{2,1,0:T(8,128)(2,1)S(1)}, bf16[4,64,128]{2,1,0:T(8,128)(2,1)S(1)}, u32[]{:S(2)}, u32[]{:S(2)}) %collective-permute-start.14) | collective-permute-done | bytes 65568 | tf_op jit(solution)/shard_map/ppermute | solution.py:382
  99.4 2.0 %collective-permute-done.13.refs_2_ = bf16[4,64,128]{2,1,0:T(8,128)(2,1)S(1)} collective-permute-done((bf16[4,64,128]{2,1,0:T(8,128)(2,1)S(1)}, bf16[4,64,128]{2,1,0:T(8,128)(2,1)S(1)}, u32[]{:S(2)}, u32[]{:S(2)}) %collective-permute-start.13) | collective-permute-done | bytes 65568 | tf_op jit(solution)/shard_map/ppermute | solution.py:382
  102.0 1.7 %shard_map.117.refs_2_ = bf16[16,64,128]{2,1,0:T(8,128)(2,1)} custom-call(s32[4]{0:T(128)} %pad_add_fusion.at_ref, bf16[4,64,128]{2,1,0:T(8,128)(2,1)} %get-tuple-element.79.refs_0_, bf16[4,64,128]{2,1,0:T(8,128)(2,1)} %copy-done.17, bf16[4,64,128]{2,1,0:T(8,128)(2,1)} %copy-done.16, bf16[4,64,128]{2,1,0:T(8,128)(2,1)} %copy-done.15), custom_call_target="tpu_custom_call" | custom-call | tf_op jit(solution)/shard_map/pallas_call | solution.py:46
  104.4 5.0 %shard_map.118 = (bf16[16,32,128]{2,1,0:T(8,128)(2,1)}, bf16[256,256]{1,0:T(8,128)(2,1)}, f32[8,256]{1,0:T(8,128)}, f32[16,128,128]{2,1,0:T(8,128)}, f32[16,128,256]{2,1,0:T(8,128)}) custom-call(s32[4]{0:T(128)} %pad_add_fusion.at_ref, bf16[8,160,128]{2,1,0:T(8,128)(2,1)} %copy-done, bf16[8,160,128]{2,1,0:T(8,128)(2,1)} %copy-done.2, ...), custom_call_target="tpu_custom_call" | custom-call | tf_op jit(solution)/shard_map/pallas_call | solution.py:46
  110.1 6.2 %shard_map.119 = (bf16[16,32,256]{2,1,0:T(8,128)(2,1)}, f32[128,256]{1,0:T(8,128)}) custom-call(s32[4]{0:T(128)} %pad_add_fusion.at_ref, bf16[8,160,128]{2,1,0:T(8,128)(2,1)} %copy-done, bf16[8,160,128]{2,1,0:T(8,128)(2,1)} %copy-done.2, bf16[8,128,128]{2,1,0:T(8,128)(2,1)} %copy-done.4, bf16[8,128,128]{2,1,0:T(8,128)(2,1)} %copy-done.7, ...), custom_call_target="tpu_custom_call" | custom-call | tf_op jit(solution)/shard_map/pallas_call | solution.py:46
  116.3 3.5 %all-to-all-start.3 = ((bf16[16,32,256]{2,1,0:T(8,128)(2,1)}), bf16[16,32,256]{2,1,0:T(8,128)(2,1)S(1)}, u32[]{:S(2)}, u32[]{:S(2)}) async-start(bf16[16,32,256]{2,1,0:T(8,128)(2,1)} %get-tuple-element.68), calls=%async_computation.3 | async-start | bytes 524288 | tf_op jit(solution)/shard_map/all_to_all | solution.py:378
  119.9 1.6 %collective-permute-start.17 = (f32[8,256]{1,0:T(8,128)S(1)}, f32[8,256]{1,0:T(8,128)S(1)}, u32[]{:S(2)}, u32[]{:S(2)}) collective-permute-start(f32[8,256]{1,0:T(8,128)S(1)} %copy-done.22), channel_id=1, source_target_pairs={{0,3},{1,2},{2,1},{3,0},{4,7},{5,6},{6,5},{7,4},{8,11},{9,10},{10,... | collective-permute-start | bytes 24584 | tf_op jit(solution)/shard_map/ppermute | solution.py:382
  121.9 1.5 %collective-permute-start.22 = (f32[128,256]{1,0:T(8,128)}, f32[128,256]{1,0:T(8,128)S(1)}, u32[]{:S(2)}, u32[]{:S(2)}) collective-permute-start(f32[128,256]{1,0:T(8,128)} %get-tuple-element.74.a_ref), channel_id=1, source_target_pairs={{0,16},{16,0},{1,17},{17,1},{2,18},{18,2},{3,19},{19,3},{4,20},{20... | collective-permute-start | bytes 393224 | tf_op jit(solution)/shard_map/ppermute | solution.py:534
  123.4 1.8 %collective-permute-done.16 = f32[8,256]{1,0:T(8,128)S(1)} collective-permute-done((f32[8,256]{1,0:T(8,128)S(1)}, f32[8,256]{1,0:T(8,128)S(1)}, u32[]{:S(2)}, u32[]{:S(2)}) %collective-permute-start.16) | collective-permute-done | bytes 8224 | tf_op jit(solution)/shard_map/ppermute | solution.py:382
  125.1 3.5 %collective-permute-start.20 = (f32[8,256]{1,0:T(8,128)S(1)}, f32[8,256]{1,0:T(8,128)S(1)}, u32[]{:S(2)}, u32[]{:S(2)}) collective-permute-start(f32[8,256]{1,0:T(8,128)S(1)} %add_add_fusion.refs_0_), channel_id=1, source_target_pairs={{0,12},{1,13},{2,14},{3,15},{4,8},{5,9},{6,10},{7,11},{8,4},{9,5},... | collective-permute-start | bytes 24584 | tf_op jit(solution)/shard_map/ppermute | solution.py:382
  130.7 2.6 %collective-permute-done.19.refs_2_ = f32[8,256]{1,0:T(8,128)S(1)} collective-permute-done((f32[8,256]{1,0:T(8,128)S(1)}, f32[8,256]{1,0:T(8,128)S(1)}, u32[]{:S(2)}, u32[]{:S(2)}) %collective-permute-start.19) | collective-permute-done | bytes 8224 | tf_op jit(solution)/shard_map/ppermute | solution.py:382
  133.8 1.7 %shard_map.120.part_ref = f32[8,128]{1,0:T(8,128)} custom-call(bf16[256,128]{1,0:T(8,128)(2,1)} %get-tuple-element.69.x_ref, f32[8,256]{1,0:T(8,128)} %get-tuple-element.70.gate_ref, f32[8,256]{1,0:T(8,128)} %copy-done.21, f32[8,256]{1,0:T(8,128)} %copy-done.25, f32[8,256]{1,0:T(8,128)} %copy-done.24, f32[8,256]{1,0:T(8,128)} %copy-done.23), custom_call_target="tpu_custom_call" | custom-call | tf_op jit(solution)/shard_map/pallas_call | solution.py:46
  137.6 1.6 %shard_map.122 = f32[128,256]{1,0:T(8,128)} custom-call(f32[128,256]{1,0:T(8,128)} %get-tuple-element.74.a_ref, f32[128,256]{1,0:T(8,128)} %copy-done.11), custom_call_target="tpu_custom_call" | custom-call | tf_op jit(solution)/shard_map/pallas_call | solution.py:46
  140.0 2.9 %shard_map.121 = (bf16[128,2048]{1,0:T(8,128)(2,1)}, bf16[128,2048]{1,0:T(8,128)(2,1)}, f32[1,128]{1,0:T(1,128)}) custom-call(bf16[128,2048]{1,0:T(8,128)(2,1)} %bitcast.21, bf16[128,2048]{1,0:T(8,128)(2,1)} %bitcast.23, s32[1,128]{1,0:T(1,128)} %picks_ref.3, f32[1,2048]{1,0:T(1,128)} %bitcast.27, f32[32,1]{1,0:T(8,128)} %get-tuple-element.40.gate_ref, ...), custom_call_target="tpu_custom_call" | custom-call | tf_op jit(solution)/shard_map/pallas_call | solution.py:46
  (89 shorter events, 17.3 us)
Async XLA Ops:
  27.0 21.9 %copy-start.1 = (bf16[8,32,1152]{2,1,0:T(8,128)(2,1)}, bf16[8,32,1152]{2,1,0:T(8,128)(2,1)S(1)}, u32[]{:S(2)}) copy-start(bf16[8,32,1152]{2,1,0:T(8,128)(2,1)S(1)} %all_to_all.20.mine_ref) | copy-start | bytes 1769476
  27.0 21.9 %collective-permute-start = (bf16[8,32,1152]{2,1,0:T(8,128)(2,1)S(1)}, bf16[8,32,1152]{2,1,0:T(8,128)(2,1)S(1)}, u32[]{:S(2)}, u32[]{:S(2)}) collective-permute-start(bf16[8,32,1152]{2,1,0:T(8,128)(2,1)S(1)} %all_to_all.20.mine_ref), channel_id=1, source_target_pairs={{0,1},{1,0},{2,3},{3,2},{4,5},{5,4},{6,7},{7,6},{8,9},{9,8},{10,11... | collective-permute-start | bytes 1769480 | tf_op jit(solution)/shard_map/ppermute | solution.py:382
  30.2 4.6 %collective-permute-start.4 = (bf16[64,512]{1,0:T(8,128)(2,1)}, bf16[64,512]{1,0:T(8,128)(2,1)S(1)}, u32[]{:S(2)}, u32[]{:S(2)}) collective-permute-start(bf16[64,512]{1,0:T(8,128)(2,1)} %get-tuple-element.50), channel_id=1, source_target_pairs={{0,4},{1,5},{2,6},{3,7},{4,0},{5,1},{6,2},{7,3},{8,12},{9,13},{10,... | collective-permute-start | bytes 196616 | tf_op jit(solution)/shard_map/ppermute | solution.py:382
  30.9 6.7 %collective-permute-start.5 = (bf16[64,512]{1,0:T(8,128)(2,1)}, bf16[64,512]{1,0:T(8,128)(2,1)S(1)}, u32[]{:S(2)}, u32[]{:S(2)}) collective-permute-start(bf16[64,512]{1,0:T(8,128)(2,1)} %get-tuple-element.51), channel_id=1, source_target_pairs={{0,8},{1,9},{2,10},{3,11},{4,12},{5,13},{6,14},{7,15},{8,0},{9,1},... | collective-permute-start | bytes 196616 | tf_op jit(solution)/shard_map/ppermute | solution.py:382
  32.2 14.0 %collective-permute-start.1 = (bf16[128,320]{1,0:T(8,128)(2,1)}, bf16[128,320]{1,0:T(8,128)(2,1)S(1)}, u32[]{:S(2)}, u32[]{:S(2)}) collective-permute-start(bf16[128,320]{1,0:T(8,128)(2,1)} %get-tuple-element.46), channel_id=1, source_target_pairs={{0,1},{1,0},{2,3},{3,2},{4,5},{5,4},{6,7},{7,6},{8,9},{9,8},{10,11... | collective-permute-start | bytes 245768 | tf_op jit(solution)/shard_map/ppermute | solution.py:382
  32.2 14.0 %collective-permute-start.2 = (bf16[128,320]{1,0:T(8,128)(2,1)}, bf16[128,320]{1,0:T(8,128)(2,1)S(1)}, u32[]{:S(2)}, u32[]{:S(2)}) collective-permute-start(bf16[128,320]{1,0:T(8,128)(2,1)} %get-tuple-element.47), channel_id=1, source_target_pairs={{0,2},{1,3},{2,0},{3,1},{4,6},{5,7},{6,4},{7,5},{8,10},{9,11},{10,... | collective-permute-start | bytes 245768 | tf_op jit(solution)/shard_map/ppermute | solution.py:382
  34.8 9.1 %copy-start.18 = (bf16[64,512]{1,0:T(8,128)(2,1)}, bf16[64,512]{1,0:T(8,128)(2,1)S(1)}, u32[]{:S(2)}) copy-start(bf16[64,512]{1,0:T(8,128)(2,1)S(1)} %collective-permute-done.4.refs_1_) | copy-start | bytes 196612
  34.8 11.5 %collective-permute-start.3 = (bf16[128,320]{1,0:T(8,128)(2,1)}, bf16[128,320]{1,0:T(8,128)(2,1)S(1)}, u32[]{:S(2)}, u32[]{:S(2)}) collective-permute-start(bf16[128,320]{1,0:T(8,128)(2,1)} %get-tuple-element.48), channel_id=1, source_target_pairs={{0,3},{1,2},{2,1},{3,0},{4,7},{5,6},{6,5},{7,4},{8,11},{9,10},{10,... | collective-permute-start | bytes 245768 | tf_op jit(solution)/shard_map/ppermute | solution.py:382
  37.6 6.3 %collective-permute-start.6 = (bf16[64,512]{1,0:T(8,128)(2,1)}, bf16[64,512]{1,0:T(8,128)(2,1)S(1)}, u32[]{:S(2)}, u32[]{:S(2)}) collective-permute-start(bf16[64,512]{1,0:T(8,128)(2,1)} %get-tuple-element.52), channel_id=1, source_target_pairs={{0,12},{1,13},{2,14},{3,15},{4,8},{5,9},{6,10},{7,11},{8,4},{9,5},... | collective-permute-start | bytes 196616 | tf_op jit(solution)/shard_map/ppermute | solution.py:382
  47.0 47.9 %copy-start.6 = (bf16[4,4,64,128]{3,2,1,0:T(8,128)(2,1)S(1)}, bf16[4,4,64,128]{3,2,1,0:T(8,128)(2,1)}, u32[]{:S(2)}) copy-start(bf16[4,4,64,128]{3,2,1,0:T(8,128)(2,1)} %get-tuple-element.60) | copy-start | bytes 786436
  54.5 6.0 %collective-permute-start.7 = (f32[288,128]{1,0:T(8,128)}, f32[288,128]{1,0:T(8,128)S(1)}, u32[]{:S(2)}, u32[]{:S(2)}) collective-permute-start(f32[288,128]{1,0:T(8,128)} %get-tuple-element.55), channel_id=1, source_target_pairs={{0,4},{1,5},{2,6},{3,7},{4,0},{5,1},{6,2},{7,3},{8,12},{9,13},{10,... | collective-permute-start | bytes 442376 | tf_op jit(solution)/shard_map/ppermute | solution.py:382
  54.5 13.0 %collective-permute-start.8 = (f32[288,128]{1,0:T(8,128)}, f32[288,128]{1,0:T(8,128)S(1)}, u32[]{:S(2)}, u32[]{:S(2)}) collective-permute-start(f32[288,128]{1,0:T(8,128)} %get-tuple-element.56), channel_id=1, source_target_pairs={{0,8},{1,9},{2,10},{3,11},{4,12},{5,13},{6,14},{7,15},{8,0},{9,1},... | collective-permute-start | bytes 442376 | tf_op jit(solution)/shard_map/ppermute | solution.py:382
  56.5 10.9 %collective-permute-start.9 = (f32[288,128]{1,0:T(8,128)}, f32[288,128]{1,0:T(8,128)S(1)}, u32[]{:S(2)}, u32[]{:S(2)}) collective-permute-start(f32[288,128]{1,0:T(8,128)} %get-tuple-element.57), channel_id=1, source_target_pairs={{0,12},{1,13},{2,14},{3,15},{4,8},{5,9},{6,10},{7,11},{8,4},{9,5},... | collective-permute-start | bytes 442376 | tf_op jit(solution)/shard_map/ppermute | solution.py:382
  83.2 20.5 %copy-start = (bf16[8,160,128]{2,1,0:T(8,128)(2,1)}, bf16[8,160,128]{2,1,0:T(8,128)(2,1)S(1)}, u32[]{:S(2)}) copy-start(bf16[8,160,128]{2,1,0:T(8,128)(2,1)S(1)} %all_to_all.21.refs_0_) | copy-start | bytes 983044
  83.3 11.6 %all-to-all-start.2 = ((bf16[8,128,128]{2,1,0:T(8,128)(2,1)}), bf16[8,128,128]{2,1,0:T(8,128)(2,1)S(1)}, u32[]{:S(2)}, u32[]{:S(2)}) async-start(bf16[8,128,128]{2,1,0:T(8,128)(2,1)} %get-tuple-element.59), calls=%async_computation.2 | async-start | bytes 524288 | tf_op jit(solution)/shard_map/all_to_all | solution.py:378
  86.7 17.0 %collective-permute-start.10 = (bf16[8,160,128]{2,1,0:T(8,128)(2,1)S(1)}, bf16[8,160,128]{2,1,0:T(8,128)(2,1)S(1)}, u32[]{:S(2)}, u32[]{:S(2)}) collective-permute-start(bf16[8,160,128]{2,1,0:T(8,128)(2,1)S(1)} %all_to_all.21.refs_0_), channel_id=1, source_target_pairs={{0,1},{1,0},{2,3},{3,2},{4,5},{5,4},{6,7},{7,6},{8,9},{9,8},{10,11... | collective-permute-start | bytes 983048 | tf_op jit(solution)/shard_map/ppermute | solution.py:382
  94.8 14.6 %copy-start.4 = (bf16[8,128,128]{2,1,0:T(8,128)(2,1)}, bf16[8,128,128]{2,1,0:T(8,128)(2,1)S(1)}, u32[]{:S(2)}) copy-start(bf16[8,128,128]{2,1,0:T(8,128)(2,1)S(1)} %all-to-all-done.2.refs_2_) | copy-start | bytes 786436
  94.8 14.6 %collective-permute-start.11 = (bf16[8,128,128]{2,1,0:T(8,128)(2,1)S(1)}, bf16[8,128,128]{2,1,0:T(8,128)(2,1)S(1)}, u32[]{:S(2)}, u32[]{:S(2)}) collective-permute-start(bf16[8,128,128]{2,1,0:T(8,128)(2,1)S(1)} %all-to-all-done.2.refs_2_), channel_id=1, source_target_pairs={{0,1},{1,0},{2,3},{3,2},{4,5},{5,4},{6,7},{7,6},{8,9},{9,8},{10,11... | collective-permute-start | bytes 786440 | tf_op jit(solution)/shard_map/ppermute | solution.py:382
  95.6 3.8 %collective-permute-start.14 = (bf16[4,64,128]{2,1,0:T(8,128)(2,1)S(1)}, bf16[4,64,128]{2,1,0:T(8,128)(2,1)S(1)}, u32[]{:S(2)}, u32[]{:S(2)}) collective-permute-start(bf16[4,64,128]{2,1,0:T(8,128)(2,1)S(1)} %get-tuple-element.76), channel_id=1, source_target_pairs={{0,3},{1,2},{2,1},{3,0},{4,7},{5,6},{6,5},{7,4},{8,11},{9,10},{10,... | collective-permute-start | bytes 196616 | tf_op jit(solution)/shard_map/ppermute | solution.py:382
  96.9 4.5 %collective-permute-start.13 = (bf16[4,64,128]{2,1,0:T(8,128)(2,1)S(1)}, bf16[4,64,128]{2,1,0:T(8,128)(2,1)S(1)}, u32[]{:S(2)}, u32[]{:S(2)}) collective-permute-start(bf16[4,64,128]{2,1,0:T(8,128)(2,1)S(1)} %get-tuple-element.77), channel_id=1, source_target_pairs={{0,2},{1,3},{2,0},{3,1},{4,6},{5,7},{6,4},{7,5},{8,10},{9,11},{10,... | collective-permute-start | bytes 196616 | tf_op jit(solution)/shard_map/ppermute | solution.py:382
  97.6 3.7 %collective-permute-start.12 = (bf16[4,64,128]{2,1,0:T(8,128)(2,1)S(1)}, bf16[4,64,128]{2,1,0:T(8,128)(2,1)S(1)}, u32[]{:S(2)}, u32[]{:S(2)}) collective-permute-start(bf16[4,64,128]{2,1,0:T(8,128)(2,1)S(1)} %get-tuple-element.78), channel_id=1, source_target_pairs={{0,1},{1,0},{2,3},{3,2},{4,5},{5,4},{6,7},{7,6},{8,9},{9,8},{10,11... | collective-permute-start | bytes 196616 | tf_op jit(solution)/shard_map/ppermute | solution.py:382
  110.1 9.7 %copy-start.22 = (f32[8,256]{1,0:T(8,128)S(1)}, f32[8,256]{1,0:T(8,128)}, u32[]{:S(2)}) copy-start(f32[8,256]{1,0:T(8,128)} %get-tuple-element.71) | copy-start | bytes 24580
  116.3 23.0 %all-to-all-start.3 = ((bf16[16,32,256]{2,1,0:T(8,128)(2,1)}), bf16[16,32,256]{2,1,0:T(8,128)(2,1)S(1)}, u32[]{:S(2)}, u32[]{:S(2)}) async-start(bf16[16,32,256]{2,1,0:T(8,128)(2,1)} %get-tuple-element.68), calls=%async_computation.3 | async-start | bytes 524288 | tf_op jit(solution)/shard_map/all_to_all | solution.py:378
  119.9 3.5 %collective-permute-start.17 = (f32[8,256]{1,0:T(8,128)S(1)}, f32[8,256]{1,0:T(8,128)S(1)}, u32[]{:S(2)}, u32[]{:S(2)}) collective-permute-start(f32[8,256]{1,0:T(8,128)S(1)} %copy-done.22), channel_id=1, source_target_pairs={{0,3},{1,2},{2,1},{3,0},{4,7},{5,6},{6,5},{7,4},{8,11},{9,10},{10,... | collective-permute-start | bytes 24584 | tf_op jit(solution)/shard_map/ppermute | solution.py:382
  121.5 3.7 %collective-permute-start.16 = (f32[8,256]{1,0:T(8,128)S(1)}, f32[8,256]{1,0:T(8,128)S(1)}, u32[]{:S(2)}, u32[]{:S(2)}) collective-permute-start(f32[8,256]{1,0:T(8,128)S(1)} %copy-done.22), channel_id=1, source_target_pairs={{0,2},{1,3},{2,0},{3,1},{4,6},{5,7},{6,4},{7,5},{8,10},{9,11},{10,... | collective-permute-start | bytes 24584 | tf_op jit(solution)/shard_map/ppermute | solution.py:382
  121.8 3.3 %collective-permute-start.15 = (f32[8,256]{1,0:T(8,128)S(1)}, f32[8,256]{1,0:T(8,128)S(1)}, u32[]{:S(2)}, u32[]{:S(2)}) collective-permute-start(f32[8,256]{1,0:T(8,128)S(1)} %copy-done.22), channel_id=1, source_target_pairs={{0,1},{1,0},{2,3},{3,2},{4,5},{5,4},{6,7},{7,6},{8,9},{9,8},{10,11... | collective-permute-start | bytes 24584 | tf_op jit(solution)/shard_map/ppermute | solution.py:382
  121.9 15.1 %collective-permute-start.22 = (f32[128,256]{1,0:T(8,128)}, f32[128,256]{1,0:T(8,128)S(1)}, u32[]{:S(2)}, u32[]{:S(2)}) collective-permute-start(f32[128,256]{1,0:T(8,128)} %get-tuple-element.74.a_ref), channel_id=1, source_target_pairs={{0,16},{16,0},{1,17},{17,1},{2,18},{18,2},{3,19},{19,3},{4,20},{20... | collective-permute-start | bytes 393224 | tf_op jit(solution)/shard_map/ppermute | solution.py:534
  125.1 8.1 %copy-start.21 = (f32[8,256]{1,0:T(8,128)}, f32[8,256]{1,0:T(8,128)S(1)}, u32[]{:S(2)}) copy-start(f32[8,256]{1,0:T(8,128)S(1)} %add_add_fusion.refs_0_) | copy-start | bytes 24580
  125.1 5.5 %collective-permute-start.20 = (f32[8,256]{1,0:T(8,128)S(1)}, f32[8,256]{1,0:T(8,128)S(1)}, u32[]{:S(2)}, u32[]{:S(2)}) collective-permute-start(f32[8,256]{1,0:T(8,128)S(1)} %add_add_fusion.refs_0_), channel_id=1, source_target_pairs={{0,12},{1,13},{2,14},{3,15},{4,8},{5,9},{6,10},{7,11},{8,4},{9,5},... | collective-permute-start | bytes 24584 | tf_op jit(solution)/shard_map/ppermute | solution.py:382
  128.7 4.5 %collective-permute-start.19 = (f32[8,256]{1,0:T(8,128)S(1)}, f32[8,256]{1,0:T(8,128)S(1)}, u32[]{:S(2)}, u32[]{:S(2)}) collective-permute-start(f32[8,256]{1,0:T(8,128)S(1)} %add_add_fusion.refs_0_), channel_id=1, source_target_pairs={{0,8},{1,9},{2,10},{3,11},{4,12},{5,13},{6,14},{7,15},{8,0},{9,1},... | collective-permute-start | bytes 24584 | tf_op jit(solution)/shard_map/ppermute | solution.py:382
  128.7 4.6 %collective-permute-start.18 = (f32[8,256]{1,0:T(8,128)S(1)}, f32[8,256]{1,0:T(8,128)S(1)}, u32[]{:S(2)}, u32[]{:S(2)}) collective-permute-start(f32[8,256]{1,0:T(8,128)S(1)} %add_add_fusion.refs_0_), channel_id=1, source_target_pairs={{0,4},{1,5},{2,6},{3,7},{4,0},{5,1},{6,2},{7,3},{8,12},{9,13},{10,... | collective-permute-start | bytes 24584 | tf_op jit(solution)/shard_map/ppermute | solution.py:382
  135.5 3.8 %collective-permute-start.21 = (f32[8,128]{1,0:T(8,128)}, f32[8,128]{1,0:T(8,128)S(1)}, u32[]{:S(2)}, u32[]{:S(2)}) collective-permute-start(f32[8,128]{1,0:T(8,128)} %shard_map.120.part_ref), channel_id=1, source_target_pairs={{0,16},{16,0},{1,17},{17,1},{2,18},{18,2},{3,19},{19,3},{4,20},{20... | collective-permute-start | bytes 12296 | tf_op jit(solution)/shard_map/ppermute | solution.py:536
  (20 other events, 28.7 us)
